TPU v7x, 256 devices: a whole 4x4x8 slice. The times are simulated.
256 devices in a mesh: cuts: 8 (over y, core), dom: 32 (over z, x).
Axes of the slice: x: 4, y: 4, z: 8, core: 2. Of those that a mesh axis runs over, the one named last changes fastest.
Arguments:
- feats: bfloat16 [65536, 4096], P('dom', 'cuts'), may hold values from -6 to 6
- adjacency: bfloat16 [2048, 128, 128], P('dom'), may hold values from 0 to 0.024658203
- blk_dst: int32 [2048], P('dom'), may hold values from 0 to 31
- blk_src: int32 [2048], P('dom'), may hold values from 0 to 15
- blk_count: int32 [32], P('dom'), may hold values from 1 to 64, as said below
- nbr_ids: int32 [4096, 8], P('dom'), may hold values from 0 to 4095
- edge_types: int32 [4096, 8], P('dom'), may hold values from 0 to 3
- w_first: bfloat16 [4096, 128], P('cuts'), may hold values from -0.09375 to 0.09375
- w_edge: bfloat16 [128, 512], replicated, may hold values from -0.1875 to 0.1875
- w_gate_in: bfloat16 [128, 384], replicated, may hold values from -0.5 to 0.5
- w_gate_state: bfloat16 [128, 256], replicated, may hold values from -0.5 to 0.5
- w_cand: bfloat16 [128, 128], replicated, may hold values from -0.5 to 0.5
- out_grad: bfloat16 [4096, 128], P('dom'), may hold values from -0.5 to 0.5
Outputs:
- new_state: bfloat16 [4096, 128], P('dom')
- w_first_grad: float32 [4096, 128], P(('cuts', 'dom'))
Inputs may be any that keep to these rules, and one draw needn't show every extreme that they name: `blk_count`: slot b counts for partition b // 64 only if b mod 64 is below this count; the other slots are padding; some partition has all 64 slots live. `blk_dst`: a destination block number. `blk_src`: a source block number within the partition.
All inputs are finite; a program needn't handle non-finite values.
Results may differ from a plain program's by a relative error of at most 0.0075.
Values may be sent and summed in bfloat16 or wider, within the bound.
No kernel may reach another device: no remote copies, remote signals or barrier semaphores. Data moves between devices by JAX's collectives and lax.ppermute only.
A program may use at most 64 MiB of HBM per device.

v0:
```python
import math

import jax
import jax.numpy as jnp
from jax import lax
from jax.sharding import PartitionSpec as P


def edge_messages(states, nbr_ids, edge_types, w_edge):
    row_count, fanout = nbr_ids.shape
    hidden = states.shape[1]
    num_types = w_edge.shape[1] // hidden
    picked = states[nbr_ids.reshape(-1)]
    projected = jnp.dot(picked, w_edge, preferred_element_type=jnp.float32).reshape(
        row_count, fanout, num_types, hidden
    )
    one_hot = (
        edge_types[:, :, None] == jnp.arange(num_types, dtype=jnp.int32)[None, None, :]
    ).astype(jnp.float32)
    return jnp.sum(projected * one_hot[:, :, :, None], axis=(1, 2))


def edge_backward(message_grad, nbr_ids, edge_types, w_edge):
    row_count, fanout = nbr_ids.shape
    hidden = message_grad.shape[1]
    num_types = w_edge.shape[1] // hidden
    w_back = (
        w_edge.reshape(hidden, num_types, hidden)
        .transpose(2, 1, 0)
        .reshape(hidden, num_types * hidden)
    )
    per_type = jnp.dot(message_grad, w_back, preferred_element_type=jnp.float32).reshape(
        row_count, 1, num_types, hidden
    )
    one_hot = (
        edge_types[:, :, None] == jnp.arange(num_types, dtype=jnp.int32)[None, None, :]
    ).astype(jnp.float32)
    return jnp.sum(per_type * one_hot[:, :, :, None], axis=2)


def gated_update(message, states, out_grad, w_gate_in, w_gate_state, w_cand):
    hidden = states.shape[1]
    message_in = message.astype(jnp.bfloat16)
    gate_in = jnp.dot(message_in, w_gate_in, preferred_element_type=jnp.float32)
    gate_state = jnp.dot(states, w_gate_state, preferred_element_type=jnp.float32)
    state_value = states.astype(jnp.float32)
    update = jax.nn.sigmoid(gate_in[:, :hidden] + gate_state[:, :hidden])
    reset = jax.nn.sigmoid(gate_in[:, hidden : 2 * hidden] + gate_state[:, hidden:])
    reset_state = (reset * state_value).astype(jnp.bfloat16)
    candidate = jnp.tanh(
        gate_in[:, 2 * hidden :] + jnp.dot(reset_state, w_cand, preferred_element_type=jnp.float32)
    )
    new_state = ((1.0 - update) * candidate + update * state_value).astype(jnp.bfloat16)
    out_value = out_grad.astype(jnp.float32)
    cand_pre = out_value * (1.0 - update) * (1.0 - candidate * candidate)
    update_pre = out_value * (state_value - candidate) * update * (1.0 - update)
    cand_grad = cand_pre.astype(jnp.bfloat16)
    reset_grad_in = jnp.dot(cand_grad, w_cand.T, preferred_element_type=jnp.float32)
    reset_pre = reset_grad_in * state_value * reset * (1.0 - reset)
    gate_grads = jnp.concatenate([update_pre, reset_pre, cand_pre], axis=1).astype(jnp.bfloat16)
    message_grad = jnp.dot(gate_grads, w_gate_in.T, preferred_element_type=jnp.float32).astype(
        jnp.bfloat16
    )
    state_grad = (
        out_value * update
        + reset_grad_in * reset
        + jnp.dot(gate_grads[:, : 2 * hidden], w_gate_state.T, preferred_element_type=jnp.float32)
    )
    return (new_state, message_grad, state_grad)


def rows_in_window(flat_contrib, flat_targets, rows_wanted):
    inside = (flat_targets >= 0) & (flat_targets < rows_wanted)
    summed = jax.ops.segment_sum(
        jnp.where(inside[:, None], flat_contrib, 0.0),
        jnp.where(inside, flat_targets, rows_wanted),
        num_segments=rows_wanted + 1,
    )
    return summed[:rows_wanted]


def body(
    feats,
    adjacency,
    blk_dst,
    blk_src,
    blk_count,
    nbr_ids,
    edge_types,
    w_first,
    w_edge,
    w_gate_in,
    w_gate_state,
    w_cand,
    out_grad,
):
    block_count = adjacency.shape[0]
    block_rows = adjacency.shape[1]
    feat_cols = feats.shape[1]
    hidden = w_first.shape[1]
    row_count = out_grad.shape[0]
    domains = lax.axis_size("dom")
    total_rows = row_count * domains
    feat_tiles = feats.reshape(-1, block_rows, feat_cols)
    live_mask = jnp.arange(block_count, dtype=jnp.int32) < blk_count[0]
    group_size = math.gcd(block_count, 16)
    groups = block_count // group_size

    def one_group(group):
        adj_group, src_group, live_group = group
        src_rows = feat_tiles[src_group]
        aggregated = jnp.einsum(
            "bij,bjf->bif", adj_group, src_rows, preferred_element_type=jnp.float32
        ).astype(jnp.bfloat16)
        projected = jnp.einsum(
            "bif,fh->bih", aggregated, w_first, preferred_element_type=jnp.float32
        )
        return (aggregated, jnp.where(live_group[:, None, None], projected, 0.0))

    aggregated, projected = lax.map(
        one_group,
        (
            adjacency.reshape(groups, group_size, block_rows, block_rows),
            blk_src.reshape(groups, group_size),
            live_mask.reshape(groups, group_size),
        ),
    )
    aggregated = aggregated.reshape(block_count, block_rows, feat_cols)
    projected = projected.reshape(block_count, block_rows, hidden)
    partial_value = jax.ops.segment_sum(
        projected, blk_dst, num_segments=total_rows // block_rows
    ).reshape(total_rows, hidden)
    owned = lax.psum_scatter(partial_value, "dom", scatter_dimension=0, tiled=True)
    first = lax.psum(owned, "cuts")
    state_exact = jnp.tanh(first)
    states = state_exact.astype(jnp.bfloat16)
    all_states = lax.all_gather(states, "dom", axis=0, tiled=True)
    message = edge_messages(all_states, nbr_ids, edge_types, w_edge)
    new_state, message_grad, state_grad = gated_update(
        message, states, out_grad, w_gate_in, w_gate_state, w_cand
    )
    contrib = edge_backward(message_grad, nbr_ids, edge_types, w_edge)
    flat_contrib = contrib.reshape(-1, hidden)
    flat_targets = nbr_ids.reshape(-1)
    state_grad = state_grad + lax.psum_scatter(
        rows_in_window(flat_contrib, flat_targets, lax.axis_size("dom") * row_count),
        "dom",
        scatter_dimension=0,
        tiled=True,
    )
    first_grad = (state_grad * (1.0 - state_exact * state_exact)).astype(jnp.bfloat16)
    all_grads = lax.all_gather(first_grad, "dom", axis=0, tiled=True)
    picked_grads = jnp.where(
        live_mask[:, None, None],
        all_grads.reshape(-1, block_rows, hidden)[blk_dst],
        jnp.zeros((), jnp.bfloat16),
    )
    w_first_grad = lax.psum_scatter(
        jnp.einsum("bif,bih->fh", aggregated, picked_grads, preferred_element_type=jnp.float32),
        "dom",
        scatter_dimension=0,
        tiled=True,
    )
    return (new_state, w_first_grad)


def solution(mesh):
    return jax.shard_map(
        body,
        mesh=mesh,
        in_specs=(
            P("dom", "cuts"),
            P("dom", None, None),
            P("dom"),
            P("dom"),
            P("dom"),
            P("dom", None),
            P("dom", None),
            P("cuts", None),
            P(),
            P(),
            P(),
            P(),
            P("dom", None),
        ),
        out_specs=(P("dom", None), P(("cuts", "dom"), None)),
        check_vma=False,
    )
```

profile of v0, /device:TPU:1, one launch (start us, length us, event | category | flops | bytes accessed | tf_op | source)
XLA Modules:
  0.0 948.1 jit_solution(16278091829357326232)
XLA Ops:
  8.6 28.6 %while.12 = (s32[]{:T(128)}, bf16[4,16,128,512]{3,2,1,0:T(8,128)(2,1)}, f32[4,16,128,128]{3,2,1,0:T(8,128)}, bf16[4,16,128,128]{3,2,1,0:T(8,128)(2,1)}, s32[4,16...) while((s32[]{:T(128)}, ...), condition=%wide.region_1.2_spmd, body=%wide.region_0.1_spmd.sunk | while | flops 538182720 | bytes 14817201 | solution.py:120
  8.7 2.3 gather_fusion
  11.0 3.1 bitcast_dynamic-update-slice_fusion.2
  14.1 1.8 fusion.95
  15.9 2.3 gather_fusion
  18.2 3.1 bitcast_dynamic-update-slice_fusion.2
  21.3 1.7 fusion.95
  23.0 2.3 gather_fusion
  25.2 3.1 bitcast_dynamic-update-slice_fusion.2
  28.4 1.7 fusion.95
  30.1 2.3 gather_fusion
  32.4 3.1 bitcast_dynamic-update-slice_fusion.2
  35.5 1.7 fusion.95
  37.9 8.8 scatter_fusion
  48.1 217.2 %reduce-scatter.4.cloned.1.call-done = f32[128,128]{1,0:T(8,128)} async-done(((f32[4096,128]{1,0:T(8,128)}), f32[128,128]{1,0:T(8,128)}) %reduce-scatter.4.cloned.1.call-update) | async-done | bytes 65552 | tf_op jit(solution)/shard_map/reduce_scatter | solution.py:133
  265.4 68.7 %all-reduce.2.cloned.1.call-done = f32[128,128]{1,0:T(8,128)} async-done(((f32[128,128]{1,0:T(8,128)}), f32[128,128]{1,0:T(8,128)}) %all-reduce.2.cloned.1.call-update) | async-done | bytes 65552 | tf_op jit(solution)/shard_map/psum | solution.py:134
  337.4 72.1 %all-gather.3.cloned.1.call-done = bf16[4096,128]{1,0:T(8,128)(2,1)} async-done(((bf16[128,128]{1,0:T(8,128)(2,1)}), bf16[4096,128]{1,0:T(8,128)(2,1)}) %all-gather.3.cloned.1.call-update) | async-done | bytes 1048592 | tf_op jit(solution)/shard_map/all_gather | solution.py:137
  409.6 4.2 gather_fusion.1
  417.0 7.1 scatter_custom_fusion.1
  425.7 216.0 %reduce-scatter.6.cloned.1.call-done = f32[128,128]{1,0:T(8,128)} async-done(((f32[4096,128]{1,0:T(8,128)}), f32[128,128]{1,0:T(8,128)}) %reduce-scatter.6.cloned.1.call-update) | async-done | bytes 65552 | tf_op jit(solution)/shard_map/reduce_scatter | solution.py:145
  643.4 75.6 %all-gather.5.cloned.1.call-done = bf16[4096,128]{1,0:T(8,128)(2,1)} async-done(((bf16[128,128]{1,0:T(8,128)(2,1)}), bf16[4096,128]{1,0:T(8,128)(2,1)}) %all-gather.5.cloned.1.call-update) | async-done | bytes 1048592 | tf_op jit(solution)/shard_map/all_gather | solution.py:152
  719.0 2.2 gather_fusion.2
  721.2 6.7 fusion.12
  728.0 213.4 %reduce-scatter.8.cloned.1.call-done = f32[16,128]{1,0:T(8,128)} async-done(((f32[512,128]{1,0:T(8,128)}), f32[16,128]{1,0:T(8,128)}) %reduce-scatter.8.cloned.1.call-update) | async-done | bytes 8208 | tf_op jit(solution)/shard_map/reduce_scatter | solution.py:158
  (85 shorter events, 12.6 us)
Async XLA Ops:
  7.2 407.4 %copy-start = (bf16[128,384]{1,0:T(8,128)(2,1)S(1)}, bf16[128,384]{1,0:T(8,128)(2,1)}, u32[]{:S(2)}) copy-start(bf16[128,384]{1,0:T(8,128)(2,1)} %param.24) | copy-start | bytes 294916
  7.2 258.1 %reduce-scatter.4.cloned.1.call-start = ((), (), s32[]{:S(2)}) async-start(), calls=%async_computation.3 | async-start | bytes 2162688 | tf_op jit(solution)/shard_map/reduce_scatter | solution.py:133
  10.9 3.1 copy-start.2
  18.1 3.1 copy-start.2
  25.2 3.1 copy-start.2
  32.4 3.1 copy-start.2
  37.2 0.7 copy-start.10
  46.7 1.4 copy-start.1
  46.7 288.9 %copy-start.8 = (s32[128,8]{0,1:T(8,128)S(1)}, s32[128,8]{0,1:T(8,128)}, u32[]{:S(2)}) copy-start(s32[128,8]{0,1:T(8,128)} %param.20) | copy-start | bytes 12292
  46.7 289.1 %copy-start.9 = (s32[128,8]{0,1:T(8,128)S(1)}, s32[128,8]{0,1:T(8,128)}, u32[]{:S(2)}) copy-start(s32[128,8]{0,1:T(8,128)} %param.21) | copy-start | bytes 12292
  46.7 289.2 %copy-start.5 = (bf16[128,512]{1,0:T(8,128)(2,1)S(1)}, bf16[128,512]{1,0:T(8,128)(2,1)}, u32[]{:S(2)}) copy-start(bf16[128,512]{1,0:T(8,128)(2,1)} %param.23) | copy-start | bytes 393220
  46.7 289.8 %copy-start.6 = (bf16[128,256]{1,0:T(8,128)(2,1)S(1)}, bf16[128,256]{1,0:T(8,128)(2,1)}, u32[]{:S(2)}) copy-start(bf16[128,256]{1,0:T(8,128)(2,1)} %param.25) | copy-start | bytes 196612
  48.1 286.0 %all-reduce.2.cloned.1.call-start = ((), (), s32[]{:S(2)}) async-start(), calls=%async_computation.4 | async-start | bytes 131072 | tf_op jit(solution)/shard_map/psum | solution.py:134
  265.3 144.2 %all-gather.3.cloned.1.call-start = ((), (), s32[]{:S(2)}) async-start(), calls=%async_computation.5 | async-start | bytes 1081344 | tf_op jit(solution)/shard_map/all_gather | solution.py:137
  335.5 306.1 %reduce-scatter.6.cloned.1.call-start = ((), (), s32[]{:S(2)}) async-start(), calls=%async_computation.6 | async-start | bytes 2162688 | tf_op jit(solution)/shard_map/reduce_scatter | solution.py:145
  413.8 0.9 copy-start.3
  413.8 0.9 copy-start.7
  413.8 0.9 copy-start.11
  413.8 1.1 copy-start.4
  425.6 293.4 %all-gather.5.cloned.1.call-start = ((), (), s32[]{:S(2)}) async-start(), calls=%async_computation.7 | async-start | bytes 1081344 | tf_op jit(solution)/shard_map/all_gather | solution.py:152
  643.3 298.0 %reduce-scatter.8.cloned.1.call-start = ((), (), s32[]{:S(2)}) async-start(), calls=%async_computation.8 | async-start | bytes 270336 | tf_op jit(solution)/shard_map/reduce_scatter | solution.py:158
Sparse Core Ops, SparseCore 0:
  48.2 217.0 reduce-scatter.3
  267.6 66.3 all-reduce.1
  337.2 72.3 all-gather.2
  425.7 215.8 reduce-scatter.5
  644.1 74.8 all-gather.4
  728.1 213.1 reduce-scatter.7
where the time goes:
time: 954 us; the launch traced here: 948 us
  waiting for transfers between devices  863 us (90%)
  matrix products  30 us (3%)
  local copies, waits for them, and re-layouts  20.8 us (2%)
  other arithmetic  18.9 us (2%)
  between operations  15.1 us (2%)
    reduce_scatter x1, waiting for transfers between devices, body(): lax.psum_scatter(partial_value, 'dom', scatter_dimension=0, tiled=True)  217 us
    reduce_scatter x1, waiting for transfers between devices, body(): lax.psum_scatter(rows_in_window(flat_contrib, flat_targets, lax.axis_size...  216 us
    reduce_scatter x1, waiting for transfers between devices, body(): lax.psum_scatter(jnp.einsum('bif,bih->fh', aggregated, picked_grads, pref...  213 us
    all_gather x1, waiting for transfers between devices, body(): all_grads = lax.all_gather(first_grad, 'dom', axis=0, tiled=True)  75.6 us
    all_gather x1, waiting for transfers between devices, body(): all_states = lax.all_gather(states, 'dom', axis=0, tiled=True)  72.1 us
    psum x1, waiting for transfers between devices, body(): first = lax.psum(owned, 'cuts')  68.7 us
  transfers between devices with their start and end apart: 6, of which 6 were waited for; matrix products, arithmetic and copies ran while one was open for 0% of the time, Pallas kernels for 0%

commit v1 on v0

v1 whole, which is shorter than its diff:
```python
import jax
import jax.numpy as jnp
from jax import lax
from jax.experimental import pallas as pl
from jax.experimental.pallas import tpu as pltpu
from jax.sharding import PartitionSpec as P

F32 = jnp.float32
BF16 = jnp.bfloat16
VMEM = pltpu.VMEM
SMEM = pltpu.SMEM


def vspec():
    return pl.BlockSpec(memory_space=pltpu.VMEM)


def sspec():
    return pl.BlockSpec(memory_space=pltpu.SMEM)


def hspec():
    return pl.BlockSpec(memory_space=pl.ANY)


def params():
    return pltpu.CompilerParams(vmem_limit_bytes=48 * 1024 * 1024)


def dot(a, b):
    return jnp.dot(a, b, preferred_element_type=F32)


def partial_kernel(
    core_ref, dst_ref, src_ref, count_ref, feats_hbm, adj_hbm, w_ref,
    keep_ref, send_ref, feats, adj, projected, acc, sems,
):
    slots, block, _ = adj.shape
    cuts, _, _ = acc.shape
    piece = block // cuts
    nodes = feats.shape[0]
    chunk = nodes // 4
    feat_copies = [
        pltpu.make_async_copy(
            feats_hbm.at[pl.ds(i * chunk, chunk)], feats.at[pl.ds(i * chunk, chunk)], sems.at[i]
        )
        for i in range(4)
    ]
    adj_copy = pltpu.make_async_copy(adj_hbm, adj, sems.at[4])
    for copy in feat_copies:
        copy.start()
    adj_copy.start()
    acc[...] = jnp.zeros_like(acc)
    for i in range(4):
        feat_copies[i].wait()
        rows = pl.ds(i * chunk, chunk)
        projected[rows, :] = dot(feats[rows, :], w_ref[...]).astype(BF16)
    adj_copy.wait()
    count = count_ref[0]
    step = 8

    def some_slots(group, carry):
        for j in range(step):
            slot = group * step + j
            rows = pl.ds(pl.multiple_of(src_ref[slot] * block, block), block)
            right = projected[rows, :]
            right = jnp.where(slot < count, right, jnp.zeros_like(right))
            result = dot(adj[slot], right)
            at = pl.ds(pl.multiple_of(dst_ref[slot] * piece, piece), piece)
            for c in range(cuts):
                acc[c, at, :] += result[c * piece : (c + 1) * piece]
        return carry

    lax.fori_loop(0, slots // step, some_slots, 0)
    core = core_ref[0]
    for y in range(cuts // 2):
        keep_ref[y] = acc[2 * y + core]
        send_ref[y] = acc[2 * y + 1 - core]


def count_kernel(cut_ref, nbr_ref, type_ref, count_ref, *, cuts, block):
    rows, fanout = nbr_ref.shape
    cells = count_ref.shape[1]
    piece = block // cuts
    nbr = nbr_ref[...]
    within = nbr % block
    local = (nbr // block) * piece + within % piece
    per_type = cells // 4
    key = jnp.where(within // piece == cut_ref[0], type_ref[...] * per_type + local, -1)
    tile = 512
    for start in range(0, cells, tile):
        place = lax.broadcasted_iota(jnp.int32, (rows, tile), 1) + start
        total = jnp.zeros((rows, tile), F32)
        for k in range(fanout):
            total += jnp.where(key[:, k : k + 1] == place, 1.0, 0.0)
        count_ref[:, start : start + tile] = total.astype(BF16)


def state_kernel(part_ref, first_ref, out_ref):
    total = jnp.sum(part_ref[...].astype(F32), axis=0)
    exact = jnp.tanh(total)
    first_ref[...] = exact
    states = exact.astype(BF16)
    for q in range(out_ref.shape[0]):
        out_ref[q] = states


def message_kernel(count_ref, states_ref, own_ref, w_ref, out_ref):
    hidden = own_ref.shape[2]
    rows = count_ref.shape[0]
    domains, piece, _ = states_ref.shape
    local = domains * piece
    states = states_ref[...].reshape(local, hidden)
    message = jnp.zeros((rows, hidden), F32)
    for e in range(count_ref.shape[1] // local):
        picked = dot(count_ref[:, e * local : (e + 1) * local], states).astype(BF16)
        message += dot(picked, w_ref[:, e * hidden : (e + 1) * hidden])
    message = message.astype(BF16)
    for c in range(out_ref.shape[0]):
        out_ref[c, :rows] = message
        out_ref[c, rows:] = own_ref[0]


def gate_kernel(
    cut_ref, recv_ref, count_ref, grad_ref, w_edge_ref, w_in_ref, w_state_ref, w_cand_ref,
    new_ref, direct_ref, back_ref, own,
):
    rows, hidden = grad_ref.shape
    cuts = recv_ref.shape[0]
    piece = recv_ref.shape[1] - rows
    local = count_ref.shape[1] // 4
    message = jnp.sum(recv_ref[:, :rows, :].astype(F32), axis=0)
    states = recv_ref[:, rows:, :].reshape(cuts * piece, hidden)
    message_in = message.astype(BF16)
    w_in = w_in_ref[...]
    w_state = w_state_ref[...]
    w_cand = w_cand_ref[...]
    gate_in = dot(message_in, w_in)
    gate_state = dot(states, w_state)
    value = states.astype(F32)
    update = jax.nn.sigmoid(gate_in[:, :hidden] + gate_state[:, :hidden])
    reset = jax.nn.sigmoid(gate_in[:, hidden : 2 * hidden] + gate_state[:, hidden:])
    candidate = jnp.tanh(gate_in[:, 2 * hidden :] + dot((reset * value).astype(BF16), w_cand))
    new_ref[...] = ((1.0 - update) * candidate + update * value).astype(BF16)
    out_grad = grad_ref[...].astype(F32)
    cand_pre = out_grad * (1.0 - update) * (1.0 - candidate * candidate)
    update_pre = out_grad * (value - candidate) * update * (1.0 - update)
    contract = (((1,), (1,)), ((), ()))
    cand_grad = cand_pre.astype(BF16)
    reset_in = lax.dot_general(cand_grad, w_cand, contract, preferred_element_type=F32)
    reset_pre = reset_in * value * reset * (1.0 - reset)
    gates = jnp.concatenate([update_pre.astype(BF16), reset_pre.astype(BF16), cand_grad], axis=1)
    message_grad_t = lax.dot_general(w_in, gates, contract, preferred_element_type=F32).astype(BF16)
    own[...] = (
        out_grad * update
        + reset_in * reset
        + lax.dot_general(gates[:, : 2 * hidden], w_state, contract, preferred_element_type=F32)
    )
    direct_ref[...] = own[pl.ds(pl.multiple_of(cut_ref[0] * piece, piece), piece), :]
    total = jnp.zeros((hidden, local), F32)
    for e in range(count_ref.shape[1] // local):
        spread = dot(message_grad_t, count_ref[:, e * local : (e + 1) * local]).astype(BF16)
        total += dot(w_edge_ref[:, e * hidden : (e + 1) * hidden], spread)
    back_ref[...] = total.T.astype(BF16).reshape(back_ref.shape)


def grad_kernel(part_ref, direct_ref, exact_ref, out_ref):
    total = direct_ref[...] + jnp.sum(part_ref[...].astype(F32), axis=0)
    exact = exact_ref[...]
    grad = (total * (1.0 - exact * exact)).astype(BF16)
    for q in range(out_ref.shape[0]):
        out_ref[q] = grad


def weight_kernel(
    core_ref, dst_ref, src_ref, count_ref, mine_ref, other_ref, feats_hbm, adj_hbm,
    out_ref, feats, adj, grads, acc, wide, sems,
):
    slots, block, _ = adj.shape
    pairs, domains, piece, hidden = mine_ref.shape
    blocks = acc.shape[0]
    adj_copy = pltpu.make_async_copy(adj_hbm, adj, sems.at[0])
    feat_copy = pltpu.make_async_copy(feats_hbm, feats, sems.at[1])
    adj_copy.start()
    feat_copy.start()
    acc[...] = jnp.zeros_like(acc)
    core = core_ref[0]
    for y in range(pairs):
        at = pl.ds(pl.multiple_of((2 * y + core) * piece, piece), piece)
        grads[:, at, :] = mine_ref[y]
        at = pl.ds(pl.multiple_of((2 * y + 1 - core) * piece, piece), piece)
        grads[:, at, :] = other_ref[y]

    def turn(d, carry):
        grads[d] = grads[d].T
        return carry

    lax.fori_loop(0, domains, turn, 0, unroll=4)
    adj_copy.wait()
    count = count_ref[0]
    step = 8

    def some_slots(group, carry):
        for j in range(step):
            slot = group * step + j
            left = grads[dst_ref[slot]]
            left = jnp.where(slot < count, left, jnp.zeros_like(left))
            acc[src_ref[slot]] += dot(left, adj[slot])
        return carry

    lax.fori_loop(0, slots // step, some_slots, 0)
    for s in range(blocks):
        wide[:, s * block : (s + 1) * block] = acc[s].astype(BF16)
    feat_copy.wait()
    result = dot(wide[...], feats[...])
    out_ref[...] = result.T.astype(BF16).reshape(out_ref.shape)


def body(
    feats,
    adjacency,
    blk_dst,
    blk_src,
    blk_count,
    nbr_ids,
    edge_types,
    w_first,
    w_edge,
    w_gate_in,
    w_gate_state,
    w_cand,
    out_grad,
):
    slots, block, _ = adjacency.shape
    nodes, feat_cols = feats.shape
    hidden = w_first.shape[1]
    rows = out_grad.shape[0]
    domains = lax.axis_size("dom")
    cuts = lax.axis_size("cuts")
    pairs = cuts // 2
    piece = block // cuts
    local = domains * piece
    cut = lax.axis_index("cuts").reshape(1)
    core = cut % 2
    same_core = [[2 * y + k for y in range(pairs)] for k in range(2)]
    partner = [(i, i ^ 1) for i in range(cuts)]

    def over_dom(x):
        return lax.all_to_all(x, "dom", 0, 0, tiled=True)

    def over_y(x):
        return lax.all_to_all(x, "cuts", 0, 0, tiled=True, axis_index_groups=same_core)

    half = jax.ShapeDtypeStruct((pairs, local, hidden), F32)
    keep, send = pl.pallas_call(
        partial_kernel,
        out_shape=(half, half),
        in_specs=[sspec()] * 4 + [hspec(), hspec(), vspec()],
        out_specs=(vspec(), vspec()),
        scratch_shapes=[
            VMEM((nodes, feat_cols), BF16),
            VMEM((slots, block, block), BF16),
            VMEM((nodes, hidden), BF16),
            VMEM((cuts, local, hidden), F32),
            pltpu.SemaphoreType.DMA((5,)),
        ],
        compiler_params=params(),
        name="partial",
    )(core, blk_dst, blk_src, blk_count, feats, adjacency, w_first)
    got = lax.ppermute(send, "cuts", partner)
    counts = pl.pallas_call(
        lambda *refs: count_kernel(*refs, cuts=cuts, block=block),
        out_shape=jax.ShapeDtypeStruct((rows, 4 * local), BF16),
        in_specs=[sspec(), vspec(), vspec()],
        out_specs=vspec(),
        compiler_params=params(),
        name="counts",
    )(cut, nbr_ids, edge_types)
    by_y = over_y((keep + got).astype(BF16))
    by_dom = over_dom(
        jnp.sum(by_y.astype(F32), axis=0).astype(BF16).reshape(domains, piece, hidden)
    )
    spread = jax.ShapeDtypeStruct((domains, piece, hidden), BF16)
    small = jax.ShapeDtypeStruct((piece, hidden), F32)
    exact, own_states = pl.pallas_call(
        state_kernel,
        out_shape=(small, spread),
        in_specs=[vspec()],
        out_specs=(vspec(), vspec()),
        compiler_params=params(),
        name="state",
    )(by_dom)
    states = over_dom(own_states)
    sent = pl.pallas_call(
        message_kernel,
        out_shape=jax.ShapeDtypeStruct((cuts, rows + piece, hidden), BF16),
        in_specs=[vspec(), vspec(), vspec(), vspec()],
        out_specs=vspec(),
        compiler_params=params(),
        name="message",
    )(counts, states, own_states, w_edge)
    recv = lax.all_to_all(sent, "cuts", 0, 0, tiled=True)
    new_state, direct, back = pl.pallas_call(
        gate_kernel,
        out_shape=(jax.ShapeDtypeStruct((rows, hidden), BF16), small, spread),
        in_specs=[sspec()] + [vspec()] * 7,
        out_specs=(vspec(), vspec(), vspec()),
        scratch_shapes=[VMEM((rows, hidden), F32)],
        compiler_params=params(),
        name="gates",
    )(cut, recv, counts, out_grad, w_edge, w_gate_in, w_gate_state, w_cand)
    grad_part = over_dom(back)
    own_grad = pl.pallas_call(
        grad_kernel,
        out_shape=spread,
        in_specs=[vspec()] * 3,
        out_specs=vspec(),
        compiler_params=params(),
        name="first_grad",
    )(grad_part, direct, exact)
    slice_grads = over_dom(own_grad)
    mine = over_y(jnp.broadcast_to(slice_grads[None], (pairs, domains, piece, hidden)))
    other = lax.ppermute(mine, "cuts", partner)
    weight_part = pl.pallas_call(
        weight_kernel,
        out_shape=jax.ShapeDtypeStruct((domains, feat_cols // domains, hidden), BF16),
        in_specs=[sspec()] * 4 + [vspec(), vspec(), hspec(), hspec()],
        out_specs=vspec(),
        scratch_shapes=[
            VMEM((nodes, feat_cols), BF16),
            VMEM((slots, block, block), BF16),
            VMEM((domains, block, hidden), BF16),
            VMEM((nodes // block, hidden, block), F32),
            VMEM((hidden, nodes), BF16),
            pltpu.SemaphoreType.DMA((2,)),
        ],
        compiler_params=params(),
        name="weight_grad",
    )(core, blk_dst, blk_src, blk_count, mine, other, feats, adjacency)
    w_first_grad = jnp.sum(over_dom(weight_part).astype(F32), axis=0)
    return (new_state, w_first_grad)


def solution(mesh):
    return jax.shard_map(
        body,
        mesh=mesh,
        in_specs=(
            P("dom", "cuts"),
            P("dom", None, None),
            P("dom"),
            P("dom"),
            P("dom"),
            P("dom", None),
            P("dom", None),
            P("cuts", None),
            P(),
            P(),
            P(),
            P(),
            P("dom", None),
        ),
        out_specs=(P("dom", None), P(("cuts", "dom"), None)),
        check_vma=False,
    )
```

time: 954 us -> 137 us (0.14)
  waiting for transfers between devices: 863 us -> 12 us
  blocking collectives: 0 us -> 92.4 us
  matrix products: 30 us -> 0 us
  other arithmetic: 18.9 us -> 0.85 us
  local copies, waits for them, and re-layouts: 20.8 us -> 4.12 us
  Pallas kernels: 0 us -> 13.8 us
  between operations: 15.1 us -> 1.43 us
  starting transfers between devices: 0.24 us -> 11.5 us
    reduce_scatter x3 -> x0, waiting for transfers between devices: 647 us -> none  [the longest x1 217 us: body(): lax.psum_scatter(partial_value, 'dom', scatter_dimension=0, tiled=True)]
    all_gather x2 -> x0, waiting for transfers between devices: 148 us -> none  [the longest x1 75.6 us: body(): all_grads = lax.all_gather(first_grad, 'dom', axis=0, tiled=True)]
    all_to_all x0 -> x7, blocking collectives: none -> 92.4 us  [the longest x4 57.2 us: over_dom(): return lax.all_to_all(x, 'dom', 0, 0, tiled=True)]
    psum x1 -> x0, waiting for transfers between devices: 68.7 us -> none  [body(): first = lax.psum(owned, 'cuts')]
    dot_general x16 -> x0, matrix products: 30 us -> none  [the longest x4 12.4 us: one_group(): jnp.einsum('bij,bjf->bif', adj_group, src_rows, preferred_element_type=jn...]
    scatter-add x2 -> x0, other arithmetic: 15.9 us -> none  [the longest x1 8.79 us: body(): jax.ops.segment_sum(projected, blk_dst, num_segments=total_rows // block_...]
    gather x6 -> x0, local copies, waits for them, and re-layouts: 15.5 us -> none  [the longest x4 9.09 us: one_group(): src_rows = feat_tiles[src_group]]
    pallas_call x0 -> x7, Pallas kernels: none -> 13.8 us  [the longest x1 4.56 us: body(): pl.pallas_call(partial_kernel, out_shape=(half, half), in_specs=[sspec()]...]
  transfers between devices with their start and end apart: 6 -> 3, of which waited for: 6 -> 3; matrix products, arithmetic and copies ran while one was open for 0% -> 0% of each run, Pallas kernels for 0% -> 1%
where the time goes in v1:
time: 137 us; the launch traced here: 136 us
  blocking collectives  92.4 us (67%)
  Pallas kernels  13.8 us (10%)
  waiting for transfers between devices  12 us (9%)
  starting transfers between devices  11.5 us (8%)
  local copies, waits for them, and re-layouts  4.12 us (3%)
  between operations  1.43 us (1%)
    all_to_all x4, blocking collectives, over_dom(): return lax.all_to_all(x, 'dom', 0, 0, tiled=True)  57.2 us
    all_to_all x2, blocking collectives, over_y(): lax.all_to_all(x, 'cuts', 0, 0, tiled=True, axis_index_groups=same_core)  20.9 us
    all_to_all x1, blocking collectives, body(): recv = lax.all_to_all(sent, 'cuts', 0, 0, tiled=True)  14.4 us
    all_to_all x1, waiting for transfers between devices, over_dom(): return lax.all_to_all(x, 'dom', 0, 0, tiled=True)  8.15 us
    pallas_call x1, Pallas kernels, body(): pl.pallas_call(partial_kernel, out_shape=(half, half), in_specs=[sspec()]...  4.56 us
    ppermute x1, starting transfers between devices, body(): other = lax.ppermute(mine, 'cuts', partner)  4.33 us
    pallas_call x1, Pallas kernels, body(): pl.pallas_call(weight_kernel, out_shape=jax.ShapeDtypeStruct((domains, fe...  4.22 us
    unnamed x32, local copies, waits for them, and re-layouts  4.06 us
  transfers between devices with their start and end apart: 3, of which 3 were waited for; matrix products, arithmetic and copies ran while one was open for 0% of the time, Pallas kernels for 1%

profile of v1, /device:TPU:1, one launch (start us, length us, event | category | flops | bytes accessed | tf_op | source)
XLA Modules:
  0.0 136.1 jit_solution(8766963349448754641)
XLA Ops:
  1.3 1.6 %copy-done = bf16[2048,512]{1,0:T(8,128)(2,1)S(1)} copy-done((bf16[2048,512]{1,0:T(8,128)(2,1)S(1)}, bf16[2048,512]{1,0:T(8,128)(2,1)}, u32[]{:S(2)}) %copy-start) | copy-done | bytes 2097176
  2.9 0.9 copy-done.4
  3.8 0.7 copy-done.9
  4.4 0.7 copy-done.11
  5.1 4.6 %partial.1 = (f32[4,512,128]{2,1,0:T(8,128)S(1)}, f32[4,512,128]{2,1,0:T(8,128)S(1)}) custom-call(s32[1]{0:T(128)S(6)} %select_n.7.core_ref, s32[64]{0:T(128)S(1)} %copy-done.9, s32[64]{0:T(128)S(1)} %copy-done.11, s32[1]{0:T(128)S(6)} %copy.17.count_ref, bf16[2048,512]{1,0:T(8,128)(2,1)S(1)} %copy-done, bf16[64,128,128]{2,1,0:T(8,128)(2,1)} %adj_hbm.3, ...), custom_call_target="tpu_custom_call" | custom-call | tf_op jit(solution)/shard_map/partial/pallas_call | solution.py:255
  9.7 3.3 %collective-permute-start = (f32[4,512,128]{2,1,0:T(8,128)S(1)}, f32[4,512,128]{2,1,0:T(8,128)S(1)}, u32[]{:S(2)}, u32[]{:S(2)}) collective-permute-start(f32[4,512,128]{2,1,0:T(8,128)S(1)} %get-tuple-element.10), channel_id=1, source_target_pairs={{0,32},{32,0},{64,96},{96,64},{128,160},{160,128},{192,224},{224,1... | collective-permute-start | bytes 3145736 | tf_op jit(solution)/shard_map/ppermute | solution.py:270
  13.0 2.3 %collective-permute-done = f32[4,512,128]{2,1,0:T(8,128)S(1)} collective-permute-done((f32[4,512,128]{2,1,0:T(8,128)S(1)}, f32[4,512,128]{2,1,0:T(8,128)S(1)}, u32[]{:S(2)}, u32[]{:S(2)}) %collective-permute-start) | collective-permute-done | bytes 1048608 | tf_op jit(solution)/shard_map/ppermute | solution.py:270
  15.4 11.6 %all_to_all.40 = bf16[4,512,128]{2,1,0:T(8,128)(2,1)S(1)} all-to-all(bf16[4,512,128]{2,1,0:T(8,128)(2,1)S(1)} %add_convert_fusion), channel_id=1, replica_groups={{0,64,128,192},{32,96,160,224},{1,65,129,193},{33,97,161,225},{2,66,130..., dimensions={0} | all-to-all | bytes 1048576 | tf_op jit(solution)/shard_map/all_to_all | solution.py:252
  27.1 19.6 %all_to_all.41.part_ref = bf16[32,16,128]{2,1,0:T(8,128)(2,1)S(1)} all-to-all(bf16[32,16,128]{2,1,0:T(8,128)(2,1)S(1)} %bitcast.2), channel_id=1, replica_groups=mesh['cuts'=8,'dom'=32] {'dom'}, dimensions={0} | all-to-all | bytes 262144 | tf_op jit(solution)/shard_map/all_to_all | solution.py:249
  46.7 0.7 state.1
  47.4 3.9 %all-to-all-start.2 = ((bf16[32,16,128]{2,1,0:T(8,128)(2,1)}), bf16[32,16,128]{2,1,0:T(8,128)(2,1)S(1)}, u32[]{:S(2)}, u32[]{:S(2)}) async-start(bf16[32,16,128]{2,1,0:T(8,128)(2,1)} %get-tuple-element.11.own_ref), calls=%async_computation.2 | async-start | bytes 262144 | tf_op jit(solution)/shard_map/all_to_all | solution.py:249
  51.5 1.0 counts.1.count_ref
  52.5 8.2 %all-to-all-done.2.states_ref = bf16[32,16,128]{2,1,0:T(8,128)(2,1)S(1)} async-done(((bf16[32,16,128]{2,1,0:T(8,128)(2,1)}), bf16[32,16,128]{2,1,0:T(8,128)(2,1)S(1)}, u32[]{:S(2)}, u32[]{:S(2)}) %all-to-all-start.2) | async-done | bytes 131104 | tf_op jit(solution)/shard_map/all_to_all | solution.py:249
  60.7 1.4 %message.1 = bf16[8,144,128]{2,1,0:T(8,128)(2,1)S(1)} custom-call(bf16[128,2048]{1,0:T(8,128)(2,1)S(1)} %counts.1.count_ref, bf16[32,16,128]{2,1,0:T(8,128)(2,1)S(1)} %all-to-all-done.2.states_ref, bf16[32,16,128]{2,1,0:T(8,128)(2,1)} %get-tuple-element.11.own_ref, bf16[128,512]{1,0:T(8,128)(2,1)S(1)} %copy-done.3), custom_call_target="tpu_custom_call" | custom-call | tf_op jit(solution)/shard_map/message/pallas_call | solution.py:294
  62.2 14.4 %all_to_all.42.recv_ref = bf16[8,144,128]{2,1,0:T(8,128)(2,1)S(1)} all-to-all(bf16[8,144,128]{2,1,0:T(8,128)(2,1)S(1)} %message.1), channel_id=1, replica_groups=mesh['cuts'=8,'dom'=32] {'cuts'}, dimensions={0} | all-to-all | bytes 589824 | tf_op jit(solution)/shard_map/all_to_all | solution.py:302
  76.6 1.8 %gates.1 = (bf16[128,128]{1,0:T(8,128)(2,1)}, f32[16,128]{1,0:T(8,128)S(1)}, bf16[32,16,128]{2,1,0:T(8,128)(2,1)S(1)}) custom-call(s32[1]{0:T(128)} %bitcast.refs_0_.cut_ref, bf16[8,144,128]{2,1,0:T(8,128)(2,1)S(1)} %all_to_all.42.recv_ref, bf16[128,2048]{1,0:T(8,128)(2,1)S(1)} %counts.1.count_ref, bf16[128,128]{1,0:T(8,128)(2,1)S(1)} %copy-done.7, ...), custom_call_target="tpu_custom_call" | custom-call | tf_op jit(solution)/shard_map/gates/pallas_call | solution.py:303
  78.4 12.3 %all_to_all.43.part_ref = bf16[32,16,128]{2,1,0:T(8,128)(2,1)S(1)} all-to-all(bf16[32,16,128]{2,1,0:T(8,128)(2,1)S(1)} %get-tuple-element.13), channel_id=1, replica_groups=mesh['cuts'=8,'dom'=32] {'dom'}, dimensions={0} | all-to-all | bytes 262144 | tf_op jit(solution)/shard_map/all_to_all | solution.py:249
  90.7 12.9 %all_to_all.44 = bf16[32,16,128]{2,1,0:T(8,128)(2,1)S(1)} all-to-all(bf16[32,16,128]{2,1,0:T(8,128)(2,1)S(1)} %first_grad.1), channel_id=1, replica_groups=mesh['cuts'=8,'dom'=32] {'dom'}, dimensions={0} | all-to-all | bytes 262144 | tf_op jit(solution)/shard_map/all_to_all | solution.py:249
  103.6 9.3 %all_to_all.45.mine_ref = bf16[4,32,16,128]{3,2,1,0:T(8,128)(2,1)S(1)} all-to-all(bf16[4,32,16,128]{3,2,1,0:T(8,128)(2,1)S(1)} %broadcast_in_dim.2), channel_id=1, replica_groups={{0,64,128,192},{32,96,160,224},{1,65,129,193},{33,97,161,225},{2,66,130..., dimensions={0} | all-to-all | bytes 1048576 | tf_op jit(solution)/shard_map/all_to_all | solution.py:252
  113.0 4.3 %collective-permute-start.1 = (bf16[4,32,16,128]{3,2,1,0:T(8,128)(2,1)S(1)}, bf16[4,32,16,128]{3,2,1,0:T(8,128)(2,1)S(1)}, u32[]{:S(2)}, u32[]{:S(2)}) collective-permute-start(bf16[4,32,16,128]{3,2,1,0:T(8,128)(2,1)S(1)} %all_to_all.45.mine_ref), channel_id=1, source_target_pairs={{0,32},{32,0},{64,96},{96,64},{128,160},{160,128},{192,224},{224,1... | collective-permute-start | bytes 1572872 | tf_op jit(solution)/shard_map/ppermute | solution.py:323
  117.3 1.5 %collective-permute-done.1.other_ref = bf16[4,32,16,128]{3,2,1,0:T(8,128)(2,1)S(1)} collective-permute-done((bf16[4,32,16,128]{3,2,1,0:T(8,128)(2,1)S(1)}, bf16[4,32,16,128]{3,2,1,0:T(8,128)(2,1)S(1)}, u32[]{:S(2)}, u32[]{:S(2)}) %collective-permute-start.1) | collective-permute-done | bytes 524320 | tf_op jit(solution)/shard_map/ppermute | solution.py:323
  118.8 4.2 %weight_grad.1 = bf16[32,16,128]{2,1,0:T(8,128)(2,1)S(1)} custom-call(s32[1]{0:T(128)S(6)} %select_n.7.core_ref, s32[64]{0:T(128)S(1)} %copy-done.10, s32[64]{0:T(128)S(1)} %copy-done.12, s32[1]{0:T(128)S(6)} %copy.17.count_ref, bf16[4,32,16,128]{3,2,1,0:T(8,128)(2,1)S(1)} %all_to_all.45.mine_ref, ...), custom_call_target="tpu_custom_call" | custom-call | tf_op jit(solution)/shard_map/weight_grad/pallas_call | solution.py:324
  123.1 12.4 %all_to_all.46 = bf16[32,16,128]{2,1,0:T(8,128)(2,1)S(1)} all-to-all(bf16[32,16,128]{2,1,0:T(8,128)(2,1)S(1)} %weight_grad.1), channel_id=1, replica_groups=mesh['cuts'=8,'dom'=32] {'dom'}, dimensions={0} | all-to-all | bytes 262144 | tf_op jit(solution)/shard_map/all_to_all | solution.py:249
  135.5 0.6 convert_reduce_fusion
  (32 shorter events, 0.6 us)
Async XLA Ops:
  1.3 1.6 %copy-start = (bf16[2048,512]{1,0:T(8,128)(2,1)S(1)}, bf16[2048,512]{1,0:T(8,128)(2,1)}, u32[]{:S(2)}) copy-start(bf16[2048,512]{1,0:T(8,128)(2,1)} %feats_hbm.3) | copy-start | bytes 6291460
  2.9 0.9 copy-start.4
  3.8 0.7 copy-start.9
  4.4 0.7 copy-start.11
  9.7 5.6 %collective-permute-start = (f32[4,512,128]{2,1,0:T(8,128)S(1)}, f32[4,512,128]{2,1,0:T(8,128)S(1)}, u32[]{:S(2)}, u32[]{:S(2)}) collective-permute-start(f32[4,512,128]{2,1,0:T(8,128)S(1)} %get-tuple-element.10), channel_id=1, source_target_pairs={{0,32},{32,0},{64,96},{96,64},{128,160},{160,128},{192,224},{224,1... | collective-permute-start | bytes 3145736 | tf_op jit(solution)/shard_map/ppermute | solution.py:270
  15.2 36.0 %copy-start.13 = (s32[128,8]{0,1:T(8,128)S(1)}, s32[128,8]{0,1:T(8,128)}, u32[]{:S(2)}) copy-start(s32[128,8]{0,1:T(8,128)} %param.18) | copy-start | bytes 12292
  15.2 36.2 %copy-start.14 = (s32[128,8]{0,1:T(8,128)S(1)}, s32[128,8]{0,1:T(8,128)}, u32[]{:S(2)}) copy-start(s32[128,8]{0,1:T(8,128)} %param.19) | copy-start | bytes 12292
  15.4 45.3 %copy-start.3 = (bf16[128,512]{1,0:T(8,128)(2,1)S(1)}, bf16[128,512]{1,0:T(8,128)(2,1)}, u32[]{:S(2)}) copy-start(bf16[128,512]{1,0:T(8,128)(2,1)} %w_edge_ref.1) | copy-start | bytes 393220
  27.0 49.6 %copy-start.5 = (bf16[128,384]{1,0:T(8,128)(2,1)S(1)}, bf16[128,384]{1,0:T(8,128)(2,1)}, u32[]{:S(2)}) copy-start(bf16[128,384]{1,0:T(8,128)(2,1)} %w_in_ref.1) | copy-start | bytes 294916
  27.0 49.6 %copy-start.6 = (bf16[128,256]{1,0:T(8,128)(2,1)S(1)}, bf16[128,256]{1,0:T(8,128)(2,1)}, u32[]{:S(2)}) copy-start(bf16[128,256]{1,0:T(8,128)(2,1)} %w_state_ref.1) | copy-start | bytes 196612
  27.0 49.6 %copy-start.7 = (bf16[128,128]{1,0:T(8,128)(2,1)S(1)}, bf16[128,128]{1,0:T(8,128)(2,1)}, u32[]{:S(2)}) copy-start(bf16[128,128]{1,0:T(8,128)(2,1)} %grad_ref.1) | copy-start | bytes 98308
  27.0 49.6 %copy-start.8 = (bf16[128,128]{1,0:T(8,128)(2,1)S(1)}, bf16[128,128]{1,0:T(8,128)(2,1)}, u32[]{:S(2)}) copy-start(bf16[128,128]{1,0:T(8,128)(2,1)} %w_cand_ref.1) | copy-start | bytes 98308
  47.4 13.3 %all-to-all-start.2 = ((bf16[32,16,128]{2,1,0:T(8,128)(2,1)}), bf16[32,16,128]{2,1,0:T(8,128)(2,1)S(1)}, u32[]{:S(2)}, u32[]{:S(2)}) async-start(bf16[32,16,128]{2,1,0:T(8,128)(2,1)} %get-tuple-element.11.own_ref), calls=%async_computation.2 | async-start | bytes 262144 | tf_op jit(solution)/shard_map/all_to_all | solution.py:249
  62.1 56.7 %copy-start.1 = (bf16[2048,512]{1,0:T(8,128)(2,1)S(1)}, bf16[2048,512]{1,0:T(8,128)(2,1)}, u32[]{:S(2)}) copy-start(bf16[2048,512]{1,0:T(8,128)(2,1)} %feats_hbm.3) | copy-start | bytes 6291460
  62.1 56.7 %copy-start.2 = (bf16[64,128,128]{2,1,0:T(8,128)(2,1)S(1)}, bf16[64,128,128]{2,1,0:T(8,128)(2,1)}, u32[]{:S(2)}) copy-start(bf16[64,128,128]{2,1,0:T(8,128)(2,1)} %adj_hbm.3) | copy-start | bytes 6291460
  62.1 56.7 %copy-start.10 = (s32[64]{0:T(128)S(1)}, s32[64]{0:T(128)}, u32[]{:S(2)}) copy-start(s32[64]{0:T(128)} %dst_ref.3) | copy-start | bytes 772
  62.2 56.7 %copy-start.12 = (s32[64]{0:T(128)S(1)}, s32[64]{0:T(128)}, u32[]{:S(2)}) copy-start(s32[64]{0:T(128)} %src_ref.3) | copy-start | bytes 772
  113.0 5.9 %collective-permute-start.1 = (bf16[4,32,16,128]{3,2,1,0:T(8,128)(2,1)S(1)}, bf16[4,32,16,128]{3,2,1,0:T(8,128)(2,1)S(1)}, u32[]{:S(2)}, u32[]{:S(2)}) collective-permute-start(bf16[4,32,16,128]{3,2,1,0:T(8,128)(2,1)S(1)} %all_to_all.45.mine_ref), channel_id=1, source_target_pairs={{0,32},{32,0},{64,96},{96,64},{128,160},{160,128},{192,224},{224,1... | collective-permute-start | bytes 1572872 | tf_op jit(solution)/shard_map/ppermute | solution.py:323

commit v2 on v1

v2 whole, which is shorter than its diff:
```python
import jax
import jax.numpy as jnp
from jax import lax
from jax.experimental import pallas as pl
from jax.experimental.pallas import tpu as pltpu
from jax.sharding import PartitionSpec as P

F32 = jnp.float32
BF16 = jnp.bfloat16
VMEM = pltpu.VMEM
SMEM = pltpu.SMEM


def vspec():
    return pl.BlockSpec(memory_space=pltpu.VMEM)


def sspec():
    return pl.BlockSpec(memory_space=pltpu.SMEM)


def hspec():
    return pl.BlockSpec(memory_space=pltpu.HBM)


def params():
    return pltpu.CompilerParams(vmem_limit_bytes=48 * 1024 * 1024)


def dot(a, b):
    return jnp.dot(a, b, preferred_element_type=F32)


def project_kernel(feats_hbm, w_hbm, out_ref, feats, w, sems, *, start):
    rows = feats.shape[0]
    parts = 4
    chunk = rows // parts
    w_copy = pltpu.make_async_copy(w_hbm, w, sems.at[parts])
    w_copy.start()
    copies = [
        pltpu.make_async_copy(
            feats_hbm.at[pl.ds(start + i * chunk, chunk)],
            feats.at[pl.ds(i * chunk, chunk)],
            sems.at[i],
        )
        for i in range(parts)
    ]
    for copy in copies:
        copy.start()
    w_copy.wait()
    for i in range(parts):
        copies[i].wait()
        at = pl.ds(i * chunk, chunk)
        out_ref[at, :] = dot(feats[at, :], w[...])


def own_rows(adj, slot, core, piece):
    pairs = adj.shape[1] // (2 * piece)
    return jnp.concatenate(
        [
            adj[slot, pl.ds(pl.multiple_of((2 * y + core) * piece, piece), piece), :]
            for y in range(pairs)
        ],
        axis=0,
    )


def partial_kernel(
    core_ref, dst_ref, src_ref, count_ref, adj, *refs, near, far,
):
    parts = refs[: -3]
    out_ref, projected, acc = refs[-3:]
    slots, block, _ = adj.shape
    pairs = acc.shape[0]
    piece = acc.shape[1] // (near * far)
    hidden = acc.shape[2]
    half = len(parts) // 2
    rows = parts[0].shape[0]
    acc[...] = jnp.zeros_like(acc)
    for i in range(half):
        both = parts[i][...] + parts[half + i][...]
        high = both.astype(BF16)
        at = pl.ds(i * rows, rows)
        projected[at, :hidden] = high
        projected[at, hidden:] = (both - high.astype(F32)).astype(BF16)
    core = core_ref[0]
    count = count_ref[0]
    step = 8

    def some_slots(group, carry):
        for j in range(step):
            slot = group * step + j
            right = projected[pl.ds(pl.multiple_of(src_ref[slot] * block, block), block), :]
            result = dot(own_rows(adj, slot, core, piece), right)
            result = result[:, :hidden] + result[:, hidden:]
            result = jnp.where(slot < count, result, 0.0)
            d = dst_ref[slot]
            place = ((d % near) * far + d // near) * piece
            at = pl.ds(pl.multiple_of(place, piece), piece)
            for y in range(pairs):
                acc[y, at, :] += result[y * piece : (y + 1) * piece]
        return carry

    lax.fori_loop(0, slots // step, some_slots, 0)
    out_ref[...] = acc[...].astype(BF16).reshape(out_ref.shape)


def count_kernel(cut_ref, nbr_ref, type_ref, count_ref, *, cuts, block):
    rows, fanout = nbr_ref.shape
    cells = count_ref.shape[1]
    piece = block // cuts
    nbr = nbr_ref[...]
    within = nbr % block
    local = (nbr // block) * piece + within % piece
    per_type = cells // 4
    key = jnp.where(within // piece == cut_ref[0], type_ref[...] * per_type + local, -1)
    tile = 512
    for start in range(0, cells, tile):
        place = lax.broadcasted_iota(jnp.int32, (rows, tile), 1) + start
        total = jnp.zeros((rows, tile), F32)
        for k in range(fanout):
            total += jnp.where(key[:, k : k + 1] == place, 1.0, 0.0)
        count_ref[:, start : start + tile] = total.astype(BF16)


def state_kernel(part_ref, first_ref, out_ref):
    total = jnp.sum(part_ref[...].astype(F32), axis=0)
    exact = jnp.tanh(total)
    first_ref[...] = exact
    states = exact.astype(BF16)
    for q in range(out_ref.shape[0]):
        out_ref[q] = states


def message_kernel(count_ref, states_ref, own_ref, w_ref, out_ref):
    hidden = own_ref.shape[2]
    rows = count_ref.shape[0]
    domains, piece, _ = states_ref.shape
    local = domains * piece
    states = states_ref[...].reshape(local, hidden)
    message = jnp.zeros((rows, hidden), F32)
    for e in range(count_ref.shape[1] // local):
        picked = dot(count_ref[:, e * local : (e + 1) * local], states).astype(BF16)
        message += dot(picked, w_ref[:, e * hidden : (e + 1) * hidden])
    message = message.astype(BF16)
    for c in range(out_ref.shape[0]):
        out_ref[c, :rows] = message
        out_ref[c, rows:] = own_ref[0]


def gate_kernel(
    cut_ref, recv_ref, count_ref, grad_ref, w_edge_ref, w_in_ref, w_state_ref, w_cand_ref,
    new_ref, direct_ref, back_ref, own,
):
    rows, hidden = grad_ref.shape
    cuts = recv_ref.shape[0]
    piece = recv_ref.shape[1] - rows
    local = count_ref.shape[1] // 4
    message = jnp.sum(recv_ref[:, :rows, :].astype(F32), axis=0)
    states = recv_ref[:, rows:, :].reshape(cuts * piece, hidden)
    message_in = message.astype(BF16)
    w_in = w_in_ref[...]
    w_state = w_state_ref[...]
    w_cand = w_cand_ref[...]
    gate_in = dot(message_in, w_in)
    gate_state = dot(states, w_state)
    value = states.astype(F32)
    update = jax.nn.sigmoid(gate_in[:, :hidden] + gate_state[:, :hidden])
    reset = jax.nn.sigmoid(gate_in[:, hidden : 2 * hidden] + gate_state[:, hidden:])
    candidate = jnp.tanh(gate_in[:, 2 * hidden :] + dot((reset * value).astype(BF16), w_cand))
    new_ref[...] = ((1.0 - update) * candidate + update * value).astype(BF16)
    out_grad = grad_ref[...].astype(F32)
    cand_pre = out_grad * (1.0 - update) * (1.0 - candidate * candidate)
    update_pre = out_grad * (value - candidate) * update * (1.0 - update)
    contract = (((1,), (1,)), ((), ()))
    cand_grad = cand_pre.astype(BF16)
    reset_in = lax.dot_general(cand_grad, w_cand, contract, preferred_element_type=F32)
    reset_pre = reset_in * value * reset * (1.0 - reset)
    gates = jnp.concatenate([update_pre.astype(BF16), reset_pre.astype(BF16), cand_grad], axis=1)
    message_grad_t = lax.dot_general(w_in, gates, contract, preferred_element_type=F32).astype(BF16)
    own[...] = (
        out_grad * update
        + reset_in * reset
        + lax.dot_general(gates[:, : 2 * hidden], w_state, contract, preferred_element_type=F32)
    )
    direct_ref[...] = own[pl.ds(pl.multiple_of(cut_ref[0] * piece, piece), piece), :]
    total = jnp.zeros((hidden, local), F32)
    for e in range(count_ref.shape[1] // local):
        spread = dot(message_grad_t, count_ref[:, e * local : (e + 1) * local]).astype(BF16)
        total += dot(w_edge_ref[:, e * hidden : (e + 1) * hidden], spread)
    back_ref[...] = total.T.astype(BF16).reshape(back_ref.shape)


def grad_kernel(part_ref, direct_ref, exact_ref, out_ref):
    total = direct_ref[...] + jnp.sum(part_ref[...].astype(F32), axis=0)
    exact = exact_ref[...]
    grad = (total * (1.0 - exact * exact)).astype(BF16)
    for q in range(out_ref.shape[0]):
        out_ref[q] = grad


def spread_kernel(
    core_ref, dst_ref, src_ref, count_ref, grads_ref, adj, out_ref, turned, acc, *, near, far
):
    slots, block, _ = adj.shape
    hidden = grads_ref.shape[2]
    piece = grads_ref.shape[1] // far
    pairs = grads_ref.shape[0] // near
    acc[...] = jnp.zeros_like(acc)
    for z in range(far):
        for x in range(near):
            rows = jnp.concatenate(
                [grads_ref[y * near + x, z * piece : (z + 1) * piece, :] for y in range(pairs)],
                axis=0,
            )
            turned[z * near + x] = rows.T
    core = core_ref[0]
    count = count_ref[0]
    step = 8

    def some_slots(group, carry):
        for j in range(step):
            slot = group * step + j
            result = dot(turned[dst_ref[slot]], own_rows(adj, slot, core, piece))
            acc[src_ref[slot]] += jnp.where(slot < count, result, 0.0)
        return carry

    lax.fori_loop(0, slots // step, some_slots, 0)
    for s in range(acc.shape[0]):
        out_ref[:, s * block : (s + 1) * block] = acc[s].astype(BF16)


def weight_kernel(spread_ref, feats_ref, out_ref):
    out_ref[...] = dot(spread_ref[...], feats_ref[...])


def weight_out_kernel(spread_ref, feats_ref, part_ref, out_ref):
    total = part_ref[...] + dot(spread_ref[...], feats_ref[...])
    out_ref[...] = total.T.astype(BF16).reshape(out_ref.shape)


def body(
    feats,
    adjacency,
    blk_dst,
    blk_src,
    blk_count,
    nbr_ids,
    edge_types,
    w_first,
    w_edge,
    w_gate_in,
    w_gate_state,
    w_cand,
    out_grad,
):
    slots, block, _ = adjacency.shape
    nodes, feat_cols = feats.shape
    hidden = w_first.shape[1]
    rows = out_grad.shape[0]
    far = lax.axis_size("z")
    near = lax.axis_size("x")
    pairs = lax.axis_size("y")
    domains = far * near
    cuts = 2 * pairs
    piece = block // cuts
    local = domains * piece
    core = lax.axis_index("core").reshape(1)
    cut = (2 * lax.axis_index("y") + lax.axis_index("core")).reshape(1)

    def over_dom(x):
        return lax.all_to_all(x, ("z", "x"), 0, 0, tiled=True)

    def over_plane(x):
        return lax.all_to_all(x, ("y", "x"), 0, 0, tiled=True)

    def over_far(x):
        return lax.all_to_all(x, "z", 0, 0, tiled=True)

    def swap(x):
        return lax.ppermute(x, "core", [(0, 1), (1, 0)])

    halves = 2
    rows_half = nodes // halves
    projected = [
        pl.pallas_call(
            lambda *refs, i=i: project_kernel(*refs, start=i * rows_half),
            out_shape=jax.ShapeDtypeStruct((rows_half, hidden), F32),
            in_specs=[hspec(), hspec()],
            out_specs=vspec(),
            scratch_shapes=[
                VMEM((rows_half, feat_cols), BF16),
                VMEM((feat_cols, hidden), BF16),
                pltpu.SemaphoreType.DMA((5,)),
            ],
            compiler_params=params(),
            name=f"project{i}",
        )(feats, w_first)
        for i in range(halves)
    ]
    swapped = [swap(p) for p in projected]
    counts = pl.pallas_call(
        lambda *refs: count_kernel(*refs, cuts=cuts, block=block),
        out_shape=jax.ShapeDtypeStruct((rows, 4 * local), BF16),
        in_specs=[sspec(), vspec(), vspec()],
        out_specs=vspec(),
        compiler_params=params(),
        name="counts",
    )(cut, nbr_ids, edge_types)
    partial = pl.pallas_call(
        lambda *refs: partial_kernel(*refs, near=near, far=far),
        out_shape=jax.ShapeDtypeStruct((pairs * near, far * piece, hidden), BF16),
        in_specs=[sspec()] * 4 + [vspec()] * (1 + 2 * halves),
        out_specs=vspec(),
        scratch_shapes=[VMEM((nodes, 2 * hidden), BF16), VMEM((pairs, local, hidden), F32)],
        compiler_params=params(),
        name="partial",
    )(core, blk_dst, blk_src, blk_count, adjacency, *projected, *swapped)
    by_plane = jnp.sum(over_plane(partial).astype(F32), axis=0)
    by_far = over_far(by_plane.reshape(far, piece, hidden))
    spread = jax.ShapeDtypeStruct((domains, piece, hidden), BF16)
    small = jax.ShapeDtypeStruct((piece, hidden), F32)
    exact, own_states = pl.pallas_call(
        state_kernel,
        out_shape=(small, spread),
        in_specs=[vspec()],
        out_specs=(vspec(), vspec()),
        compiler_params=params(),
        name="state",
    )(by_far)
    states = over_dom(own_states)
    sent = pl.pallas_call(
        message_kernel,
        out_shape=jax.ShapeDtypeStruct((cuts, rows + piece, hidden), BF16),
        in_specs=[vspec(), vspec(), vspec(), vspec()],
        out_specs=vspec(),
        compiler_params=params(),
        name="message",
    )(counts, states, own_states, w_edge)
    recv = lax.all_to_all(sent, ("y", "core"), 0, 0, tiled=True)
    new_state, direct, back = pl.pallas_call(
        gate_kernel,
        out_shape=(jax.ShapeDtypeStruct((rows, hidden), BF16), small, spread),
        in_specs=[sspec()] + [vspec()] * 7,
        out_specs=(vspec(), vspec(), vspec()),
        scratch_shapes=[VMEM((rows, hidden), F32)],
        compiler_params=params(),
        name="gates",
    )(cut, recv, counts, out_grad, w_edge, w_gate_in, w_gate_state, w_cand)
    grad_part = over_dom(back)
    own_grad = pl.pallas_call(
        grad_kernel,
        out_shape=jax.ShapeDtypeStruct((far, piece, hidden), BF16),
        in_specs=[vspec()] * 3,
        out_specs=vspec(),
        compiler_params=params(),
        name="first_grad",
    )(grad_part, direct, exact)
    far_grads = over_far(own_grad).reshape(1, far * piece, hidden)
    grads = over_plane(jnp.broadcast_to(far_grads, (pairs * near, far * piece, hidden)))
    mine = pl.pallas_call(
        lambda *refs: spread_kernel(*refs, near=near, far=far),
        out_shape=jax.ShapeDtypeStruct((hidden, nodes), BF16),
        in_specs=[sspec()] * 4 + [vspec()] * 2,
        out_specs=vspec(),
        scratch_shapes=[
            VMEM((domains, hidden, pairs * piece), BF16),
            VMEM((nodes // block, hidden, block), F32),
        ],
        compiler_params=params(),
        name="spread",
    )(core, blk_dst, blk_src, blk_count, grads, adjacency)
    other = swap(mine)
    own_part = pl.pallas_call(
        weight_kernel,
        out_shape=jax.ShapeDtypeStruct((hidden, feat_cols), F32),
        in_specs=[vspec()] * 2,
        out_specs=vspec(),
        compiler_params=params(),
        name="weight_own",
    )(mine, feats)
    weight_part = pl.pallas_call(
        weight_out_kernel,
        out_shape=jax.ShapeDtypeStruct((domains, feat_cols // domains, hidden), BF16),
        in_specs=[vspec()] * 3,
        out_specs=vspec(),
        compiler_params=params(),
        name="weight_all",
    )(other, feats, own_part)
    w_first_grad = jnp.sum(over_dom(weight_part).astype(F32), axis=0)
    return (new_state, w_first_grad)


def solution(mesh):
    cuts, domains = mesh.devices.shape
    fine = jax.sharding.Mesh(
        mesh.devices.reshape(cuts // 2, 2, domains // 4, 4), ("y", "core", "z", "x")
    )
    dom = ("z", "x")
    cut = ("y", "core")
    return jax.shard_map(
        body,
        mesh=fine,
        in_specs=(
            P(dom, cut),
            P(dom, None, None),
            P(dom),
            P(dom),
            P(dom),
            P(dom, None),
            P(dom, None),
            P(cut, None),
            P(),
            P(),
            P(),
            P(),
            P(dom, None),
        ),
        out_specs=(P(dom, None), P(cut + dom, None)),
        check_vma=False,
    )
```

time: 137 us -> 134 us (0.978)
  waiting for transfers between devices: 12 us -> 10.6 us
    ppermute x2 -> x3, waiting for transfers between devices: 3.82 us -> 2.42 us  [swap(): return lax.ppermute(x, 'core', [(0, 1), (1, 0)])]
    unnamed x32 -> x28, local copies, waits for them, and re-layouts: 4.06 us -> 2.75 us
    pallas_call x3 -> x7, Pallas kernels: 8.83 us -> 9.47 us  [the longest x1 3.42 us: body(): pl.pallas_call(lambda *refs: partial_kernel(*refs, near=near, far=far), o...]
    ppermute x2 -> x3, starting transfers between devices: 7.62 us -> 7.92 us  [swap(): return lax.ppermute(x, 'core', [(0, 1), (1, 0)])]
  transfers between devices with their start and end apart: 3 -> 4, of which waited for: 3 -> 3; matrix products, arithmetic and copies ran while one was open for 0% -> 0% of each run, Pallas kernels for 1% -> 2%
where the time goes in v2:
time: 134 us; the launch traced here: 133 us
  blocking collectives  91.5 us (68%)
  Pallas kernels  14.4 us (11%)
  starting transfers between devices  11.8 us (9%)
  waiting for transfers between devices  10.6 us (8%)
  local copies, waits for them, and re-layouts  2.85 us (2%)
  between operations  1.49 us (1%)
    all_to_all x2, blocking collectives, over_plane(): return lax.all_to_all(x, ('y', 'x'), 0, 0, tiled=True)  28 us
    all_to_all x2, blocking collectives, over_dom(): return lax.all_to_all(x, ('z', 'x'), 0, 0, tiled=True)  25.1 us
    all_to_all x2, blocking collectives, over_far(): return lax.all_to_all(x, 'z', 0, 0, tiled=True)  24.7 us
    all_to_all x1, blocking collectives, body(): recv = lax.all_to_all(sent, ('y', 'core'), 0, 0, tiled=True)  13.7 us
    all_to_all x1, waiting for transfers between devices, over_dom(): return lax.all_to_all(x, ('z', 'x'), 0, 0, tiled=True)  8.14 us
    ppermute x3, starting transfers between devices, swap(): return lax.ppermute(x, 'core', [(0, 1), (1, 0)])  7.92 us
    all_to_all x1, starting transfers between devices, over_dom(): return lax.all_to_all(x, ('z', 'x'), 0, 0, tiled=True)  3.85 us
    pallas_call x1, Pallas kernels, body(): pl.pallas_call(lambda *refs: partial_kernel(*refs, near=near, far=far), o...  3.42 us
  transfers between devices with their start and end apart: 4, of which 3 were waited for; matrix products, arithmetic and copies ran while one was open for 0% of the time, Pallas kernels for 2%

profile of v2, /device:TPU:1, one launch (start us, length us, event | category | flops | bytes accessed | tf_op | source)
XLA Modules:
  0.0 133.3 jit_solution(13824255929848429130)
XLA Ops:
  0.6 1.6 %copy-done = bf16[2048,512]{1,0:T(8,128)(2,1)S(1)} copy-done((bf16[2048,512]{1,0:T(8,128)(2,1)S(1)}, bf16[2048,512]{1,0:T(8,128)(2,1)}, u32[]{:S(2)}) %copy-start) | copy-done | bytes 2097176
  2.2 0.9 copy-done.4
  3.1 1.1 project0.1.refs_5_
  4.3 3.3 %collective-permute-start = (f32[1024,128]{1,0:T(8,128)S(1)}, f32[1024,128]{1,0:T(8,128)}, u32[]{:S(2)}, u32[]{:S(2)}) collective-permute-start(f32[1024,128]{1,0:T(8,128)S(1)} %project0.1.refs_5_), channel_id=1, source_target_pairs={{0,32},{32,0},{1,33},{33,1},{2,34},{34,2},{3,35},{35,3},{4,36},{36... | collective-permute-start | bytes 1572872 | tf_op jit(solution)/shard_map/ppermute | solution.py:281
  7.6 1.1 project1.1.refs_6_
  9.5 1.3 collective-permute-done.1.refs_8_
  10.8 3.4 %partial.1 = bf16[16,128,128]{2,1,0:T(8,128)(2,1)S(1)} custom-call(s32[1]{0:T(128)} %bitcast.1.refs_0_, s32[64]{0:T(128)S(1)} %copy-done.9, s32[64]{0:T(128)S(1)} %copy-done.10, s32[1]{0:T(128)S(6)} %copy.17.refs_3_, bf16[64,128,128]{2,1,0:T(8,128)(2,1)S(1)} %copy-done.2, f32[1024,128]{1,0:T(8,128)S(1)} %project0.1.refs_5_, ...), custom_call_target="tpu_custom_call" | custom-call | tf_op jit(solution)/shard_map/partial/pallas_call | solution.py:310
  14.4 15.9 %all_to_all.40 = bf16[16,128,128]{2,1,0:T(8,128)(2,1)S(1)} all-to-all(bf16[16,128,128]{2,1,0:T(8,128)(2,1)S(1)} %partial.1), channel_id=1, replica_groups=mesh['y'=4,'core'=2,'z'=8,'x'=4] {'y','x'}, dimensions={0} | all-to-all | bytes 1048576 | tf_op jit(solution)/shard_map/all_to_all | solution.py:275
  30.3 15.4 %all_to_all.41.part_ref = f32[8,16,128]{2,1,0:T(8,128)S(1)} all-to-all(f32[8,16,128]{2,1,0:T(8,128)S(1)} %bitcast.4), channel_id=1, replica_groups=mesh['y'=4,'core'=2,'z'=8,'x'=4] {'z'}, dimensions={0} | all-to-all | bytes 131072 | tf_op jit(solution)/shard_map/all_to_all | solution.py:278
  45.7 0.7 state.1
  46.3 3.9 %all-to-all-start.2 = ((bf16[32,16,128]{2,1,0:T(8,128)(2,1)}), bf16[32,16,128]{2,1,0:T(8,128)(2,1)S(1)}, u32[]{:S(2)}, u32[]{:S(2)}) async-start(bf16[32,16,128]{2,1,0:T(8,128)(2,1)} %get-tuple-element.7.own_ref), calls=%async_computation.2 | async-start | bytes 262144 | tf_op jit(solution)/shard_map/all_to_all | solution.py:272
  50.4 1.0 counts.1.count_ref
  51.5 8.1 %all-to-all-done.2.states_ref = bf16[32,16,128]{2,1,0:T(8,128)(2,1)S(1)} async-done(((bf16[32,16,128]{2,1,0:T(8,128)(2,1)}), bf16[32,16,128]{2,1,0:T(8,128)(2,1)S(1)}, u32[]{:S(2)}, u32[]{:S(2)}) %all-to-all-start.2) | async-done | bytes 131104 | tf_op jit(solution)/shard_map/all_to_all | solution.py:272
  59.6 1.4 %message.1 = bf16[8,144,128]{2,1,0:T(8,128)(2,1)S(1)} custom-call(bf16[128,2048]{1,0:T(8,128)(2,1)S(1)} %counts.1.count_ref, bf16[32,16,128]{2,1,0:T(8,128)(2,1)S(1)} %all-to-all-done.2.states_ref, bf16[32,16,128]{2,1,0:T(8,128)(2,1)} %get-tuple-element.7.own_ref, bf16[128,512]{1,0:T(8,128)(2,1)S(1)} %copy-done.3), custom_call_target="tpu_custom_call" | custom-call | tf_op jit(solution)/shard_map/message/pallas_call | solution.py:332
  61.0 13.7 %all_to_all.42.recv_ref = bf16[8,144,128]{2,1,0:T(8,128)(2,1)S(1)} all-to-all(bf16[8,144,128]{2,1,0:T(8,128)(2,1)S(1)} %message.1), channel_id=1, replica_groups=mesh['y'=4,'core'=2,'z'=8,'x'=4] {'y','core'}, dimensions={0} | all-to-all | bytes 589824 | tf_op jit(solution)/shard_map/all_to_all | solution.py:340
  74.8 1.8 %gates.1 = (bf16[128,128]{1,0:T(8,128)(2,1)}, f32[16,128]{1,0:T(8,128)S(1)}, bf16[32,16,128]{2,1,0:T(8,128)(2,1)S(1)}) custom-call(s32[1]{0:T(128)} %bitcast.refs_0_.cut_ref, bf16[8,144,128]{2,1,0:T(8,128)(2,1)S(1)} %all_to_all.42.recv_ref, bf16[128,2048]{1,0:T(8,128)(2,1)S(1)} %counts.1.count_ref, bf16[128,128]{1,0:T(8,128)(2,1)S(1)} %copy-done.7, ...), custom_call_target="tpu_custom_call" | custom-call | tf_op jit(solution)/shard_map/gates/pallas_call | solution.py:341
  76.6 12.4 %all_to_all.43.part_ref = bf16[32,16,128]{2,1,0:T(8,128)(2,1)S(1)} all-to-all(bf16[32,16,128]{2,1,0:T(8,128)(2,1)S(1)} %get-tuple-element.9), channel_id=1, replica_groups=mesh['y'=4,'core'=2,'z'=8,'x'=4] {'z','x'}, dimensions={0} | all-to-all | bytes 262144 | tf_op jit(solution)/shard_map/all_to_all | solution.py:272
  89.0 9.3 %all_to_all.44 = bf16[8,16,128]{2,1,0:T(8,128)(2,1)S(1)} all-to-all(bf16[8,16,128]{2,1,0:T(8,128)(2,1)S(1)} %first_grad.1), channel_id=1, replica_groups=mesh['y'=4,'core'=2,'z'=8,'x'=4] {'z'}, dimensions={0} | all-to-all | bytes 65536 | tf_op jit(solution)/shard_map/all_to_all | solution.py:278
  98.4 12.1 %all_to_all.45.refs_4_ = bf16[16,128,128]{2,1,0:T(8,128)(2,1)S(1)} all-to-all(bf16[16,128,128]{2,1,0:T(8,128)(2,1)S(1)} %broadcast_in_dim.8), channel_id=1, replica_groups=mesh['y'=4,'core'=2,'z'=8,'x'=4] {'y','x'}, dimensions={0} | all-to-all | bytes 1048576 | tf_op jit(solution)/shard_map/all_to_all | solution.py:275
  110.5 2.8 %spread.1.spread_ref = bf16[128,2048]{1,0:T(8,128)(2,1)S(1)} custom-call(s32[1]{0:T(128)} %bitcast.1.refs_0_, s32[64]{0:T(128)S(1)} %copy-done.9, s32[64]{0:T(128)S(1)} %copy-done.10, s32[1]{0:T(128)S(6)} %copy.17.refs_3_, bf16[16,128,128]{2,1,0:T(8,128)(2,1)S(1)} %all_to_all.45.refs_4_, bf16[64,128,128]{2,1,0:T(8,128)(2,1)S(1)} %copy-done.2), custom_call_target="tpu_custom_call" | custom-call | tf_op jit(solution)/shard_map/spread/pallas_call | solution.py:361
  113.3 4.5 %collective-permute-start.2 = (bf16[128,2048]{1,0:T(8,128)(2,1)S(1)}, bf16[128,2048]{1,0:T(8,128)(2,1)S(1)}, u32[]{:S(2)}, u32[]{:S(2)}) collective-permute-start(bf16[128,2048]{1,0:T(8,128)(2,1)S(1)} %spread.1.spread_ref), channel_id=1, source_target_pairs={{0,32},{32,0},{1,33},{33,1},{2,34},{34,2},{3,35},{35,3},{4,36},{36... | collective-permute-start | bytes 1572872 | tf_op jit(solution)/shard_map/ppermute | solution.py:281
  118.3 1.1 collective-permute-done.2.spread_ref
  119.9 12.7 %all_to_all.46 = bf16[32,16,128]{2,1,0:T(8,128)(2,1)S(1)} all-to-all(bf16[32,16,128]{2,1,0:T(8,128)(2,1)S(1)} %weight_all.1), channel_id=1, replica_groups=mesh['y'=4,'core'=2,'z'=8,'x'=4] {'z','x'}, dimensions={0} | all-to-all | bytes 262144 | tf_op jit(solution)/shard_map/all_to_all | solution.py:272
  132.6 0.6 convert_reduce_fusion.1
  (33 shorter events, 1.6 us)
Async XLA Ops:
  0.6 1.6 %copy-start = (bf16[2048,512]{1,0:T(8,128)(2,1)S(1)}, bf16[2048,512]{1,0:T(8,128)(2,1)}, u32[]{:S(2)}) copy-start(bf16[2048,512]{1,0:T(8,128)(2,1)} %feats_ref.3) | copy-start | bytes 6291460
  2.2 0.9 copy-start.4
  3.1 7.7 %copy-start.2 = (bf16[64,128,128]{2,1,0:T(8,128)(2,1)S(1)}, bf16[64,128,128]{2,1,0:T(8,128)(2,1)}, u32[]{:S(2)}) copy-start(bf16[64,128,128]{2,1,0:T(8,128)(2,1)} %refs_5_.1) | copy-start | bytes 6291460
  3.1 7.7 %copy-start.9 = (s32[64]{0:T(128)S(1)}, s32[64]{0:T(128)}, u32[]{:S(2)}) copy-start(s32[64]{0:T(128)} %refs_1_.8) | copy-start | bytes 772
  3.1 7.7 %copy-start.10 = (s32[64]{0:T(128)S(1)}, s32[64]{0:T(128)}, u32[]{:S(2)}) copy-start(s32[64]{0:T(128)} %refs_2_.4) | copy-start | bytes 772
  4.3 5.2 %collective-permute-start = (f32[1024,128]{1,0:T(8,128)S(1)}, f32[1024,128]{1,0:T(8,128)}, u32[]{:S(2)}, u32[]{:S(2)}) collective-permute-start(f32[1024,128]{1,0:T(8,128)S(1)} %project0.1.refs_5_), channel_id=1, source_target_pairs={{0,32},{32,0},{1,33},{33,1},{2,34},{34,2},{3,35},{35,3},{4,36},{36... | collective-permute-start | bytes 1572872 | tf_op jit(solution)/shard_map/ppermute | solution.py:281
  8.7 2.1 %collective-permute-start.1 = (f32[1024,128]{1,0:T(8,128)S(1)}, f32[1024,128]{1,0:T(8,128)}, u32[]{:S(2)}, u32[]{:S(2)}) collective-permute-start(f32[1024,128]{1,0:T(8,128)S(1)} %project1.1.refs_6_), channel_id=1, source_target_pairs={{0,32},{32,0},{1,33},{33,1},{2,34},{34,2},{3,35},{35,3},{4,36},{36... | collective-permute-start | bytes 1572872 | tf_op jit(solution)/shard_map/ppermute | solution.py:281
  14.3 35.9 %copy-start.11 = (s32[128,8]{0,1:T(8,128)S(1)}, s32[128,8]{0,1:T(8,128)}, u32[]{:S(2)}) copy-start(s32[128,8]{0,1:T(8,128)} %param.18) | copy-start | bytes 12292
  14.3 36.0 %copy-start.12 = (s32[128,8]{0,1:T(8,128)S(1)}, s32[128,8]{0,1:T(8,128)}, u32[]{:S(2)}) copy-start(s32[128,8]{0,1:T(8,128)} %param.19) | copy-start | bytes 12292
  14.3 45.3 %copy-start.3 = (bf16[128,512]{1,0:T(8,128)(2,1)S(1)}, bf16[128,512]{1,0:T(8,128)(2,1)}, u32[]{:S(2)}) copy-start(bf16[128,512]{1,0:T(8,128)(2,1)} %w_edge_ref.1) | copy-start | bytes 393220
  14.3 60.5 %copy-start.5 = (bf16[128,384]{1,0:T(8,128)(2,1)S(1)}, bf16[128,384]{1,0:T(8,128)(2,1)}, u32[]{:S(2)}) copy-start(bf16[128,384]{1,0:T(8,128)(2,1)} %w_in_ref.1) | copy-start | bytes 294916
  14.3 60.5 %copy-start.6 = (bf16[128,256]{1,0:T(8,128)(2,1)S(1)}, bf16[128,256]{1,0:T(8,128)(2,1)}, u32[]{:S(2)}) copy-start(bf16[128,256]{1,0:T(8,128)(2,1)} %w_state_ref.1) | copy-start | bytes 196612
  14.3 60.5 %copy-start.7 = (bf16[128,128]{1,0:T(8,128)(2,1)S(1)}, bf16[128,128]{1,0:T(8,128)(2,1)}, u32[]{:S(2)}) copy-start(bf16[128,128]{1,0:T(8,128)(2,1)} %grad_ref.1) | copy-start | bytes 98308
  14.3 60.4 %copy-start.8 = (bf16[128,128]{1,0:T(8,128)(2,1)S(1)}, bf16[128,128]{1,0:T(8,128)(2,1)}, u32[]{:S(2)}) copy-start(bf16[128,128]{1,0:T(8,128)(2,1)} %w_cand_ref.1) | copy-start | bytes 98308
  46.3 13.3 %all-to-all-start.2 = ((bf16[32,16,128]{2,1,0:T(8,128)(2,1)}), bf16[32,16,128]{2,1,0:T(8,128)(2,1)S(1)}, u32[]{:S(2)}, u32[]{:S(2)}) async-start(bf16[32,16,128]{2,1,0:T(8,128)(2,1)} %get-tuple-element.7.own_ref), calls=%async_computation.2 | async-start | bytes 262144 | tf_op jit(solution)/shard_map/all_to_all | solution.py:272
  98.4 19.4 %copy-start.1 = (bf16[2048,512]{1,0:T(8,128)(2,1)S(1)}, bf16[2048,512]{1,0:T(8,128)(2,1)}, u32[]{:S(2)}) copy-start(bf16[2048,512]{1,0:T(8,128)(2,1)} %feats_ref.3) | copy-start | bytes 6291460
  113.3 6.0 %collective-permute-start.2 = (bf16[128,2048]{1,0:T(8,128)(2,1)S(1)}, bf16[128,2048]{1,0:T(8,128)(2,1)S(1)}, u32[]{:S(2)}, u32[]{:S(2)}) collective-permute-start(bf16[128,2048]{1,0:T(8,128)(2,1)S(1)} %spread.1.spread_ref), channel_id=1, source_target_pairs={{0,32},{32,0},{1,33},{33,1},{2,34},{34,2},{3,35},{35,3},{4,36},{36... | collective-permute-start | bytes 1572872 | tf_op jit(solution)/shard_map/ppermute | solution.py:281

commit v3 on v2

--- a/solution.py
+++ b/solution.py
@@ -23,8 +23,22 @@
     return pl.BlockSpec(memory_space=pltpu.HBM)
 
 
+def aspec():
+    return pl.BlockSpec(memory_space=pl.ANY)
+
+
+def start_all(pairs, sems):
+    copies = [
+        pltpu.make_async_copy(source, target, sems.at[i])
+        for i, (source, target) in enumerate(pairs)
+    ]
+    for copy in copies:
+        copy.start()
+    return copies
+
+
 def params():
-    return pltpu.CompilerParams(vmem_limit_bytes=48 * 1024 * 1024)
+    return pltpu.CompilerParams(vmem_limit_bytes=12 * 1024 * 1024)
 
 
 def dot(a, b):
@@ -66,10 +80,13 @@
 
 
 def partial_kernel(
-    core_ref, dst_ref, src_ref, count_ref, adj, *refs, near, far,
+    core_ref, dst_any, src_any, count_any, counts_any, adj, *refs, near, far,
 ):
-    parts = refs[: -3]
-    out_ref, projected, acc = refs[-3:]
+    parts = refs[:-7]
+    out_ref, projected, acc, dst_ref, src_ref, count_ref, sems = refs[-7:]
+    copies = start_all(
+        [(dst_any, dst_ref), (src_any, src_ref), (count_any, count_ref)], sems
+    )
     slots, block, _ = adj.shape
     pairs = acc.shape[0]
     piece = acc.shape[1] // (near * far)
@@ -83,6 +100,8 @@
         at = pl.ds(i * rows, rows)
         projected[at, :hidden] = high
         projected[at, hidden:] = (both - high.astype(F32)).astype(BF16)
+    for copy in copies:
+        copy.wait()
     core = core_ref[0]
     count = count_ref[0]
     step = 8
@@ -123,17 +142,18 @@
         count_ref[:, start : start + tile] = total.astype(BF16)
 
 
-def state_kernel(part_ref, first_ref, out_ref):
+def state_kernel(part_ref, first_ref, own_ref, out_ref):
     total = jnp.sum(part_ref[...].astype(F32), axis=0)
     exact = jnp.tanh(total)
     first_ref[...] = exact
     states = exact.astype(BF16)
+    own_ref[...] = states
     for q in range(out_ref.shape[0]):
         out_ref[q] = states
 
 
 def message_kernel(count_ref, states_ref, own_ref, w_ref, out_ref):
-    hidden = own_ref.shape[2]
+    hidden = own_ref.shape[1]
     rows = count_ref.shape[0]
     domains, piece, _ = states_ref.shape
     local = domains * piece
@@ -145,7 +165,7 @@
     message = message.astype(BF16)
     for c in range(out_ref.shape[0]):
         out_ref[c, :rows] = message
-        out_ref[c, rows:] = own_ref[0]
+        out_ref[c, rows:] = own_ref[...]
 
 
 def gate_kernel(
@@ -200,12 +220,16 @@
 
 
 def spread_kernel(
-    core_ref, dst_ref, src_ref, count_ref, grads_ref, adj, out_ref, turned, acc, *, near, far
+    core_ref, dst_any, src_any, count_any, new_any, grads_ref, adj, out_ref, new_out,
+    turned, acc, dst_ref, src_ref, count_ref, sems, *, near, far,
 ):
     slots, block, _ = adj.shape
     hidden = grads_ref.shape[2]
     piece = grads_ref.shape[1] // far
     pairs = grads_ref.shape[0] // near
+    copies = start_all(
+        [(dst_any, dst_ref), (src_any, src_ref), (count_any, count_ref), (new_any, new_out)], sems
+    )
     acc[...] = jnp.zeros_like(acc)
     for z in range(far):
         for x in range(near):
@@ -214,6 +238,8 @@
                 axis=0,
             )
             turned[z * near + x] = rows.T
+    for copy in copies[:3]:
+        copy.wait()
     core = core_ref[0]
     count = count_ref[0]
     step = 8
@@ -228,6 +254,7 @@
     lax.fori_loop(0, slots // step, some_slots, 0)
     for s in range(acc.shape[0]):
         out_ref[:, s * block : (s + 1) * block] = acc[s].astype(BF16)
+    copies[3].wait()
 
 
 def weight_kernel(spread_ref, feats_ref, out_ref):
@@ -281,6 +308,8 @@
         return lax.ppermute(x, "core", [(0, 1), (1, 0)])
 
     halves = 2
+    feats_far = pltpu.with_memory_space_constraint(feats, pltpu.HBM)
+    w_far = pltpu.with_memory_space_constraint(w_first, pltpu.HBM)
     rows_half = nodes // halves
     projected = [
         pl.pallas_call(
@@ -295,7 +324,7 @@
             ],
             compiler_params=params(),
             name=f"project{i}",
-        )(feats, w_first)
+        )(feats_far, w_far)
         for i in range(halves)
     ]
     swapped = [swap(p) for p in projected]
@@ -310,25 +339,32 @@
     partial = pl.pallas_call(
         lambda *refs: partial_kernel(*refs, near=near, far=far),
         out_shape=jax.ShapeDtypeStruct((pairs * near, far * piece, hidden), BF16),
-        in_specs=[sspec()] * 4 + [vspec()] * (1 + 2 * halves),
-        out_specs=vspec(),
-        scratch_shapes=[VMEM((nodes, 2 * hidden), BF16), VMEM((pairs, local, hidden), F32)],
+        in_specs=[sspec()] + [aspec()] * 4 + [vspec()] * (1 + 2 * halves),
+        out_specs=vspec(),
+        scratch_shapes=[
+            VMEM((nodes, 2 * hidden), BF16),
+            VMEM((pairs, local, hidden), F32),
+            SMEM((slots,), jnp.int32),
+            SMEM((slots,), jnp.int32),
+            SMEM((1,), jnp.int32),
+            pltpu.SemaphoreType.DMA((3,)),
+        ],
         compiler_params=params(),
         name="partial",
-    )(core, blk_dst, blk_src, blk_count, adjacency, *projected, *swapped)
+    )(core, blk_dst, blk_src, blk_count, counts, adjacency, *projected, *swapped)
     by_plane = jnp.sum(over_plane(partial).astype(F32), axis=0)
     by_far = over_far(by_plane.reshape(far, piece, hidden))
     spread = jax.ShapeDtypeStruct((domains, piece, hidden), BF16)
     small = jax.ShapeDtypeStruct((piece, hidden), F32)
-    exact, own_states = pl.pallas_call(
+    exact, own_states, tiled_states = pl.pallas_call(
         state_kernel,
-        out_shape=(small, spread),
+        out_shape=(small, jax.ShapeDtypeStruct((piece, hidden), BF16), spread),
         in_specs=[vspec()],
-        out_specs=(vspec(), vspec()),
+        out_specs=(vspec(), vspec(), vspec()),
         compiler_params=params(),
         name="state",
     )(by_far)
-    states = over_dom(own_states)
+    states = over_dom(tiled_states)
     sent = pl.pallas_call(
         message_kernel,
         out_shape=jax.ShapeDtypeStruct((cuts, rows + piece, hidden), BF16),
@@ -338,7 +374,7 @@
         name="message",
     )(counts, states, own_states, w_edge)
     recv = lax.all_to_all(sent, ("y", "core"), 0, 0, tiled=True)
-    new_state, direct, back = pl.pallas_call(
+    new_rows, direct, back = pl.pallas_call(
         gate_kernel,
         out_shape=(jax.ShapeDtypeStruct((rows, hidden), BF16), small, spread),
         in_specs=[sspec()] + [vspec()] * 7,
@@ -358,18 +394,25 @@
     )(grad_part, direct, exact)
     far_grads = over_far(own_grad).reshape(1, far * piece, hidden)
     grads = over_plane(jnp.broadcast_to(far_grads, (pairs * near, far * piece, hidden)))
-    mine = pl.pallas_call(
+    mine, new_state = pl.pallas_call(
         lambda *refs: spread_kernel(*refs, near=near, far=far),
-        out_shape=jax.ShapeDtypeStruct((hidden, nodes), BF16),
-        in_specs=[sspec()] * 4 + [vspec()] * 2,
-        out_specs=vspec(),
+        out_shape=(
+            jax.ShapeDtypeStruct((hidden, nodes), BF16),
+            jax.ShapeDtypeStruct((rows, hidden), BF16),
+        ),
+        in_specs=[sspec()] + [aspec()] * 4 + [vspec()] * 2,
+        out_specs=(vspec(), aspec()),
         scratch_shapes=[
             VMEM((domains, hidden, pairs * piece), BF16),
             VMEM((nodes // block, hidden, block), F32),
+            SMEM((slots,), jnp.int32),
+            SMEM((slots,), jnp.int32),
+            SMEM((1,), jnp.int32),
+            pltpu.SemaphoreType.DMA((4,)),
         ],
         compiler_params=params(),
         name="spread",
-    )(core, blk_dst, blk_src, blk_count, grads, adjacency)
+    )(core, blk_dst, blk_src, blk_count, new_rows, grads, adjacency)
     other = swap(mine)
     own_part = pl.pallas_call(
         weight_kernel,

time: 134 us -> 130 us (0.970)
  blocking collectives: 91.5 us -> 104 us
  waiting for transfers between devices: 10.6 us -> 1.09 us
  starting transfers between devices: 11.8 us -> 8.02 us
  local copies, waits for them, and re-layouts: 2.85 us -> 0.36 us
    all_to_all x2 -> x3, blocking collectives: 25.1 us -> 37.7 us  [over_dom(): return lax.all_to_all(x, ('z', 'x'), 0, 0, tiled=True)]
    all_to_all x1 -> x0, waiting for transfers between devices: 8.14 us -> none  [over_dom(): return lax.all_to_all(x, ('z', 'x'), 0, 0, tiled=True)]
    all_to_all x1 -> x0, starting transfers between devices: 3.85 us -> none  [over_dom(): return lax.all_to_all(x, ('z', 'x'), 0, 0, tiled=True)]
    unnamed x28 -> x24, local copies, waits for them, and re-layouts: 2.75 us -> 0.27 us
    pallas_call x2, Pallas kernels: 2.26 us -> 3.86 us  [body(): pl.pallas_call(lambda *refs, i=i: project_kernel(*refs, start=i * rows_ha...]
  transfers between devices with their start and end apart: 4 -> 3, of which waited for: 3 -> 1; matrix products, arithmetic and copies ran while one was open for 0% -> 0% of each run, Pallas kernels for 2% -> 3%
where the time goes in v3:
time: 130 us
  blocking collectives  104 us (80%)
  Pallas kernels  14.3 us (11%)
  starting transfers between devices  8.02 us (6%)
  between operations  1.52 us (1%)
    all_to_all x3, blocking collectives, over_dom(): return lax.all_to_all(x, ('z', 'x'), 0, 0, tiled=True)  37.7 us
    all_to_all x2, blocking collectives, over_plane(): return lax.all_to_all(x, ('y', 'x'), 0, 0, tiled=True)  27.8 us
    all_to_all x2, blocking collectives, over_far(): return lax.all_to_all(x, 'z', 0, 0, tiled=True)  24.6 us
    all_to_all x1, blocking collectives, body(): recv = lax.all_to_all(sent, ('y', 'core'), 0, 0, tiled=True)  13.8 us
    ppermute x3, starting transfers between devices, swap(): return lax.ppermute(x, 'core', [(0, 1), (1, 0)])  8.02 us
    pallas_call x2, Pallas kernels, body(): pl.pallas_call(lambda *refs, i=i: project_kernel(*refs, start=i * rows_ha...  3.86 us
    pallas_call x1, Pallas kernels, body(): pl.pallas_call(lambda *refs: partial_kernel(*refs, near=near, far=far), o...  3.7 us
    pallas_call x1, Pallas kernels, body(): pl.pallas_call(lambda *refs: spread_kernel(*refs, near=near, far=far), ou...  2.72 us
  transfers between devices with their start and end apart: 3, of which 1 were waited for; matrix products, arithmetic and copies ran while one was open for 0% of the time, Pallas kernels for 3%

profile of v3, /device:TPU:1, one launch (start us, length us, event | category | flops | bytes accessed | tf_op | source)
XLA Modules:
  0.0 129.9 jit_solution(4498146679322194360)
XLA Ops:
  0.6 1.9 %project0.1.refs_6_ = f32[1024,128]{1,0:T(8,128)S(1)} custom-call(bf16[2048,512]{1,0:T(8,128)(2,1)} %feats_ref.3, bf16[512,128]{1,0:T(8,128)(2,1)} %refs_1_.6), custom_call_target="tpu_custom_call" | custom-call | tf_op jit(solution)/shard_map/project0/pallas_call | solution.py:315
  2.6 3.3 %collective-permute-start = (f32[1024,128]{1,0:T(8,128)S(1)}, f32[1024,128]{1,0:T(8,128)}, u32[]{:S(2)}, u32[]{:S(2)}) collective-permute-start(f32[1024,128]{1,0:T(8,128)S(1)} %project0.1.refs_6_), channel_id=1, source_target_pairs={{0,32},{32,0},{1,33},{33,1},{2,34},{34,2},{3,35},{35,3},{4,36},{36... | collective-permute-start | bytes 1572872 | tf_op jit(solution)/shard_map/ppermute | solution.py:308
  5.9 1.9 %project1.1.refs_7_ = f32[1024,128]{1,0:T(8,128)S(1)} custom-call(bf16[2048,512]{1,0:T(8,128)(2,1)} %feats_ref.3, bf16[512,128]{1,0:T(8,128)(2,1)} %refs_1_.6), custom_call_target="tpu_custom_call" | custom-call | tf_op jit(solution)/shard_map/project1/pallas_call | solution.py:315
  7.9 0.2 collective-permute-start.1
  8.7 0.1 copy.15.refs_1_
  8.8 0.1 copy.16.refs_2_
  8.9 1.0 counts.1.refs_4_.count_ref
  10.0 3.7 %partial.1 = bf16[16,128,128]{2,1,0:T(8,128)(2,1)S(1)} custom-call(s32[1]{0:T(128)} %bitcast.refs_0_, s32[64]{0:T(128)S(1)} %copy-done.7, s32[64]{0:T(128)S(1)} %copy-done.8, s32[1]{0:T(128)S(6)} %copy.17.refs_3_, bf16[128,2048]{1,0:T(8,128)(2,1)S(1)} %counts.1.refs_4_.count_ref, bf16[64,128,128]{2,1,0:T(8,128)(2,1)S(1)} %copy-done.1, ...), custom_call_target="tpu_custom_call" | custom-call | tf_op jit(solution)/shard_map/partial/pallas_call | solution.py:339
  13.8 15.7 %all_to_all.40 = bf16[16,128,128]{2,1,0:T(8,128)(2,1)S(1)} all-to-all(bf16[16,128,128]{2,1,0:T(8,128)(2,1)S(1)} %partial.1), channel_id=1, replica_groups=mesh['y'=4,'core'=2,'z'=8,'x'=4] {'y','x'}, dimensions={0} | all-to-all | bytes 1048576 | tf_op jit(solution)/shard_map/all_to_all | solution.py:302
  29.5 15.3 %all_to_all.41.part_ref = f32[8,16,128]{2,1,0:T(8,128)S(1)} all-to-all(f32[8,16,128]{2,1,0:T(8,128)S(1)} %bitcast.4), channel_id=1, replica_groups=mesh['y'=4,'core'=2,'z'=8,'x'=4] {'z'}, dimensions={0} | all-to-all | bytes 131072 | tf_op jit(solution)/shard_map/all_to_all | solution.py:305
  44.9 12.6 %all_to_all.42.states_ref = bf16[32,16,128]{2,1,0:T(8,128)(2,1)S(1)} all-to-all(bf16[32,16,128]{2,1,0:T(8,128)(2,1)S(1)} %get-tuple-element.10), channel_id=1, replica_groups=mesh['y'=4,'core'=2,'z'=8,'x'=4] {'z','x'}, dimensions={0} | all-to-all | bytes 262144 | tf_op jit(solution)/shard_map/all_to_all | solution.py:299
  57.5 0.5 message.1
  58.0 13.8 %all_to_all.43.recv_ref = bf16[8,144,128]{2,1,0:T(8,128)(2,1)S(1)} all-to-all(bf16[8,144,128]{2,1,0:T(8,128)(2,1)S(1)} %message.1), channel_id=1, replica_groups=mesh['y'=4,'core'=2,'z'=8,'x'=4] {'y','core'}, dimensions={0} | all-to-all | bytes 589824 | tf_op jit(solution)/shard_map/all_to_all | solution.py:376
  71.8 1.4 %gates.1 = (bf16[128,128]{1,0:T(8,128)(2,1)S(1)}, f32[16,128]{1,0:T(8,128)S(1)}, bf16[32,16,128]{2,1,0:T(8,128)(2,1)S(1)}) custom-call(s32[1]{0:T(128)} %bitcast.1.refs_0_.cut_ref, bf16[8,144,128]{2,1,0:T(8,128)(2,1)S(1)} %all_to_all.43.recv_ref, bf16[128,2048]{1,0:T(8,128)(2,1)S(1)} %counts.1.refs_4_.count_ref, bf16[128,128]{1,0:T(8,128)(2,1)S(1)} %copy-done.5, ...), custom_call_target="tpu_custom_call" | custom-call | tf_op jit(solution)/shard_map/gates/pallas_call | solution.py:377
  73.3 12.4 %all_to_all.44.part_ref = bf16[32,16,128]{2,1,0:T(8,128)(2,1)S(1)} all-to-all(bf16[32,16,128]{2,1,0:T(8,128)(2,1)S(1)} %get-tuple-element.13), channel_id=1, replica_groups=mesh['y'=4,'core'=2,'z'=8,'x'=4] {'z','x'}, dimensions={0} | all-to-all | bytes 262144 | tf_op jit(solution)/shard_map/all_to_all | solution.py:299
  85.7 9.3 %all_to_all.45 = bf16[8,16,128]{2,1,0:T(8,128)(2,1)S(1)} all-to-all(bf16[8,16,128]{2,1,0:T(8,128)(2,1)S(1)} %first_grad.1), channel_id=1, replica_groups=mesh['y'=4,'core'=2,'z'=8,'x'=4] {'z'}, dimensions={0} | all-to-all | bytes 65536 | tf_op jit(solution)/shard_map/all_to_all | solution.py:305
  95.1 12.1 %all_to_all.46.refs_5_ = bf16[16,128,128]{2,1,0:T(8,128)(2,1)S(1)} all-to-all(bf16[16,128,128]{2,1,0:T(8,128)(2,1)S(1)} %broadcast_in_dim.8), channel_id=1, replica_groups=mesh['y'=4,'core'=2,'z'=8,'x'=4] {'y','x'}, dimensions={0} | all-to-all | bytes 1048576 | tf_op jit(solution)/shard_map/all_to_all | solution.py:302
  107.2 2.7 %spread.1 = (bf16[128,2048]{1,0:T(8,128)(2,1)S(1)}, bf16[128,128]{1,0:T(8,128)(2,1)}) custom-call(s32[1]{0:T(128)} %bitcast.refs_0_, s32[64]{0:T(128)S(1)} %copy-done.7, s32[64]{0:T(128)S(1)} %copy-done.8, s32[1]{0:T(128)S(6)} %copy.17.refs_3_, bf16[128,128]{1,0:T(8,128)(2,1)S(1)} %get-tuple-element.12.refs_4_, ...), custom_call_target="tpu_custom_call" | custom-call | tf_op jit(solution)/shard_map/spread/pallas_call | solution.py:397
  109.9 4.5 %collective-permute-start.2 = (bf16[128,2048]{1,0:T(8,128)(2,1)S(1)}, bf16[128,2048]{1,0:T(8,128)(2,1)S(1)}, u32[]{:S(2)}, u32[]{:S(2)}) collective-permute-start(bf16[128,2048]{1,0:T(8,128)(2,1)S(1)} %get-tuple-element.17.spread_ref), channel_id=1, source_target_pairs={{0,32},{32,0},{1,33},{33,1},{2,34},{34,2},{3,35},{35,3},{4,36},{36... | collective-permute-start | bytes 1572872 | tf_op jit(solution)/shard_map/ppermute | solution.py:308
  114.4 0.4 weight_own.1.part_ref
  114.9 1.1 collective-permute-done.2.spread_ref
  115.9 0.5 weight_all.1
  116.5 12.7 %all_to_all.47 = bf16[32,16,128]{2,1,0:T(8,128)(2,1)S(1)} all-to-all(bf16[32,16,128]{2,1,0:T(8,128)(2,1)S(1)} %weight_all.1), channel_id=1, replica_groups=mesh['y'=4,'core'=2,'z'=8,'x'=4] {'z','x'}, dimensions={0} | all-to-all | bytes 262144 | tf_op jit(solution)/shard_map/all_to_all | solution.py:299
  129.2 0.6 convert_reduce_fusion.1
  (28 shorter events, 0.3 us)
Async XLA Ops:
  0.6 8.1 %copy-start.9 = (s32[128,8]{0,1:T(8,128)S(1)}, s32[128,8]{0,1:T(8,128)}, u32[]{:S(2)}) copy-start(s32[128,8]{0,1:T(8,128)} %param.18) | copy-start | bytes 12292
  2.6 6.3 %copy-start.10 = (s32[128,8]{0,1:T(8,128)S(1)}, s32[128,8]{0,1:T(8,128)}, u32[]{:S(2)}) copy-start(s32[128,8]{0,1:T(8,128)} %param.19) | copy-start | bytes 12292
  2.6 7.4 %copy-start.1 = (bf16[64,128,128]{2,1,0:T(8,128)(2,1)S(1)}, bf16[64,128,128]{2,1,0:T(8,128)(2,1)}, u32[]{:S(2)}) copy-start(bf16[64,128,128]{2,1,0:T(8,128)(2,1)} %refs_6_.1) | copy-start | bytes 6291460
  2.6 7.4 %copy-start.7 = (s32[64]{0:T(128)S(1)}, s32[64]{0:T(128)}, u32[]{:S(2)}) copy-start(s32[64]{0:T(128)} %refs_1_.8) | copy-start | bytes 772
  2.6 7.4 %copy-start.8 = (s32[64]{0:T(128)S(1)}, s32[64]{0:T(128)}, u32[]{:S(2)}) copy-start(s32[64]{0:T(128)} %refs_2_.4) | copy-start | bytes 772
  2.6 7.4 %collective-permute-start = (f32[1024,128]{1,0:T(8,128)S(1)}, f32[1024,128]{1,0:T(8,128)}, u32[]{:S(2)}, u32[]{:S(2)}) collective-permute-start(f32[1024,128]{1,0:T(8,128)S(1)} %project0.1.refs_6_), channel_id=1, source_target_pairs={{0,32},{32,0},{1,33},{33,1},{2,34},{34,2},{3,35},{35,3},{4,36},{36... | collective-permute-start | bytes 1572872 | tf_op jit(solution)/shard_map/ppermute | solution.py:308
  7.9 2.1 %collective-permute-start.1 = (f32[1024,128]{1,0:T(8,128)S(1)}, f32[1024,128]{1,0:T(8,128)}, u32[]{:S(2)}, u32[]{:S(2)}) collective-permute-start(f32[1024,128]{1,0:T(8,128)S(1)} %project1.1.refs_7_), channel_id=1, source_target_pairs={{0,32},{32,0},{1,33},{33,1},{2,34},{34,2},{3,35},{35,3},{4,36},{36... | collective-permute-start | bytes 1572872 | tf_op jit(solution)/shard_map/ppermute | solution.py:308
  13.7 43.8 %copy-start.2 = (bf16[128,512]{1,0:T(8,128)(2,1)S(1)}, bf16[128,512]{1,0:T(8,128)(2,1)}, u32[]{:S(2)}) copy-start(bf16[128,512]{1,0:T(8,128)(2,1)} %w_edge_ref.1) | copy-start | bytes 393220
  13.8 58.0 %copy-start.3 = (bf16[128,384]{1,0:T(8,128)(2,1)S(1)}, bf16[128,384]{1,0:T(8,128)(2,1)}, u32[]{:S(2)}) copy-start(bf16[128,384]{1,0:T(8,128)(2,1)} %w_in_ref.1) | copy-start | bytes 294916
  13.8 58.0 %copy-start.4 = (bf16[128,256]{1,0:T(8,128)(2,1)S(1)}, bf16[128,256]{1,0:T(8,128)(2,1)}, u32[]{:S(2)}) copy-start(bf16[128,256]{1,0:T(8,128)(2,1)} %w_state_ref.1) | copy-start | bytes 196612
  13.8 58.0 %copy-start.5 = (bf16[128,128]{1,0:T(8,128)(2,1)S(1)}, bf16[128,128]{1,0:T(8,128)(2,1)}, u32[]{:S(2)}) copy-start(bf16[128,128]{1,0:T(8,128)(2,1)} %grad_ref.1) | copy-start | bytes 98308
  13.8 58.0 %copy-start.6 = (bf16[128,128]{1,0:T(8,128)(2,1)S(1)}, bf16[128,128]{1,0:T(8,128)(2,1)}, u32[]{:S(2)}) copy-start(bf16[128,128]{1,0:T(8,128)(2,1)} %w_cand_ref.1) | copy-start | bytes 98308
  94.9 19.5 %copy-start = (bf16[2048,512]{1,0:T(8,128)(2,1)S(1)}, bf16[2048,512]{1,0:T(8,128)(2,1)}, u32[]{:S(2)}) copy-start(bf16[2048,512]{1,0:T(8,128)(2,1)} %feats_ref.3) | copy-start | bytes 6291460
  109.9 6.0 %collective-permute-start.2 = (bf16[128,2048]{1,0:T(8,128)(2,1)S(1)}, bf16[128,2048]{1,0:T(8,128)(2,1)S(1)}, u32[]{:S(2)}, u32[]{:S(2)}) collective-permute-start(bf16[128,2048]{1,0:T(8,128)(2,1)S(1)} %get-tuple-element.17.spread_ref), channel_id=1, source_target_pairs={{0,32},{32,0},{1,33},{33,1},{2,34},{34,2},{3,35},{35,3},{4,36},{36... | collective-permute-start | bytes 1572872 | tf_op jit(solution)/shard_map/ppermute | solution.py:308

commit v4 on v3

--- a/solution.py
+++ b/solution.py
@@ -41,31 +41,44 @@
     return pltpu.CompilerParams(vmem_limit_bytes=12 * 1024 * 1024)
 
 
+def cut_index():
+    return 2 * lax.axis_index("y") + lax.axis_index("core")
+
+
 def dot(a, b):
     return jnp.dot(a, b, preferred_element_type=F32)
 
 
-def project_kernel(feats_hbm, w_hbm, out_ref, feats, w, sems, *, start):
-    rows = feats.shape[0]
+def project_kernel(feats_hbm, w_hbm, out_ref, rest_ref, w_ref, feats, sems):
+    rows, rest = feats.shape[0], rest_ref.shape[0]
     parts = 4
-    chunk = rows // parts
-    w_copy = pltpu.make_async_copy(w_hbm, w, sems.at[parts])
-    w_copy.start()
-    copies = [
-        pltpu.make_async_copy(
-            feats_hbm.at[pl.ds(start + i * chunk, chunk)],
-            feats.at[pl.ds(i * chunk, chunk)],
-            sems.at[i],
-        )
-        for i in range(parts)
-    ]
-    for copy in copies:
-        copy.start()
-    w_copy.wait()
+    chunk, rest_chunk = rows // parts, rest // parts
+    copies = start_all(
+        [(w_hbm, w_ref)]
+        + [
+            (feats_hbm.at[pl.ds(i * chunk, chunk)], feats.at[pl.ds(i * chunk, chunk)])
+            for i in range(parts)
+        ]
+        + [
+            (
+                feats_hbm.at[pl.ds(rows + i * rest_chunk, rest_chunk)],
+                rest_ref.at[pl.ds(i * rest_chunk, rest_chunk)],
+            )
+            for i in range(parts)
+        ],
+        sems,
+    )
+    copies[0].wait()
     for i in range(parts):
-        copies[i].wait()
+        copies[1 + i].wait()
         at = pl.ds(i * chunk, chunk)
-        out_ref[at, :] = dot(feats[at, :], w[...])
+        out_ref[at, :] = dot(feats[at, :], w_ref[...])
+    for copy in copies[1 + parts :]:
+        copy.wait()
+
+
+def project_rest_kernel(rest_ref, w_ref, out_ref):
+    out_ref[...] = dot(rest_ref[...], w_ref[...])
 
 
 def own_rows(adj, slot, core, piece):
@@ -80,7 +93,7 @@
 
 
 def partial_kernel(
-    core_ref, dst_any, src_any, count_any, counts_any, adj, *refs, near, far,
+    dst_any, src_any, count_any, counts_any, adj, *refs, near, far,
 ):
     parts = refs[:-7]
     out_ref, projected, acc, dst_ref, src_ref, count_ref, sems = refs[-7:]
@@ -92,17 +105,18 @@
     piece = acc.shape[1] // (near * far)
     hidden = acc.shape[2]
     half = len(parts) // 2
-    rows = parts[0].shape[0]
     acc[...] = jnp.zeros_like(acc)
+    start = 0
     for i in range(half):
         both = parts[i][...] + parts[half + i][...]
         high = both.astype(BF16)
-        at = pl.ds(i * rows, rows)
+        at = pl.ds(start, both.shape[0])
+        start += both.shape[0]
         projected[at, :hidden] = high
         projected[at, hidden:] = (both - high.astype(F32)).astype(BF16)
     for copy in copies:
         copy.wait()
-    core = core_ref[0]
+    core = lax.axis_index("core")
     count = count_ref[0]
     step = 8
 
@@ -124,15 +138,16 @@
     out_ref[...] = acc[...].astype(BF16).reshape(out_ref.shape)
 
 
-def count_kernel(cut_ref, nbr_ref, type_ref, count_ref, *, cuts, block):
-    rows, fanout = nbr_ref.shape
+def count_kernel(nbr_ref, type_ref, count_ref, *, cuts, block):
+    fanout, rows = nbr_ref.shape
     cells = count_ref.shape[1]
     piece = block // cuts
     nbr = nbr_ref[...]
     within = nbr % block
     local = (nbr // block) * piece + within % piece
     per_type = cells // 4
-    key = jnp.where(within // piece == cut_ref[0], type_ref[...] * per_type + local, -1)
+    key = jnp.where(within // piece == cut_index(), type_ref[...] * per_type + local, -1)
+    key = jnp.concatenate([key, jnp.zeros((rows - fanout, rows), jnp.int32)], axis=0).T
     tile = 512
     for start in range(0, cells, tile):
         place = lax.broadcasted_iota(jnp.int32, (rows, tile), 1) + start
@@ -169,7 +184,7 @@
 
 
 def gate_kernel(
-    cut_ref, recv_ref, count_ref, grad_ref, w_edge_ref, w_in_ref, w_state_ref, w_cand_ref,
+    recv_ref, count_ref, grad_ref, w_edge_ref, w_in_ref, w_state_ref, w_cand_ref,
     new_ref, direct_ref, back_ref, own,
 ):
     rows, hidden = grad_ref.shape
@@ -203,7 +218,7 @@
         + reset_in * reset
         + lax.dot_general(gates[:, : 2 * hidden], w_state, contract, preferred_element_type=F32)
     )
-    direct_ref[...] = own[pl.ds(pl.multiple_of(cut_ref[0] * piece, piece), piece), :]
+    direct_ref[...] = own[pl.ds(pl.multiple_of(cut_index() * piece, piece), piece), :]
     total = jnp.zeros((hidden, local), F32)
     for e in range(count_ref.shape[1] // local):
         spread = dot(message_grad_t, count_ref[:, e * local : (e + 1) * local]).astype(BF16)
@@ -220,7 +235,7 @@
 
 
 def spread_kernel(
-    core_ref, dst_any, src_any, count_any, new_any, grads_ref, adj, out_ref, new_out,
+    dst_any, src_any, count_any, new_any, grads_ref, adj, out_ref, new_out,
     turned, acc, dst_ref, src_ref, count_ref, sems, *, near, far,
 ):
     slots, block, _ = adj.shape
@@ -240,7 +255,7 @@
             turned[z * near + x] = rows.T
     for copy in copies[:3]:
         copy.wait()
-    core = core_ref[0]
+    core = lax.axis_index("core")
     count = count_ref[0]
     step = 8
 
@@ -292,8 +307,6 @@
     cuts = 2 * pairs
     piece = block // cuts
     local = domains * piece
-    core = lax.axis_index("core").reshape(1)
-    cut = (2 * lax.axis_index("y") + lax.axis_index("core")).reshape(1)
 
     def over_dom(x):
         return lax.all_to_all(x, ("z", "x"), 0, 0, tiled=True)
@@ -307,39 +320,46 @@
     def swap(x):
         return lax.ppermute(x, "core", [(0, 1), (1, 0)])
 
-    halves = 2
-    feats_far = pltpu.with_memory_space_constraint(feats, pltpu.HBM)
-    w_far = pltpu.with_memory_space_constraint(w_first, pltpu.HBM)
-    rows_half = nodes // halves
-    projected = [
-        pl.pallas_call(
-            lambda *refs, i=i: project_kernel(*refs, start=i * rows_half),
-            out_shape=jax.ShapeDtypeStruct((rows_half, hidden), F32),
-            in_specs=[hspec(), hspec()],
-            out_specs=vspec(),
-            scratch_shapes=[
-                VMEM((rows_half, feat_cols), BF16),
-                VMEM((feat_cols, hidden), BF16),
-                pltpu.SemaphoreType.DMA((5,)),
-            ],
-            compiler_params=params(),
-            name=f"project{i}",
-        )(feats_far, w_far)
-        for i in range(halves)
-    ]
-    swapped = [swap(p) for p in projected]
+    first_rows = nodes // 2
+    rest_rows = nodes - first_rows
+    projected, rest, w = pl.pallas_call(
+        project_kernel,
+        out_shape=(
+            jax.ShapeDtypeStruct((first_rows, hidden), F32),
+            jax.ShapeDtypeStruct((rest_rows, feat_cols), BF16),
+            jax.ShapeDtypeStruct((feat_cols, hidden), BF16),
+        ),
+        in_specs=[hspec(), hspec()],
+        out_specs=(vspec(), vspec(), vspec()),
+        scratch_shapes=[VMEM((first_rows, feat_cols), BF16), pltpu.SemaphoreType.DMA((9,))],
+        compiler_params=params(),
+        name="project",
+    )(
+        pltpu.with_memory_space_constraint(feats, pltpu.HBM),
+        pltpu.with_memory_space_constraint(w_first, pltpu.HBM),
+    )
+    projected_rest = pl.pallas_call(
+        project_rest_kernel,
+        out_shape=jax.ShapeDtypeStruct((rest_rows, hidden), F32),
+        in_specs=[vspec(), vspec()],
+        out_specs=vspec(),
+        compiler_params=params(),
+        name="project_rest",
+    )(rest, w)
+    mine_parts = [projected, projected_rest]
+    swapped = [swap(p) for p in mine_parts]
     counts = pl.pallas_call(
         lambda *refs: count_kernel(*refs, cuts=cuts, block=block),
         out_shape=jax.ShapeDtypeStruct((rows, 4 * local), BF16),
-        in_specs=[sspec(), vspec(), vspec()],
+        in_specs=[vspec(), vspec()],
         out_specs=vspec(),
         compiler_params=params(),
         name="counts",
-    )(cut, nbr_ids, edge_types)
+    )(nbr_ids.T, edge_types.T)
     partial = pl.pallas_call(
         lambda *refs: partial_kernel(*refs, near=near, far=far),
         out_shape=jax.ShapeDtypeStruct((pairs * near, far * piece, hidden), BF16),
-        in_specs=[sspec()] + [aspec()] * 4 + [vspec()] * (1 + 2 * halves),
+        in_specs=[aspec()] * 4 + [vspec()] * (1 + 2 * len(mine_parts)),
         out_specs=vspec(),
         scratch_shapes=[
             VMEM((nodes, 2 * hidden), BF16),
@@ -351,7 +371,7 @@
         ],
         compiler_params=params(),
         name="partial",
-    )(core, blk_dst, blk_src, blk_count, counts, adjacency, *projected, *swapped)
+    )(blk_dst, blk_src, blk_count, counts, adjacency, *mine_parts, *swapped)
     by_plane = jnp.sum(over_plane(partial).astype(F32), axis=0)
     by_far = over_far(by_plane.reshape(far, piece, hidden))
     spread = jax.ShapeDtypeStruct((domains, piece, hidden), BF16)
@@ -377,12 +397,12 @@
     new_rows, direct, back = pl.pallas_call(
         gate_kernel,
         out_shape=(jax.ShapeDtypeStruct((rows, hidden), BF16), small, spread),
-        in_specs=[sspec()] + [vspec()] * 7,
+        in_specs=[vspec()] * 7,
         out_specs=(vspec(), vspec(), vspec()),
         scratch_shapes=[VMEM((rows, hidden), F32)],
         compiler_params=params(),
         name="gates",
-    )(cut, recv, counts, out_grad, w_edge, w_gate_in, w_gate_state, w_cand)
+    )(recv, counts, out_grad, w_edge, w_gate_in, w_gate_state, w_cand)
     grad_part = over_dom(back)
     own_grad = pl.pallas_call(
         grad_kernel,
@@ -400,7 +420,7 @@
             jax.ShapeDtypeStruct((hidden, nodes), BF16),
             jax.ShapeDtypeStruct((rows, hidden), BF16),
         ),
-        in_specs=[sspec()] + [aspec()] * 4 + [vspec()] * 2,
+        in_specs=[aspec()] * 4 + [vspec()] * 2,
         out_specs=(vspec(), aspec()),
         scratch_shapes=[
             VMEM((domains, hidden, pairs * piece), BF16),
@@ -412,7 +432,7 @@
         ],
         compiler_params=params(),
         name="spread",
-    )(core, blk_dst, blk_src, blk_count, new_rows, grads, adjacency)
+    )(blk_dst, blk_src, blk_count, new_rows, grads, adjacency)
     other = swap(mine)
     own_part = pl.pallas_call(
         weight_kernel,

time: 130 us -> 128 us (0.985)
  Pallas kernels: 14.3 us -> 11.8 us
    pallas_call x2, Pallas kernels: 3.86 us -> 2.52 us  [the longest x1 2.09 us: body(): pl.pallas_call(project_kernel, out_shape=(jax.ShapeDtypeStruct((first_row...]
  transfers between devices with their start and end apart: 3 -> 3, of which waited for: 1 -> 2; matrix products, arithmetic and copies ran while one was open for 0% -> 0% of each run, Pallas kernels for 3% -> 1%
where the time goes in v4:
time: 128 us; the launch traced here: 127 us
  blocking collectives  104 us (81%)
  Pallas kernels  11.8 us (9%)
  starting transfers between devices  7.88 us (6%)
  waiting for transfers between devices  1.52 us (1%)
  between operations  1.49 us (1%)
    all_to_all x3, blocking collectives, over_dom(): return lax.all_to_all(x, ('z', 'x'), 0, 0, tiled=True)  37.6 us
    all_to_all x2, blocking collectives, over_plane(): return lax.all_to_all(x, ('y', 'x'), 0, 0, tiled=True)  28 us
    all_to_all x2, blocking collectives, over_far(): return lax.all_to_all(x, 'z', 0, 0, tiled=True)  24.4 us
    all_to_all x1, blocking collectives, body(): recv = lax.all_to_all(sent, ('y', 'core'), 0, 0, tiled=True)  13.8 us
    ppermute x3, starting transfers between devices, swap(): return lax.ppermute(x, 'core', [(0, 1), (1, 0)])  7.88 us
    pallas_call x1, Pallas kernels, body(): pl.pallas_call(lambda *refs: spread_kernel(*refs, near=near, far=far), ou...  2.74 us
  transfers between devices with their start and end apart: 3, of which 2 were waited for; matrix products, arithmetic and copies ran while one was open for 0% of the time, Pallas kernels for 1%

profile of v4, /device:TPU:1, one launch (start us, length us, event | category | flops | bytes accessed | tf_op | source)
XLA Modules:
  0.0 127.4 jit_solution(15878263103123142003)
XLA Ops:
  0.7 2.1 %project.1 = (f32[1024,128]{1,0:T(8,128)S(1)}, bf16[1024,512]{1,0:T(8,128)(2,1)S(1)}, bf16[512,128]{1,0:T(8,128)(2,1)S(1)}) custom-call(bf16[2048,512]{1,0:T(8,128)(2,1)} %feats_ref.3, bf16[512,128]{1,0:T(8,128)(2,1)} %w_hbm.1), custom_call_target="tpu_custom_call" | custom-call | tf_op jit(solution)/shard_map/project/pallas_call | solution.py:325
  2.8 0.4 project_rest.1.refs_6_
  3.2 3.3 %collective-permute-start.1 = (f32[1024,128]{1,0:T(8,128)S(1)}, f32[1024,128]{1,0:T(8,128)S(1)}, u32[]{:S(2)}, u32[]{:S(2)}) collective-permute-start(f32[1024,128]{1,0:T(8,128)S(1)} %project_rest.1.refs_6_), channel_id=1, source_target_pairs={{0,32},{32,0},{1,33},{33,1},{2,34},{34,2},{3,35},{35,3},{4,36},{36... | collective-permute-start | bytes 1572872 | tf_op jit(solution)/shard_map/ppermute | solution.py:321
  6.5 0.1 collective-permute-start
  7.3 1.1 counts.1.refs_3_.count_ref
  8.4 0.4 collective-permute-done.refs_7_
  8.8 2.5 %partial.1 = bf16[16,128,128]{2,1,0:T(8,128)(2,1)S(1)} custom-call(s32[64]{0:T(128)S(1)} %copy-done.9, s32[64]{0:T(128)S(1)} %copy-done.10, s32[1]{0:T(128)S(6)} %copy.15.refs_2_, bf16[128,2048]{1,0:T(8,128)(2,1)S(1)} %counts.1.refs_3_.count_ref, bf16[64,128,128]{2,1,0:T(8,128)(2,1)S(1)} %copy-done.1, f32[1024,128]{1,0:T(8,128)S(1)} %get-tuple-element.13.refs_5_, ...), custom_call_target="tpu_custom_call" | custom-call | tf_op jit(solution)/shard_map/partial/pallas_call | solution.py:359
  11.4 15.7 %all_to_all.40 = bf16[16,128,128]{2,1,0:T(8,128)(2,1)S(1)} all-to-all(bf16[16,128,128]{2,1,0:T(8,128)(2,1)S(1)} %partial.1), channel_id=1, replica_groups=mesh['y'=4,'core'=2,'z'=8,'x'=4] {'y','x'}, dimensions={0} | all-to-all | bytes 1048576 | tf_op jit(solution)/shard_map/all_to_all | solution.py:315
  27.2 15.2 %all_to_all.41.part_ref = f32[8,16,128]{2,1,0:T(8,128)S(1)} all-to-all(f32[8,16,128]{2,1,0:T(8,128)S(1)} %bitcast.6), channel_id=1, replica_groups=mesh['y'=4,'core'=2,'z'=8,'x'=4] {'z'}, dimensions={0} | all-to-all | bytes 131072 | tf_op jit(solution)/shard_map/all_to_all | solution.py:318
  42.4 12.6 %all_to_all.42.states_ref = bf16[32,16,128]{2,1,0:T(8,128)(2,1)S(1)} all-to-all(bf16[32,16,128]{2,1,0:T(8,128)(2,1)S(1)} %get-tuple-element.16), channel_id=1, replica_groups=mesh['y'=4,'core'=2,'z'=8,'x'=4] {'z','x'}, dimensions={0} | all-to-all | bytes 262144 | tf_op jit(solution)/shard_map/all_to_all | solution.py:312
  55.0 0.5 message.1
  55.6 13.8 %all_to_all.43.recv_ref = bf16[8,144,128]{2,1,0:T(8,128)(2,1)S(1)} all-to-all(bf16[8,144,128]{2,1,0:T(8,128)(2,1)S(1)} %message.1), channel_id=1, replica_groups=mesh['y'=4,'core'=2,'z'=8,'x'=4] {'y','core'}, dimensions={0} | all-to-all | bytes 589824 | tf_op jit(solution)/shard_map/all_to_all | solution.py:396
  69.4 1.4 %gates.1 = (bf16[128,128]{1,0:T(8,128)(2,1)S(1)}, f32[16,128]{1,0:T(8,128)S(1)}, bf16[32,16,128]{2,1,0:T(8,128)(2,1)S(1)}) custom-call(bf16[8,144,128]{2,1,0:T(8,128)(2,1)S(1)} %all_to_all.43.recv_ref, bf16[128,2048]{1,0:T(8,128)(2,1)S(1)} %counts.1.refs_3_.count_ref, bf16[128,128]{1,0:T(8,128)(2,1)S(1)} %copy-done.5, bf16[128,512]{1,0:T(8,128)(2,1)S(1)} %copy-done.2, ...), custom_call_target="tpu_custom_call" | custom-call | tf_op jit(solution)/shard_map/gates/pallas_call | solution.py:397
  70.8 12.3 %all_to_all.44.part_ref = bf16[32,16,128]{2,1,0:T(8,128)(2,1)S(1)} all-to-all(bf16[32,16,128]{2,1,0:T(8,128)(2,1)S(1)} %get-tuple-element.19), channel_id=1, replica_groups=mesh['y'=4,'core'=2,'z'=8,'x'=4] {'z','x'}, dimensions={0} | all-to-all | bytes 262144 | tf_op jit(solution)/shard_map/all_to_all | solution.py:312
  83.1 9.2 %all_to_all.45 = bf16[8,16,128]{2,1,0:T(8,128)(2,1)S(1)} all-to-all(bf16[8,16,128]{2,1,0:T(8,128)(2,1)S(1)} %first_grad.1), channel_id=1, replica_groups=mesh['y'=4,'core'=2,'z'=8,'x'=4] {'z'}, dimensions={0} | all-to-all | bytes 65536 | tf_op jit(solution)/shard_map/all_to_all | solution.py:318
  92.4 0.1 broadcast_in_dim.8
  92.5 12.2 %all_to_all.46.refs_4_ = bf16[16,128,128]{2,1,0:T(8,128)(2,1)S(1)} all-to-all(bf16[16,128,128]{2,1,0:T(8,128)(2,1)S(1)} %broadcast_in_dim.8), channel_id=1, replica_groups=mesh['y'=4,'core'=2,'z'=8,'x'=4] {'y','x'}, dimensions={0} | all-to-all | bytes 1048576 | tf_op jit(solution)/shard_map/all_to_all | solution.py:315
  104.7 2.7 %spread.1 = (bf16[128,2048]{1,0:T(8,128)(2,1)S(1)}, bf16[128,128]{1,0:T(8,128)(2,1)}) custom-call(s32[64]{0:T(128)S(1)} %copy-done.9, s32[64]{0:T(128)S(1)} %copy-done.10, s32[1]{0:T(128)S(6)} %copy.15.refs_2_, bf16[128,128]{1,0:T(8,128)(2,1)S(1)} %get-tuple-element.18.refs_3_, bf16[16,128,128]{2,1,0:T(8,128)(2,1)S(1)} %all_to_all.46.refs_4_, ...), custom_call_target="tpu_custom_call" | custom-call | tf_op jit(solution)/shard_map/spread/pallas_call | solution.py:417
  107.4 4.5 %collective-permute-start.2 = (bf16[128,2048]{1,0:T(8,128)(2,1)S(1)}, bf16[128,2048]{1,0:T(8,128)(2,1)S(1)}, u32[]{:S(2)}, u32[]{:S(2)}) collective-permute-start(bf16[128,2048]{1,0:T(8,128)(2,1)S(1)} %get-tuple-element.23.spread_ref), channel_id=1, source_target_pairs={{0,32},{32,0},{1,33},{33,1},{2,34},{34,2},{3,35},{35,3},{4,36},{36... | collective-permute-start | bytes 1572872 | tf_op jit(solution)/shard_map/ppermute | solution.py:321
  111.9 0.4 weight_own.1.part_ref
  112.4 1.1 collective-permute-done.2.spread_ref
  113.5 0.5 weight_all.1
  114.0 12.7 %all_to_all.47 = bf16[32,16,128]{2,1,0:T(8,128)(2,1)S(1)} all-to-all(bf16[32,16,128]{2,1,0:T(8,128)(2,1)S(1)} %weight_all.1), channel_id=1, replica_groups=mesh['y'=4,'core'=2,'z'=8,'x'=4] {'z','x'}, dimensions={0} | all-to-all | bytes 262144 | tf_op jit(solution)/shard_map/all_to_all | solution.py:312
  126.7 0.6 convert_reduce_fusion.1
  (26 shorter events, 0.2 us)
Async XLA Ops:
  0.6 6.6 %copy-start.8 = (s32[128,8]{0,1:T(8,128)S(1)}, s32[128,8]{0,1:T(8,128)}, u32[]{:S(2)}) copy-start(s32[128,8]{0,1:T(8,128)} %param.19) | copy-start | bytes 12292
  0.6 6.6 %copy-start.7 = (s32[128,8]{0,1:T(8,128)S(1)}, s32[128,8]{0,1:T(8,128)}, u32[]{:S(2)}) copy-start(s32[128,8]{0,1:T(8,128)} %param.18) | copy-start | bytes 12292
  0.7 8.1 %copy-start.10 = (s32[64]{0:T(128)S(1)}, s32[64]{0:T(128)}, u32[]{:S(2)}) copy-start(s32[64]{0:T(128)} %refs_1_.3) | copy-start | bytes 772
  0.7 8.1 %copy-start.9 = (s32[64]{0:T(128)S(1)}, s32[64]{0:T(128)}, u32[]{:S(2)}) copy-start(s32[64]{0:T(128)} %refs_0_.3) | copy-start | bytes 772
  0.7 8.1 %copy-start.1 = (bf16[64,128,128]{2,1,0:T(8,128)(2,1)S(1)}, bf16[64,128,128]{2,1,0:T(8,128)(2,1)}, u32[]{:S(2)}) copy-start(bf16[64,128,128]{2,1,0:T(8,128)(2,1)} %refs_5_.1) | copy-start | bytes 6291460
  3.2 5.1 %collective-permute-start.1 = (f32[1024,128]{1,0:T(8,128)S(1)}, f32[1024,128]{1,0:T(8,128)S(1)}, u32[]{:S(2)}, u32[]{:S(2)}) collective-permute-start(f32[1024,128]{1,0:T(8,128)S(1)} %project_rest.1.refs_6_), channel_id=1, source_target_pairs={{0,32},{32,0},{1,33},{33,1},{2,34},{34,2},{3,35},{35,3},{4,36},{36... | collective-permute-start | bytes 1572872 | tf_op jit(solution)/shard_map/ppermute | solution.py:321
  6.5 2.3 %collective-permute-start = (f32[1024,128]{1,0:T(8,128)S(1)}, f32[1024,128]{1,0:T(8,128)S(1)}, u32[]{:S(2)}, u32[]{:S(2)}) collective-permute-start(f32[1024,128]{1,0:T(8,128)S(1)} %get-tuple-element.13.refs_5_), channel_id=1, source_target_pairs={{0,32},{32,0},{1,33},{33,1},{2,34},{34,2},{3,35},{35,3},{4,36},{36... | collective-permute-start | bytes 1572872 | tf_op jit(solution)/shard_map/ppermute | solution.py:321
  11.3 43.7 %copy-start.2 = (bf16[128,512]{1,0:T(8,128)(2,1)S(1)}, bf16[128,512]{1,0:T(8,128)(2,1)}, u32[]{:S(2)}) copy-start(bf16[128,512]{1,0:T(8,128)(2,1)} %w_edge_ref.1) | copy-start | bytes 393220
  11.3 58.0 %copy-start.3 = (bf16[128,384]{1,0:T(8,128)(2,1)S(1)}, bf16[128,384]{1,0:T(8,128)(2,1)}, u32[]{:S(2)}) copy-start(bf16[128,384]{1,0:T(8,128)(2,1)} %w_in_ref.1) | copy-start | bytes 294916
  11.4 58.0 %copy-start.4 = (bf16[128,256]{1,0:T(8,128)(2,1)S(1)}, bf16[128,256]{1,0:T(8,128)(2,1)}, u32[]{:S(2)}) copy-start(bf16[128,256]{1,0:T(8,128)(2,1)} %w_state_ref.1) | copy-start | bytes 196612
  11.4 58.0 %copy-start.5 = (bf16[128,128]{1,0:T(8,128)(2,1)S(1)}, bf16[128,128]{1,0:T(8,128)(2,1)}, u32[]{:S(2)}) copy-start(bf16[128,128]{1,0:T(8,128)(2,1)} %grad_ref.1) | copy-start | bytes 98308
  11.4 58.0 %copy-start.6 = (bf16[128,128]{1,0:T(8,128)(2,1)S(1)}, bf16[128,128]{1,0:T(8,128)(2,1)}, u32[]{:S(2)}) copy-start(bf16[128,128]{1,0:T(8,128)(2,1)} %w_cand_ref.1) | copy-start | bytes 98308
  92.4 19.6 %copy-start = (bf16[2048,512]{1,0:T(8,128)(2,1)S(1)}, bf16[2048,512]{1,0:T(8,128)(2,1)}, u32[]{:S(2)}) copy-start(bf16[2048,512]{1,0:T(8,128)(2,1)} %feats_ref.3) | copy-start | bytes 6291460
  107.4 6.0 %collective-permute-start.2 = (bf16[128,2048]{1,0:T(8,128)(2,1)S(1)}, bf16[128,2048]{1,0:T(8,128)(2,1)S(1)}, u32[]{:S(2)}, u32[]{:S(2)}) collective-permute-start(bf16[128,2048]{1,0:T(8,128)(2,1)S(1)} %get-tuple-element.23.spread_ref), channel_id=1, source_target_pairs={{0,32},{32,0},{1,33},{33,1},{2,34},{34,2},{3,35},{35,3},{4,36},{36... | collective-permute-start | bytes 1572872 | tf_op jit(solution)/shard_map/ppermute | solution.py:321

commit v5 on v4

--- a/solution.py
+++ b/solution.py
@@ -118,7 +118,7 @@
         copy.wait()
     core = lax.axis_index("core")
     count = count_ref[0]
-    step = 8
+    step = 16
 
     def some_slots(group, carry):
         for j in range(step):
@@ -138,13 +138,14 @@
     out_ref[...] = acc[...].astype(BF16).reshape(out_ref.shape)
 
 
-def count_kernel(nbr_ref, type_ref, count_ref, *, cuts, block):
+def count_kernel(nbr_ref, type_ref, count_ref, *, cuts, block, near, far):
     fanout, rows = nbr_ref.shape
     cells = count_ref.shape[1]
     piece = block // cuts
     nbr = nbr_ref[...]
     within = nbr % block
-    local = (nbr // block) * piece + within % piece
+    owner = nbr // block
+    local = ((owner % near) * far + owner // near) * piece + within % piece
     per_type = cells // 4
     key = jnp.where(within // piece == cut_index(), type_ref[...] * per_type + local, -1)
     key = jnp.concatenate([key, jnp.zeros((rows - fanout, rows), jnp.int32)], axis=0).T
@@ -157,21 +158,27 @@
         count_ref[:, start : start + tile] = total.astype(BF16)
 
 
-def state_kernel(part_ref, first_ref, own_ref, out_ref):
+def fold_kernel(part_ref, out_ref):
+    total = jnp.sum(part_ref[...].astype(F32), axis=0).astype(BF16)
+    for i in range(out_ref.shape[0]):
+        out_ref[i] = total
+
+
+def state_kernel(part_ref, exact_ref, own_ref, out_ref):
     total = jnp.sum(part_ref[...].astype(F32), axis=0)
     exact = jnp.tanh(total)
-    first_ref[...] = exact
+    exact_ref[...] = exact
     states = exact.astype(BF16)
-    own_ref[...] = states
-    for q in range(out_ref.shape[0]):
-        out_ref[q] = states
+    for i in range(out_ref.shape[0]):
+        out_ref[i] = states
+    piece = own_ref.shape[0]
+    own_ref[...] = out_ref[0, pl.ds(pl.multiple_of(lax.axis_index("z") * piece, piece), piece), :]
 
 
 def message_kernel(count_ref, states_ref, own_ref, w_ref, out_ref):
     hidden = own_ref.shape[1]
     rows = count_ref.shape[0]
-    domains, piece, _ = states_ref.shape
-    local = domains * piece
+    local = states_ref.shape[0] * states_ref.shape[1]
     states = states_ref[...].reshape(local, hidden)
     message = jnp.zeros((rows, hidden), F32)
     for e in range(count_ref.shape[1] // local):
@@ -185,7 +192,7 @@
 
 def gate_kernel(
     recv_ref, count_ref, grad_ref, w_edge_ref, w_in_ref, w_state_ref, w_cand_ref,
-    new_ref, direct_ref, back_ref, own,
+    new_ref, back_ref, own, spread,
 ):
     rows, hidden = grad_ref.shape
     cuts = recv_ref.shape[0]
@@ -218,16 +225,21 @@
         + reset_in * reset
         + lax.dot_general(gates[:, : 2 * hidden], w_state, contract, preferred_element_type=F32)
     )
-    direct_ref[...] = own[pl.ds(pl.multiple_of(cut_index() * piece, piece), piece), :]
     total = jnp.zeros((hidden, local), F32)
     for e in range(count_ref.shape[1] // local):
-        spread = dot(message_grad_t, count_ref[:, e * local : (e + 1) * local]).astype(BF16)
-        total += dot(w_edge_ref[:, e * hidden : (e + 1) * hidden], spread)
-    back_ref[...] = total.T.astype(BF16).reshape(back_ref.shape)
-
-
-def grad_kernel(part_ref, direct_ref, exact_ref, out_ref):
-    total = direct_ref[...] + jnp.sum(part_ref[...].astype(F32), axis=0)
+        picked = dot(message_grad_t, count_ref[:, e * local : (e + 1) * local]).astype(BF16)
+        total += dot(w_edge_ref[:, e * hidden : (e + 1) * hidden], picked)
+    spread[...] = total.T
+    far = back_ref.shape[1] // piece
+    place = (lax.axis_index("x") * far + lax.axis_index("z")) * piece
+    spread[pl.ds(pl.multiple_of(place, piece), piece), :] += own[
+        pl.ds(pl.multiple_of(cut_index() * piece, piece), piece), :
+    ]
+    back_ref[...] = spread[...].astype(BF16).reshape(back_ref.shape)
+
+
+def grad_kernel(part_ref, exact_ref, out_ref):
+    total = jnp.sum(part_ref[...].astype(F32), axis=0)
     exact = exact_ref[...]
     grad = (total * (1.0 - exact * exact)).astype(BF16)
     for q in range(out_ref.shape[0]):
@@ -235,7 +247,7 @@
 
 
 def spread_kernel(
-    dst_any, src_any, count_any, new_any, grads_ref, adj, out_ref, new_out,
+    dst_any, src_any, count_any, new_any, grads_ref, adj, out_ref, low_ref, new_out,
     turned, acc, dst_ref, src_ref, count_ref, sems, *, near, far,
 ):
     slots, block, _ = adj.shape
@@ -257,7 +269,7 @@
         copy.wait()
     core = lax.axis_index("core")
     count = count_ref[0]
-    step = 8
+    step = 16
 
     def some_slots(group, carry):
         for j in range(step):
@@ -268,12 +280,17 @@
 
     lax.fori_loop(0, slots // step, some_slots, 0)
     for s in range(acc.shape[0]):
-        out_ref[:, s * block : (s + 1) * block] = acc[s].astype(BF16)
+        high = acc[s].astype(BF16)
+        out_ref[:, s * block : (s + 1) * block] = high
+        low_ref[:, s * block : (s + 1) * block] = (acc[s] - high.astype(F32)).astype(BF16)
     copies[3].wait()
 
 
-def weight_kernel(spread_ref, feats_ref, out_ref):
-    out_ref[...] = dot(spread_ref[...], feats_ref[...])
+def weight_kernel(high_ref, low_ref, feats_ref, out_ref):
+    hidden = high_ref.shape[0]
+    both = jnp.concatenate([high_ref[...], low_ref[...]], axis=0)
+    total = dot(both, feats_ref[...])
+    out_ref[...] = total[:hidden] + total[hidden:]
 
 
 def weight_out_kernel(spread_ref, feats_ref, part_ref, out_ref):
@@ -314,6 +331,9 @@
     def over_plane(x):
         return lax.all_to_all(x, ("y", "x"), 0, 0, tiled=True)
 
+    def over_near(x):
+        return lax.all_to_all(x, "x", 0, 0, tiled=True)
+
     def over_far(x):
         return lax.all_to_all(x, "z", 0, 0, tiled=True)
 
@@ -329,7 +349,7 @@
             jax.ShapeDtypeStruct((rest_rows, feat_cols), BF16),
             jax.ShapeDtypeStruct((feat_cols, hidden), BF16),
         ),
-        in_specs=[hspec(), hspec()],
+        in_specs=[hspec()] * 2,
         out_specs=(vspec(), vspec(), vspec()),
         scratch_shapes=[VMEM((first_rows, feat_cols), BF16), pltpu.SemaphoreType.DMA((9,))],
         compiler_params=params(),
@@ -349,7 +369,7 @@
     mine_parts = [projected, projected_rest]
     swapped = [swap(p) for p in mine_parts]
     counts = pl.pallas_call(
-        lambda *refs: count_kernel(*refs, cuts=cuts, block=block),
+        lambda *refs: count_kernel(*refs, cuts=cuts, block=block, near=near, far=far),
         out_shape=jax.ShapeDtypeStruct((rows, 4 * local), BF16),
         in_specs=[vspec(), vspec()],
         out_specs=vspec(),
@@ -372,19 +392,33 @@
         compiler_params=params(),
         name="partial",
     )(blk_dst, blk_src, blk_count, counts, adjacency, *mine_parts, *swapped)
-    by_plane = jnp.sum(over_plane(partial).astype(F32), axis=0)
-    by_far = over_far(by_plane.reshape(far, piece, hidden))
-    spread = jax.ShapeDtypeStruct((domains, piece, hidden), BF16)
-    small = jax.ShapeDtypeStruct((piece, hidden), F32)
+    group = far * piece
+    tiled = lambda n: jax.ShapeDtypeStruct((n, group, hidden), BF16)
+
+    def fold(x):
+        return pl.pallas_call(
+            fold_kernel,
+            out_shape=tiled(far),
+            in_specs=[vspec()],
+            out_specs=vspec(),
+            compiler_params=params(),
+            name="fold",
+        )(x)
+
+    by_far = over_far(fold(over_plane(partial)))
     exact, own_states, tiled_states = pl.pallas_call(
         state_kernel,
-        out_shape=(small, jax.ShapeDtypeStruct((piece, hidden), BF16), spread),
+        out_shape=(
+            jax.ShapeDtypeStruct((group, hidden), F32),
+            jax.ShapeDtypeStruct((piece, hidden), BF16),
+            tiled(near),
+        ),
         in_specs=[vspec()],
         out_specs=(vspec(), vspec(), vspec()),
         compiler_params=params(),
         name="state",
     )(by_far)
-    states = over_dom(tiled_states)
+    states = over_near(tiled_states)
     sent = pl.pallas_call(
         message_kernel,
         out_shape=jax.ShapeDtypeStruct((cuts, rows + piece, hidden), BF16),
@@ -394,34 +428,34 @@
         name="message",
     )(counts, states, own_states, w_edge)
     recv = lax.all_to_all(sent, ("y", "core"), 0, 0, tiled=True)
-    new_rows, direct, back = pl.pallas_call(
+    new_rows, back = pl.pallas_call(
         gate_kernel,
-        out_shape=(jax.ShapeDtypeStruct((rows, hidden), BF16), small, spread),
+        out_shape=(jax.ShapeDtypeStruct((rows, hidden), BF16), tiled(near)),
         in_specs=[vspec()] * 7,
-        out_specs=(vspec(), vspec(), vspec()),
-        scratch_shapes=[VMEM((rows, hidden), F32)],
+        out_specs=(vspec(), vspec()),
+        scratch_shapes=[VMEM((rows, hidden), F32), VMEM((local, hidden), F32)],
         compiler_params=params(),
         name="gates",
     )(recv, counts, out_grad, w_edge, w_gate_in, w_gate_state, w_cand)
-    grad_part = over_dom(back)
+    grad_part = over_far(fold(over_near(back)))
     own_grad = pl.pallas_call(
         grad_kernel,
-        out_shape=jax.ShapeDtypeStruct((far, piece, hidden), BF16),
-        in_specs=[vspec()] * 3,
+        out_shape=tiled(pairs * near),
+        in_specs=[vspec()] * 2,
         out_specs=vspec(),
         compiler_params=params(),
         name="first_grad",
-    )(grad_part, direct, exact)
-    far_grads = over_far(own_grad).reshape(1, far * piece, hidden)
-    grads = over_plane(jnp.broadcast_to(far_grads, (pairs * near, far * piece, hidden)))
-    mine, new_state = pl.pallas_call(
+    )(grad_part, exact)
+    grads = over_plane(own_grad)
+    mine, mine_low, new_state = pl.pallas_call(
         lambda *refs: spread_kernel(*refs, near=near, far=far),
         out_shape=(
+            jax.ShapeDtypeStruct((hidden, nodes), BF16),
             jax.ShapeDtypeStruct((hidden, nodes), BF16),
             jax.ShapeDtypeStruct((rows, hidden), BF16),
         ),
         in_specs=[aspec()] * 4 + [vspec()] * 2,
-        out_specs=(vspec(), aspec()),
+        out_specs=(vspec(), vspec(), aspec()),
         scratch_shapes=[
             VMEM((domains, hidden, pairs * piece), BF16),
             VMEM((nodes // block, hidden, block), F32),
@@ -437,11 +471,11 @@
     own_part = pl.pallas_call(
         weight_kernel,
         out_shape=jax.ShapeDtypeStruct((hidden, feat_cols), F32),
-        in_specs=[vspec()] * 2,
+        in_specs=[vspec()] * 3,
         out_specs=vspec(),
         compiler_params=params(),
         name="weight_own",
-    )(mine, feats)
+    )(mine, mine_low, feats)
     weight_part = pl.pallas_call(
         weight_out_kernel,
         out_shape=jax.ShapeDtypeStruct((domains, feat_cols // domains, hidden), BF16),

time: 128 us -> 122 us (0.953)
  blocking collectives: 104 us -> 99.2 us
    all_to_all x3 -> x1, blocking collectives: 37.6 us -> 12.7 us  [over_dom(): return lax.all_to_all(x, ('z', 'x'), 0, 0, tiled=True)]
    all_to_all x0 -> x2, blocking collectives: none -> 15.7 us  [over_near(): return lax.all_to_all(x, 'x', 0, 0, tiled=True)]
    all_to_all x2, blocking collectives: 24.4 us -> 29.3 us  [over_far(): return lax.all_to_all(x, 'z', 0, 0, tiled=True)]
where the time goes in v5:
time: 122 us
  blocking collectives  99.2 us (81%)
  Pallas kernels  11.2 us (9%)
  starting transfers between devices  7.64 us (6%)
  between operations  1.49 us (1%)
  waiting for transfers between devices  1.26 us (1%)
    all_to_all x2, blocking collectives, over_far(): return lax.all_to_all(x, 'z', 0, 0, tiled=True)  29.3 us
    all_to_all x2, blocking collectives, over_plane(): return lax.all_to_all(x, ('y', 'x'), 0, 0, tiled=True)  27.8 us
    all_to_all x2, blocking collectives, over_near(): return lax.all_to_all(x, 'x', 0, 0, tiled=True)  15.7 us
    all_to_all x1, blocking collectives, body(): recv = lax.all_to_all(sent, ('y', 'core'), 0, 0, tiled=True)  13.6 us
    all_to_all x1, blocking collectives, over_dom(): return lax.all_to_all(x, ('z', 'x'), 0, 0, tiled=True)  12.7 us
    ppermute x3, starting transfers between devices, swap(): return lax.ppermute(x, 'core', [(0, 1), (1, 0)])  7.64 us
  transfers between devices with their start and end apart: 3, of which 2 were waited for; matrix products, arithmetic and copies ran while one was open for 0% of the time, Pallas kernels for 1%

profile of v5, /device:TPU:1, one launch (start us, length us, event | category | flops | bytes accessed | tf_op | source)
XLA Modules:
  0.0 121.5 jit_solution(17797166864509699100)
XLA Ops:
  0.7 2.1 %project.1 = (f32[1024,128]{1,0:T(8,128)S(1)}, bf16[1024,512]{1,0:T(8,128)(2,1)S(1)}, bf16[512,128]{1,0:T(8,128)(2,1)S(1)}) custom-call(bf16[2048,512]{1,0:T(8,128)(2,1)} %feats_ref.3, bf16[512,128]{1,0:T(8,128)(2,1)} %w_hbm.1), custom_call_target="tpu_custom_call" | custom-call | tf_op jit(solution)/shard_map/project/pallas_call | solution.py:345
  2.8 0.4 project_rest.1.refs_6_
  3.2 3.3 %collective-permute-start.1 = (f32[1024,128]{1,0:T(8,128)S(1)}, f32[1024,128]{1,0:T(8,128)S(1)}, u32[]{:S(2)}, u32[]{:S(2)}) collective-permute-start(f32[1024,128]{1,0:T(8,128)S(1)} %project_rest.1.refs_6_), channel_id=1, source_target_pairs={{0,32},{32,0},{1,33},{33,1},{2,34},{34,2},{3,35},{35,3},{4,36},{36... | collective-permute-start | bytes 1572872 | tf_op jit(solution)/shard_map/ppermute | solution.py:341
  6.5 0.1 collective-permute-start
  7.3 1.1 counts.1.refs_3_.count_ref
  8.4 0.4 collective-permute-done.refs_7_
  8.8 1.9 %partial.1 = bf16[16,128,128]{2,1,0:T(8,128)(2,1)S(1)} custom-call(s32[64]{0:T(128)S(1)} %copy-done.9, s32[64]{0:T(128)S(1)} %copy-done.10, s32[1]{0:T(128)S(6)} %copy.15.refs_2_, bf16[128,2048]{1,0:T(8,128)(2,1)S(1)} %counts.1.refs_3_.count_ref, bf16[64,128,128]{2,1,0:T(8,128)(2,1)S(1)} %copy-done.1, f32[1024,128]{1,0:T(8,128)S(1)} %get-tuple-element.13.refs_5_, ...), custom_call_target="tpu_custom_call" | custom-call | tf_op jit(solution)/shard_map/partial/pallas_call | solution.py:379
  10.8 15.7 %all_to_all.40.part_ref = bf16[16,128,128]{2,1,0:T(8,128)(2,1)S(1)} all-to-all(bf16[16,128,128]{2,1,0:T(8,128)(2,1)S(1)} %partial.1), channel_id=1, replica_groups=mesh['y'=4,'core'=2,'z'=8,'x'=4] {'y','x'}, dimensions={0} | all-to-all | bytes 1048576 | tf_op jit(solution)/shard_map/all_to_all | solution.py:332
  26.5 0.1 fold.2
  26.6 17.1 %all_to_all.41.part_ref = bf16[8,128,128]{2,1,0:T(8,128)(2,1)S(1)} all-to-all(bf16[8,128,128]{2,1,0:T(8,128)(2,1)S(1)} %fold.2), channel_id=1, replica_groups=mesh['y'=4,'core'=2,'z'=8,'x'=4] {'z'}, dimensions={0} | all-to-all | bytes 524288 | tf_op jit(solution)/shard_map/all_to_all | solution.py:338
  43.8 8.5 %all_to_all.42.states_ref = bf16[4,128,128]{2,1,0:T(8,128)(2,1)S(1)} all-to-all(bf16[4,128,128]{2,1,0:T(8,128)(2,1)S(1)} %get-tuple-element.16), channel_id=1, replica_groups=mesh['y'=4,'core'=2,'z'=8,'x'=4] {'x'}, dimensions={0} | all-to-all | bytes 262144 | tf_op jit(solution)/shard_map/all_to_all | solution.py:335
  52.3 0.5 message.1
  52.8 13.6 %all_to_all.43.recv_ref = bf16[8,144,128]{2,1,0:T(8,128)(2,1)S(1)} all-to-all(bf16[8,144,128]{2,1,0:T(8,128)(2,1)S(1)} %message.1), channel_id=1, replica_groups=mesh['y'=4,'core'=2,'z'=8,'x'=4] {'y','core'}, dimensions={0} | all-to-all | bytes 589824 | tf_op jit(solution)/shard_map/all_to_all | solution.py:430
  66.4 1.5 %gates.1 = (bf16[128,128]{1,0:T(8,128)(2,1)S(1)}, bf16[4,128,128]{2,1,0:T(8,128)(2,1)S(1)}) custom-call(bf16[8,144,128]{2,1,0:T(8,128)(2,1)S(1)} %all_to_all.43.recv_ref, bf16[128,2048]{1,0:T(8,128)(2,1)S(1)} %counts.1.refs_3_.count_ref, bf16[128,128]{1,0:T(8,128)(2,1)S(1)} %copy-done.5, bf16[128,512]{1,0:T(8,128)(2,1)S(1)} %copy-done.2, ...), custom_call_target="tpu_custom_call" | custom-call | tf_op jit(solution)/shard_map/gates/pallas_call | solution.py:431
  67.9 7.2 %all_to_all.44.part_ref = bf16[4,128,128]{2,1,0:T(8,128)(2,1)S(1)} all-to-all(bf16[4,128,128]{2,1,0:T(8,128)(2,1)S(1)} %get-tuple-element.19), channel_id=1, replica_groups=mesh['y'=4,'core'=2,'z'=8,'x'=4] {'x'}, dimensions={0} | all-to-all | bytes 262144 | tf_op jit(solution)/shard_map/all_to_all | solution.py:335
  75.2 12.2 %all_to_all.45.part_ref = bf16[8,128,128]{2,1,0:T(8,128)(2,1)S(1)} all-to-all(bf16[8,128,128]{2,1,0:T(8,128)(2,1)S(1)} %fold.3), channel_id=1, replica_groups=mesh['y'=4,'core'=2,'z'=8,'x'=4] {'z'}, dimensions={0} | all-to-all | bytes 524288 | tf_op jit(solution)/shard_map/all_to_all | solution.py:338
  87.4 12.1 %all_to_all.46.refs_4_ = bf16[16,128,128]{2,1,0:T(8,128)(2,1)S(1)} all-to-all(bf16[16,128,128]{2,1,0:T(8,128)(2,1)S(1)} %first_grad.1), channel_id=1, replica_groups=mesh['y'=4,'core'=2,'z'=8,'x'=4] {'y','x'}, dimensions={0} | all-to-all | bytes 1048576 | tf_op jit(solution)/shard_map/all_to_all | solution.py:332
  99.5 2.3 %spread.1 = (bf16[128,2048]{1,0:T(8,128)(2,1)S(1)}, bf16[128,2048]{1,0:T(8,128)(2,1)S(1)}, bf16[128,128]{1,0:T(8,128)(2,1)}) custom-call(s32[64]{0:T(128)S(1)} %copy-done.9, s32[64]{0:T(128)S(1)} %copy-done.10, s32[1]{0:T(128)S(6)} %copy.15.refs_2_, bf16[128,128]{1,0:T(8,128)(2,1)S(1)} %get-tuple-element.18.refs_3_, ...), custom_call_target="tpu_custom_call" | custom-call | tf_op jit(solution)/shard_map/spread/pallas_call | solution.py:450
  101.8 4.2 %collective-permute-start.2 = (bf16[128,2048]{1,0:T(8,128)(2,1)S(1)}, bf16[128,2048]{1,0:T(8,128)(2,1)S(1)}, u32[]{:S(2)}, u32[]{:S(2)}) collective-permute-start(bf16[128,2048]{1,0:T(8,128)(2,1)S(1)} %get-tuple-element.22.high_ref), channel_id=1, source_target_pairs={{0,32},{32,0},{1,33},{33,1},{2,34},{34,2},{3,35},{35,3},{4,36},{36... | collective-permute-start | bytes 1572872 | tf_op jit(solution)/shard_map/ppermute | solution.py:341
  106.1 0.7 weight_own.1.part_ref
  106.8 0.8 collective-permute-done.2.spread_ref
  107.6 0.5 weight_all.1
  108.1 12.7 %all_to_all.47 = bf16[32,16,128]{2,1,0:T(8,128)(2,1)S(1)} all-to-all(bf16[32,16,128]{2,1,0:T(8,128)(2,1)S(1)} %weight_all.1), channel_id=1, replica_groups=mesh['y'=4,'core'=2,'z'=8,'x'=4] {'z','x'}, dimensions={0} | all-to-all | bytes 262144 | tf_op jit(solution)/shard_map/all_to_all | solution.py:329
  120.9 0.6 convert_reduce_fusion
  (26 shorter events, 0.2 us)
Async XLA Ops:
  0.6 6.6 %copy-start.8 = (s32[128,8]{0,1:T(8,128)S(1)}, s32[128,8]{0,1:T(8,128)}, u32[]{:S(2)}) copy-start(s32[128,8]{0,1:T(8,128)} %param.19) | copy-start | bytes 12292
  0.6 6.6 %copy-start.7 = (s32[128,8]{0,1:T(8,128)S(1)}, s32[128,8]{0,1:T(8,128)}, u32[]{:S(2)}) copy-start(s32[128,8]{0,1:T(8,128)} %param.18) | copy-start | bytes 12292
  0.7 8.1 %copy-start.10 = (s32[64]{0:T(128)S(1)}, s32[64]{0:T(128)}, u32[]{:S(2)}) copy-start(s32[64]{0:T(128)} %refs_1_.3) | copy-start | bytes 772
  0.7 8.1 %copy-start.9 = (s32[64]{0:T(128)S(1)}, s32[64]{0:T(128)}, u32[]{:S(2)}) copy-start(s32[64]{0:T(128)} %refs_0_.3) | copy-start | bytes 772
  0.7 8.1 %copy-start.1 = (bf16[64,128,128]{2,1,0:T(8,128)(2,1)S(1)}, bf16[64,128,128]{2,1,0:T(8,128)(2,1)}, u32[]{:S(2)}) copy-start(bf16[64,128,128]{2,1,0:T(8,128)(2,1)} %refs_5_.1) | copy-start | bytes 6291460
  3.2 5.1 %collective-permute-start.1 = (f32[1024,128]{1,0:T(8,128)S(1)}, f32[1024,128]{1,0:T(8,128)S(1)}, u32[]{:S(2)}, u32[]{:S(2)}) collective-permute-start(f32[1024,128]{1,0:T(8,128)S(1)} %project_rest.1.refs_6_), channel_id=1, source_target_pairs={{0,32},{32,0},{1,33},{33,1},{2,34},{34,2},{3,35},{35,3},{4,36},{36... | collective-permute-start | bytes 1572872 | tf_op jit(solution)/shard_map/ppermute | solution.py:341
  6.5 2.3 %collective-permute-start = (f32[1024,128]{1,0:T(8,128)S(1)}, f32[1024,128]{1,0:T(8,128)S(1)}, u32[]{:S(2)}, u32[]{:S(2)}) collective-permute-start(f32[1024,128]{1,0:T(8,128)S(1)} %get-tuple-element.13.refs_5_), channel_id=1, source_target_pairs={{0,32},{32,0},{1,33},{33,1},{2,34},{34,2},{3,35},{35,3},{4,36},{36... | collective-permute-start | bytes 1572872 | tf_op jit(solution)/shard_map/ppermute | solution.py:341
  10.7 41.6 %copy-start.2 = (bf16[128,512]{1,0:T(8,128)(2,1)S(1)}, bf16[128,512]{1,0:T(8,128)(2,1)}, u32[]{:S(2)}) copy-start(bf16[128,512]{1,0:T(8,128)(2,1)} %w_edge_ref.1) | copy-start | bytes 393220
  10.7 55.7 %copy-start.3 = (bf16[128,384]{1,0:T(8,128)(2,1)S(1)}, bf16[128,384]{1,0:T(8,128)(2,1)}, u32[]{:S(2)}) copy-start(bf16[128,384]{1,0:T(8,128)(2,1)} %w_in_ref.1) | copy-start | bytes 294916
  10.7 55.7 %copy-start.4 = (bf16[128,256]{1,0:T(8,128)(2,1)S(1)}, bf16[128,256]{1,0:T(8,128)(2,1)}, u32[]{:S(2)}) copy-start(bf16[128,256]{1,0:T(8,128)(2,1)} %w_state_ref.1) | copy-start | bytes 196612
  10.7 55.7 %copy-start.5 = (bf16[128,128]{1,0:T(8,128)(2,1)S(1)}, bf16[128,128]{1,0:T(8,128)(2,1)}, u32[]{:S(2)}) copy-start(bf16[128,128]{1,0:T(8,128)(2,1)} %grad_ref.1) | copy-start | bytes 98308
  10.8 55.7 %copy-start.6 = (bf16[128,128]{1,0:T(8,128)(2,1)S(1)}, bf16[128,128]{1,0:T(8,128)(2,1)}, u32[]{:S(2)}) copy-start(bf16[128,128]{1,0:T(8,128)(2,1)} %w_cand_ref.1) | copy-start | bytes 98308
  87.4 18.7 %copy-start = (bf16[2048,512]{1,0:T(8,128)(2,1)S(1)}, bf16[2048,512]{1,0:T(8,128)(2,1)}, u32[]{:S(2)}) copy-start(bf16[2048,512]{1,0:T(8,128)(2,1)} %feats_ref.3) | copy-start | bytes 6291460
  101.8 5.8 %collective-permute-start.2 = (bf16[128,2048]{1,0:T(8,128)(2,1)S(1)}, bf16[128,2048]{1,0:T(8,128)(2,1)S(1)}, u32[]{:S(2)}, u32[]{:S(2)}) collective-permute-start(bf16[128,2048]{1,0:T(8,128)(2,1)S(1)} %get-tuple-element.22.high_ref), channel_id=1, source_target_pairs={{0,32},{32,0},{1,33},{33,1},{2,34},{34,2},{3,35},{35,3},{4,36},{36... | collective-permute-start | bytes 1572872 | tf_op jit(solution)/shard_map/ppermute | solution.py:341

commit v6 on v5

--- a/solution.py
+++ b/solution.py
@@ -118,7 +118,7 @@
         copy.wait()
     core = lax.axis_index("core")
     count = count_ref[0]
-    step = 16
+    step = 32
 
     def some_slots(group, carry):
         for j in range(step):
@@ -138,7 +138,10 @@
     out_ref[...] = acc[...].astype(BF16).reshape(out_ref.shape)
 
 
-def count_kernel(nbr_ref, type_ref, count_ref, *, cuts, block, near, far):
+def count_kernel(
+    nbr_ref, type_ref, adj_hbm, count_ref, adj_ref, sems, *, cuts, block, near, far
+):
+    copies = start_all([(adj_hbm, adj_ref)], sems)
     fanout, rows = nbr_ref.shape
     cells = count_ref.shape[1]
     piece = block // cuts
@@ -156,6 +159,7 @@
         for k in range(fanout):
             total += jnp.where(key[:, k : k + 1] == place, 1.0, 0.0)
         count_ref[:, start : start + tile] = total.astype(BF16)
+    copies[0].wait()
 
 
 def fold_kernel(part_ref, out_ref):
@@ -269,7 +273,7 @@
         copy.wait()
     core = lax.axis_index("core")
     count = count_ref[0]
-    step = 16
+    step = 32
 
     def some_slots(group, carry):
         for j in range(step):
@@ -368,14 +372,18 @@
     )(rest, w)
     mine_parts = [projected, projected_rest]
     swapped = [swap(p) for p in mine_parts]
-    counts = pl.pallas_call(
+    counts, adj = pl.pallas_call(
         lambda *refs: count_kernel(*refs, cuts=cuts, block=block, near=near, far=far),
-        out_shape=jax.ShapeDtypeStruct((rows, 4 * local), BF16),
-        in_specs=[vspec(), vspec()],
-        out_specs=vspec(),
+        out_shape=(
+            jax.ShapeDtypeStruct((rows, 4 * local), BF16),
+            jax.ShapeDtypeStruct(adjacency.shape, BF16),
+        ),
+        in_specs=[vspec(), vspec(), hspec()],
+        out_specs=(vspec(), vspec()),
+        scratch_shapes=[pltpu.SemaphoreType.DMA((1,))],
         compiler_params=params(),
         name="counts",
-    )(nbr_ids.T, edge_types.T)
+    )(nbr_ids.T, edge_types.T, pltpu.with_memory_space_constraint(adjacency, pltpu.HBM))
     partial = pl.pallas_call(
         lambda *refs: partial_kernel(*refs, near=near, far=far),
         out_shape=jax.ShapeDtypeStruct((pairs * near, far * piece, hidden), BF16),
@@ -391,7 +399,7 @@
         ],
         compiler_params=params(),
         name="partial",
-    )(blk_dst, blk_src, blk_count, counts, adjacency, *mine_parts, *swapped)
+    )(blk_dst, blk_src, blk_count, counts, adj, *mine_parts, *swapped)
     group = far * piece
     tiled = lambda n: jax.ShapeDtypeStruct((n, group, hidden), BF16)
 
@@ -466,7 +474,7 @@
         ],
         compiler_params=params(),
         name="spread",
-    )(blk_dst, blk_src, blk_count, new_rows, grads, adjacency)
+    )(blk_dst, blk_src, blk_count, new_rows, grads, adj)
     other = swap(mine)
     own_part = pl.pallas_call(
         weight_kernel,

time: 122 us -> 121 us (level)
  transfers between devices with their start and end apart: 3 -> 3, of which waited for: 2 -> 1; matrix products, arithmetic and copies ran while one was open for 0% -> 0% of each run, Pallas kernels for 1% -> 2%
where the time goes in v6:
time: 121 us
  blocking collectives  99.2 us (82%)
  Pallas kernels  11.1 us (9%)
  starting transfers between devices  7.57 us (6%)
  between operations  1.51 us (1%)
    all_to_all x2, blocking collectives, over_far(): return lax.all_to_all(x, 'z', 0, 0, tiled=True)  29.4 us
    all_to_all x2, blocking collectives, over_plane(): return lax.all_to_all(x, ('y', 'x'), 0, 0, tiled=True)  27.8 us
    all_to_all x2, blocking collectives, over_near(): return lax.all_to_all(x, 'x', 0, 0, tiled=True)  15.5 us
    all_to_all x1, blocking collectives, body(): recv = lax.all_to_all(sent, ('y', 'core'), 0, 0, tiled=True)  13.7 us
    all_to_all x1, blocking collectives, over_dom(): return lax.all_to_all(x, ('z', 'x'), 0, 0, tiled=True)  12.7 us
    ppermute x3, starting transfers between devices, swap(): return lax.ppermute(x, 'core', [(0, 1), (1, 0)])  7.57 us
  transfers between devices with their start and end apart: 3, of which 1 were waited for; matrix products, arithmetic and copies ran while one was open for 0% of the time, Pallas kernels for 2%

profile of v6, /device:TPU:1, one launch (start us, length us, event | category | flops | bytes accessed | tf_op | source)
XLA Modules:
  0.0 120.9 jit_solution(14767449667963339030)
XLA Ops:
  0.7 2.0 %project.1 = (f32[1024,128]{1,0:T(8,128)S(1)}, bf16[1024,512]{1,0:T(8,128)(2,1)S(1)}, bf16[512,128]{1,0:T(8,128)(2,1)S(1)}) custom-call(bf16[2048,512]{1,0:T(8,128)(2,1)} %feats_ref.3, bf16[512,128]{1,0:T(8,128)(2,1)} %w_hbm.1), custom_call_target="tpu_custom_call" | custom-call | tf_op jit(solution)/shard_map/project/pallas_call | solution.py:349
  2.7 0.4 project_rest.1.refs_6_
  3.1 3.3 %collective-permute-start.1 = (f32[1024,128]{1,0:T(8,128)S(1)}, f32[1024,128]{1,0:T(8,128)S(1)}, u32[]{:S(2)}, u32[]{:S(2)}) collective-permute-start(f32[1024,128]{1,0:T(8,128)S(1)} %project_rest.1.refs_6_), channel_id=1, source_target_pairs={{0,32},{32,0},{1,33},{33,1},{2,34},{34,2},{3,35},{35,3},{4,36},{36... | collective-permute-start | bytes 1572872 | tf_op jit(solution)/shard_map/ppermute | solution.py:345
  6.4 0.1 collective-permute-start
  7.2 1.6 %counts.1 = (bf16[128,2048]{1,0:T(8,128)(2,1)S(1)}, bf16[64,128,128]{2,1,0:T(8,128)(2,1)S(1)}) custom-call(s32[8,128]{1,0:T(8,128)S(1)} %bitcast.2, s32[8,128]{1,0:T(8,128)S(1)} %bitcast.3, bf16[64,128,128]{2,1,0:T(8,128)(2,1)} %refs_2_.3), custom_call_target="tpu_custom_call" | custom-call | tf_op jit(solution)/shard_map/counts/pallas_call | solution.py:375
  8.8 1.6 %partial.1 = bf16[16,128,128]{2,1,0:T(8,128)(2,1)S(1)} custom-call(s32[64]{0:T(128)S(1)} %copy-done.8, s32[64]{0:T(128)S(1)} %copy-done.9, s32[1]{0:T(128)S(6)} %copy.15.refs_2_, bf16[128,2048]{1,0:T(8,128)(2,1)S(1)} %get-tuple-element.15.refs_3_.count_ref, bf16[64,128,128]{2,1,0:T(8,128)(2,1)S(1)} %get-tuple-element.16.refs_4_.refs_5_, ...), custom_call_target="tpu_custom_call" | custom-call | tf_op jit(solution)/shard_map/partial/pallas_call | solution.py:387
  10.5 15.7 %all_to_all.40.part_ref = bf16[16,128,128]{2,1,0:T(8,128)(2,1)S(1)} all-to-all(bf16[16,128,128]{2,1,0:T(8,128)(2,1)S(1)} %partial.1), channel_id=1, replica_groups=mesh['y'=4,'core'=2,'z'=8,'x'=4] {'y','x'}, dimensions={0} | all-to-all | bytes 1048576 | tf_op jit(solution)/shard_map/all_to_all | solution.py:336
  26.2 0.1 fold.2
  26.3 17.2 %all_to_all.41.part_ref = bf16[8,128,128]{2,1,0:T(8,128)(2,1)S(1)} all-to-all(bf16[8,128,128]{2,1,0:T(8,128)(2,1)S(1)} %fold.2), channel_id=1, replica_groups=mesh['y'=4,'core'=2,'z'=8,'x'=4] {'z'}, dimensions={0} | all-to-all | bytes 524288 | tf_op jit(solution)/shard_map/all_to_all | solution.py:342
  43.5 8.3 %all_to_all.42.states_ref = bf16[4,128,128]{2,1,0:T(8,128)(2,1)S(1)} all-to-all(bf16[4,128,128]{2,1,0:T(8,128)(2,1)S(1)} %get-tuple-element.20), channel_id=1, replica_groups=mesh['y'=4,'core'=2,'z'=8,'x'=4] {'x'}, dimensions={0} | all-to-all | bytes 262144 | tf_op jit(solution)/shard_map/all_to_all | solution.py:339
  51.9 0.5 message.1
  52.4 13.7 %all_to_all.43.recv_ref = bf16[8,144,128]{2,1,0:T(8,128)(2,1)S(1)} all-to-all(bf16[8,144,128]{2,1,0:T(8,128)(2,1)S(1)} %message.1), channel_id=1, replica_groups=mesh['y'=4,'core'=2,'z'=8,'x'=4] {'y','core'}, dimensions={0} | all-to-all | bytes 589824 | tf_op jit(solution)/shard_map/all_to_all | solution.py:438
  66.1 1.5 %gates.1 = (bf16[128,128]{1,0:T(8,128)(2,1)S(1)}, bf16[4,128,128]{2,1,0:T(8,128)(2,1)S(1)}) custom-call(bf16[8,144,128]{2,1,0:T(8,128)(2,1)S(1)} %all_to_all.43.recv_ref, bf16[128,2048]{1,0:T(8,128)(2,1)S(1)} %get-tuple-element.15.refs_3_.count_ref, bf16[128,128]{1,0:T(8,128)(2,1)S(1)} %copy-done.4, bf16[128,512]{1,0:T(8,128)(2,1)S(1)} %copy-done.1, ...), custom_call_target="tpu_custom_call" | custom-call | tf_op jit(solution)/shard_map/gates/pallas_call | solution.py:439
  67.6 7.2 %all_to_all.44.part_ref = bf16[4,128,128]{2,1,0:T(8,128)(2,1)S(1)} all-to-all(bf16[4,128,128]{2,1,0:T(8,128)(2,1)S(1)} %get-tuple-element.23), channel_id=1, replica_groups=mesh['y'=4,'core'=2,'z'=8,'x'=4] {'x'}, dimensions={0} | all-to-all | bytes 262144 | tf_op jit(solution)/shard_map/all_to_all | solution.py:339
  74.8 12.2 %all_to_all.45.part_ref = bf16[8,128,128]{2,1,0:T(8,128)(2,1)S(1)} all-to-all(bf16[8,128,128]{2,1,0:T(8,128)(2,1)S(1)} %fold.3), channel_id=1, replica_groups=mesh['y'=4,'core'=2,'z'=8,'x'=4] {'z'}, dimensions={0} | all-to-all | bytes 524288 | tf_op jit(solution)/shard_map/all_to_all | solution.py:342
  87.0 0.1 first_grad.1
  87.1 12.2 %all_to_all.46.refs_4_ = bf16[16,128,128]{2,1,0:T(8,128)(2,1)S(1)} all-to-all(bf16[16,128,128]{2,1,0:T(8,128)(2,1)S(1)} %first_grad.1), channel_id=1, replica_groups=mesh['y'=4,'core'=2,'z'=8,'x'=4] {'y','x'}, dimensions={0} | all-to-all | bytes 1048576 | tf_op jit(solution)/shard_map/all_to_all | solution.py:336
  99.2 2.0 %spread.1 = (bf16[128,2048]{1,0:T(8,128)(2,1)S(1)}, bf16[128,2048]{1,0:T(8,128)(2,1)S(1)}, bf16[128,128]{1,0:T(8,128)(2,1)}) custom-call(s32[64]{0:T(128)S(1)} %copy-done.8, s32[64]{0:T(128)S(1)} %copy-done.9, s32[1]{0:T(128)S(6)} %copy.15.refs_2_, bf16[128,128]{1,0:T(8,128)(2,1)S(1)} %get-tuple-element.22.refs_3_, ...), custom_call_target="tpu_custom_call" | custom-call | tf_op jit(solution)/shard_map/spread/pallas_call | solution.py:458
  101.2 4.2 %collective-permute-start.2 = (bf16[128,2048]{1,0:T(8,128)(2,1)S(1)}, bf16[128,2048]{1,0:T(8,128)(2,1)S(1)}, u32[]{:S(2)}, u32[]{:S(2)}) collective-permute-start(bf16[128,2048]{1,0:T(8,128)(2,1)S(1)} %get-tuple-element.26.high_ref), channel_id=1, source_target_pairs={{0,32},{32,0},{1,33},{33,1},{2,34},{34,2},{3,35},{35,3},{4,36},{36... | collective-permute-start | bytes 1572872 | tf_op jit(solution)/shard_map/ppermute | solution.py:345
  105.4 0.7 weight_own.1.part_ref
  106.1 0.8 collective-permute-done.2.spread_ref
  107.0 0.5 weight_all.1
  107.5 12.7 %all_to_all.47 = bf16[32,16,128]{2,1,0:T(8,128)(2,1)S(1)} all-to-all(bf16[32,16,128]{2,1,0:T(8,128)(2,1)S(1)} %weight_all.1), channel_id=1, replica_groups=mesh['y'=4,'core'=2,'z'=8,'x'=4] {'z','x'}, dimensions={0} | all-to-all | bytes 262144 | tf_op jit(solution)/shard_map/all_to_all | solution.py:333
  120.2 0.6 convert_reduce_fusion
  (24 shorter events, 0.1 us)
Async XLA Ops:
  0.6 6.5 %copy-start.7 = (s32[128,8]{0,1:T(8,128)S(1)}, s32[128,8]{0,1:T(8,128)}, u32[]{:S(2)}) copy-start(s32[128,8]{0,1:T(8,128)} %param.19) | copy-start | bytes 12292
  0.6 6.5 %copy-start.6 = (s32[128,8]{0,1:T(8,128)S(1)}, s32[128,8]{0,1:T(8,128)}, u32[]{:S(2)}) copy-start(s32[128,8]{0,1:T(8,128)} %param.18) | copy-start | bytes 12292
  2.6 6.2 %copy-start.8 = (s32[64]{0:T(128)S(1)}, s32[64]{0:T(128)}, u32[]{:S(2)}) copy-start(s32[64]{0:T(128)} %refs_0_.3) | copy-start | bytes 772
  2.7 6.2 %copy-start.9 = (s32[64]{0:T(128)S(1)}, s32[64]{0:T(128)}, u32[]{:S(2)}) copy-start(s32[64]{0:T(128)} %refs_1_.3) | copy-start | bytes 772
  3.1 5.7 %collective-permute-start.1 = (f32[1024,128]{1,0:T(8,128)S(1)}, f32[1024,128]{1,0:T(8,128)S(1)}, u32[]{:S(2)}, u32[]{:S(2)}) collective-permute-start(f32[1024,128]{1,0:T(8,128)S(1)} %project_rest.1.refs_6_), channel_id=1, source_target_pairs={{0,32},{32,0},{1,33},{33,1},{2,34},{34,2},{3,35},{35,3},{4,36},{36... | collective-permute-start | bytes 1572872 | tf_op jit(solution)/shard_map/ppermute | solution.py:345
  6.4 2.4 %collective-permute-start = (f32[1024,128]{1,0:T(8,128)S(1)}, f32[1024,128]{1,0:T(8,128)S(1)}, u32[]{:S(2)}, u32[]{:S(2)}) collective-permute-start(f32[1024,128]{1,0:T(8,128)S(1)} %get-tuple-element.17.refs_5_), channel_id=1, source_target_pairs={{0,32},{32,0},{1,33},{33,1},{2,34},{34,2},{3,35},{35,3},{4,36},{36... | collective-permute-start | bytes 1572872 | tf_op jit(solution)/shard_map/ppermute | solution.py:345
  10.5 41.4 %copy-start.1 = (bf16[128,512]{1,0:T(8,128)(2,1)S(1)}, bf16[128,512]{1,0:T(8,128)(2,1)}, u32[]{:S(2)}) copy-start(bf16[128,512]{1,0:T(8,128)(2,1)} %w_edge_ref.1) | copy-start | bytes 393220
  10.5 55.6 %copy-start.2 = (bf16[128,384]{1,0:T(8,128)(2,1)S(1)}, bf16[128,384]{1,0:T(8,128)(2,1)}, u32[]{:S(2)}) copy-start(bf16[128,384]{1,0:T(8,128)(2,1)} %w_in_ref.1) | copy-start | bytes 294916
  10.5 55.6 %copy-start.3 = (bf16[128,256]{1,0:T(8,128)(2,1)S(1)}, bf16[128,256]{1,0:T(8,128)(2,1)}, u32[]{:S(2)}) copy-start(bf16[128,256]{1,0:T(8,128)(2,1)} %w_state_ref.1) | copy-start | bytes 196612
  10.5 55.6 %copy-start.4 = (bf16[128,128]{1,0:T(8,128)(2,1)S(1)}, bf16[128,128]{1,0:T(8,128)(2,1)}, u32[]{:S(2)}) copy-start(bf16[128,128]{1,0:T(8,128)(2,1)} %grad_ref.1) | copy-start | bytes 98308
  10.5 55.6 %copy-start.5 = (bf16[128,128]{1,0:T(8,128)(2,1)S(1)}, bf16[128,128]{1,0:T(8,128)(2,1)}, u32[]{:S(2)}) copy-start(bf16[128,128]{1,0:T(8,128)(2,1)} %w_cand_ref.1) | copy-start | bytes 98308
  87.0 18.4 %copy-start = (bf16[2048,512]{1,0:T(8,128)(2,1)S(1)}, bf16[2048,512]{1,0:T(8,128)(2,1)}, u32[]{:S(2)}) copy-start(bf16[2048,512]{1,0:T(8,128)(2,1)} %feats_ref.3) | copy-start | bytes 6291460
  101.2 5.7 %collective-permute-start.2 = (bf16[128,2048]{1,0:T(8,128)(2,1)S(1)}, bf16[128,2048]{1,0:T(8,128)(2,1)S(1)}, u32[]{:S(2)}, u32[]{:S(2)}) collective-permute-start(bf16[128,2048]{1,0:T(8,128)(2,1)S(1)} %get-tuple-element.26.high_ref), channel_id=1, source_target_pairs={{0,32},{32,0},{1,33},{33,1},{2,34},{34,2},{3,35},{35,3},{4,36},{36... | collective-permute-start | bytes 1572872 | tf_op jit(solution)/shard_map/ppermute | solution.py:345

commit v7 on v6

--- a/solution.py
+++ b/solution.py
@@ -143,22 +143,25 @@
 ):
     copies = start_all([(adj_hbm, adj_ref)], sems)
     fanout, rows = nbr_ref.shape
-    cells = count_ref.shape[1]
+    cells = count_ref.shape[0]
+    types = count_ref.shape[1] // rows
     piece = block // cuts
     nbr = nbr_ref[...]
     within = nbr % block
     owner = nbr // block
-    local = ((owner % near) * far + owner // near) * piece + within % piece
-    per_type = cells // 4
-    key = jnp.where(within // piece == cut_index(), type_ref[...] * per_type + local, -1)
-    key = jnp.concatenate([key, jnp.zeros((rows - fanout, rows), jnp.int32)], axis=0).T
-    tile = 512
+    cut = within // piece
+    group = ((cut // 2) * near + owner % near) * far + owner // near
+    key = jnp.where(cut % 2 == lax.axis_index("core"), group * piece + within % piece, -1)
+    digit = jnp.left_shift(1, 4 * type_ref[...])
+    tile = 128
     for start in range(0, cells, tile):
-        place = lax.broadcasted_iota(jnp.int32, (rows, tile), 1) + start
-        total = jnp.zeros((rows, tile), F32)
+        place = lax.broadcasted_iota(jnp.int32, (tile, rows), 0) + start
+        total = jnp.zeros((tile, rows), jnp.int32)
         for k in range(fanout):
-            total += jnp.where(key[:, k : k + 1] == place, 1.0, 0.0)
-        count_ref[:, start : start + tile] = total.astype(BF16)
+            total += jnp.where(key[k : k + 1] == place, digit[k : k + 1], 0)
+        for e in range(types):
+            part = jnp.bitwise_and(jnp.right_shift(total, 4 * e), 15)
+            count_ref[start : start + tile, e * rows : (e + 1) * rows] = part.astype(F32).astype(BF16)
     copies[0].wait()
 
 
@@ -168,42 +171,53 @@
         out_ref[i] = total
 
 
-def state_kernel(part_ref, exact_ref, own_ref, out_ref):
+def state_kernel(part_ref, exact_ref, out_ref):
     total = jnp.sum(part_ref[...].astype(F32), axis=0)
     exact = jnp.tanh(total)
     exact_ref[...] = exact
     states = exact.astype(BF16)
     for i in range(out_ref.shape[0]):
         out_ref[i] = states
-    piece = own_ref.shape[0]
-    own_ref[...] = out_ref[0, pl.ds(pl.multiple_of(lax.axis_index("z") * piece, piece), piece), :]
-
-
-def message_kernel(count_ref, states_ref, own_ref, w_ref, out_ref):
-    hidden = own_ref.shape[1]
-    rows = count_ref.shape[0]
-    local = states_ref.shape[0] * states_ref.shape[1]
-    states = states_ref[...].reshape(local, hidden)
-    message = jnp.zeros((rows, hidden), F32)
-    for e in range(count_ref.shape[1] // local):
-        picked = dot(count_ref[:, e * local : (e + 1) * local], states).astype(BF16)
-        message += dot(picked, w_ref[:, e * hidden : (e + 1) * hidden])
-    message = message.astype(BF16)
-    for c in range(out_ref.shape[0]):
-        out_ref[c, :rows] = message
-        out_ref[c, rows:] = own_ref[...]
+
+
+def message_kernel(count_ref, states_ref, w_ref, out_ref):
+    planes, group, hidden = states_ref.shape
+    rows = out_ref.shape[0] * 2 // 3
+    near = lax.axis_size("x")
+    pairs = planes // near
+    piece = (out_ref.shape[0] - rows) // pairs
+    turned = jnp.concatenate([states_ref[i].T for i in range(planes)], axis=1)
+    picked = dot(turned, count_ref[...]).astype(BF16)
+    total = jnp.zeros((hidden, rows), F32)
+    for e in range(count_ref.shape[1] // rows):
+        total += dot(
+            w_ref[:, e * hidden : (e + 1) * hidden].T, picked[:, e * rows : (e + 1) * rows]
+        )
+    out_ref[:rows, :] = total
+    at = pl.ds(pl.multiple_of(lax.axis_index("z") * piece, piece), piece)
+    for y in range(pairs):
+        own = states_ref[y * near + lax.axis_index("x"), at, :]
+        out_ref[rows + y * piece : rows + (y + 1) * piece, :] = own.astype(F32)
 
 
 def gate_kernel(
-    recv_ref, count_ref, grad_ref, w_edge_ref, w_in_ref, w_state_ref, w_cand_ref,
-    new_ref, back_ref, own, spread,
+    mine_ref, other_ref, count_ref, grad_ref, w_edge_ref, w_in_ref, w_state_ref, w_cand_ref,
+    new_ref, back_ref, own, spread, state_rows,
 ):
     rows, hidden = grad_ref.shape
-    cuts = recv_ref.shape[0]
-    piece = recv_ref.shape[1] - rows
-    local = count_ref.shape[1] // 4
-    message = jnp.sum(recv_ref[:, :rows, :].astype(F32), axis=0)
-    states = recv_ref[:, rows:, :].reshape(cuts * piece, hidden)
+    near, group, _ = back_ref.shape
+    local = near * group
+    pairs = count_ref.shape[0] // local
+    piece = rows // (2 * pairs)
+    core = lax.axis_index("core")
+    message = (mine_ref[:rows, :] + other_ref[:rows, :]).T
+    for y in range(pairs):
+        source = slice(rows + y * piece, rows + (y + 1) * piece)
+        at = pl.ds(pl.multiple_of((2 * y + core) * piece, piece), piece)
+        state_rows[at, :] = mine_ref[source, :].astype(BF16)
+        at = pl.ds(pl.multiple_of((2 * y + 1 - core) * piece, piece), piece)
+        state_rows[at, :] = other_ref[source, :].astype(BF16)
+    states = state_rows[...]
     message_in = message.astype(BF16)
     w_in = w_in_ref[...]
     w_state = w_state_ref[...]
@@ -230,8 +244,12 @@
         + lax.dot_general(gates[:, : 2 * hidden], w_state, contract, preferred_element_type=F32)
     )
     total = jnp.zeros((hidden, local), F32)
-    for e in range(count_ref.shape[1] // local):
-        picked = dot(message_grad_t, count_ref[:, e * local : (e + 1) * local]).astype(BF16)
+    mine = pl.ds(pl.multiple_of(lax.axis_index("y") * local, local), local)
+    for e in range(count_ref.shape[1] // rows):
+        counts = count_ref[mine, e * rows : (e + 1) * rows]
+        picked = lax.dot_general(
+            message_grad_t, counts, contract, preferred_element_type=F32
+        ).astype(BF16)
         total += dot(w_edge_ref[:, e * hidden : (e + 1) * hidden], picked)
     spread[...] = total.T
     far = back_ref.shape[1] // piece
@@ -321,6 +339,7 @@
     nodes, feat_cols = feats.shape
     hidden = w_first.shape[1]
     rows = out_grad.shape[0]
+    types = w_edge.shape[1] // hidden
     far = lax.axis_size("z")
     near = lax.axis_size("x")
     pairs = lax.axis_size("y")
@@ -375,7 +394,7 @@
     counts, adj = pl.pallas_call(
         lambda *refs: count_kernel(*refs, cuts=cuts, block=block, near=near, far=far),
         out_shape=(
-            jax.ShapeDtypeStruct((rows, 4 * local), BF16),
+            jax.ShapeDtypeStruct((pairs * local, types * rows), BF16),
             jax.ShapeDtypeStruct(adjacency.shape, BF16),
         ),
         in_specs=[vspec(), vspec(), hspec()],
@@ -414,37 +433,37 @@
         )(x)
 
     by_far = over_far(fold(over_plane(partial)))
-    exact, own_states, tiled_states = pl.pallas_call(
+    exact, tiled_states = pl.pallas_call(
         state_kernel,
-        out_shape=(
-            jax.ShapeDtypeStruct((group, hidden), F32),
-            jax.ShapeDtypeStruct((piece, hidden), BF16),
-            tiled(near),
-        ),
+        out_shape=(jax.ShapeDtypeStruct((group, hidden), F32), tiled(pairs * near)),
         in_specs=[vspec()],
-        out_specs=(vspec(), vspec(), vspec()),
+        out_specs=(vspec(), vspec()),
         compiler_params=params(),
         name="state",
     )(by_far)
-    states = over_near(tiled_states)
-    sent = pl.pallas_call(
+    states = over_plane(tiled_states)
+    half_message = pl.pallas_call(
         message_kernel,
-        out_shape=jax.ShapeDtypeStruct((cuts, rows + piece, hidden), BF16),
-        in_specs=[vspec(), vspec(), vspec(), vspec()],
+        out_shape=jax.ShapeDtypeStruct((rows + rows // 2, hidden), F32),
+        in_specs=[vspec()] * 3,
         out_specs=vspec(),
         compiler_params=params(),
         name="message",
-    )(counts, states, own_states, w_edge)
-    recv = lax.all_to_all(sent, ("y", "core"), 0, 0, tiled=True)
+    )(counts, states, w_edge)
+    other_message = swap(half_message)
     new_rows, back = pl.pallas_call(
         gate_kernel,
         out_shape=(jax.ShapeDtypeStruct((rows, hidden), BF16), tiled(near)),
-        in_specs=[vspec()] * 7,
+        in_specs=[vspec()] * 8,
         out_specs=(vspec(), vspec()),
-        scratch_shapes=[VMEM((rows, hidden), F32), VMEM((local, hidden), F32)],
+        scratch_shapes=[
+            VMEM((rows, hidden), F32),
+            VMEM((local, hidden), F32),
+            VMEM((rows, hidden), BF16),
+        ],
         compiler_params=params(),
         name="gates",
-    )(recv, counts, out_grad, w_edge, w_gate_in, w_gate_state, w_cand)
+    )(half_message, other_message, counts, out_grad, w_edge, w_gate_in, w_gate_state, w_cand)
     grad_part = over_far(fold(over_near(back)))
     own_grad = pl.pallas_call(
         grad_kernel,

time: 121 us -> 117 us (0.967)
  blocking collectives: 99.2 us -> 90.5 us
  starting transfers between devices: 7.57 us -> 11.1 us
    all_to_all x1 -> x0, blocking collectives: 13.7 us -> none  [body(): recv = lax.all_to_all(sent, ('y', 'core'), 0, 0, tiled=True)]
    all_to_all x2 -> x3, blocking collectives: 27.8 us -> 41 us  [over_plane(): return lax.all_to_all(x, ('y', 'x'), 0, 0, tiled=True)]
    all_to_all x2 -> x1, blocking collectives: 15.5 us -> 7.23 us  [over_near(): return lax.all_to_all(x, 'x', 0, 0, tiled=True)]
    ppermute x3 -> x4, starting transfers between devices: 7.57 us -> 11.1 us  [swap(): return lax.ppermute(x, 'core', [(0, 1), (1, 0)])]
  transfers between devices with their start and end apart: 3 -> 4, of which waited for: 1 -> 2; matrix products, arithmetic and copies ran while one was open for 0% -> 0% of each run, Pallas kernels for 2% -> 2%
where the time goes in v7:
time: 117 us
  blocking collectives  90.5 us (77%)
  Pallas kernels  11.3 us (10%)
  starting transfers between devices  11.1 us (9%)
  waiting for transfers between devices  1.78 us (2%)
  between operations  1.48 us (1%)
    all_to_all x3, blocking collectives, over_plane(): return lax.all_to_all(x, ('y', 'x'), 0, 0, tiled=True)  41 us
    all_to_all x2, blocking collectives, over_far(): return lax.all_to_all(x, 'z', 0, 0, tiled=True)  29.8 us
    all_to_all x1, blocking collectives, over_dom(): return lax.all_to_all(x, ('z', 'x'), 0, 0, tiled=True)  12.4 us
    ppermute x4, starting transfers between devices, swap(): return lax.ppermute(x, 'core', [(0, 1), (1, 0)])  11.1 us
    all_to_all x1, blocking collectives, over_near(): return lax.all_to_all(x, 'x', 0, 0, tiled=True)  7.23 us
  transfers between devices with their start and end apart: 4, of which 2 were waited for; matrix products, arithmetic and copies ran while one was open for 0% of the time, Pallas kernels for 2%

profile of v7, /device:TPU:1, one launch (start us, length us, event | category | flops | bytes accessed | tf_op | source)
XLA Modules:
  0.0 116.8 jit_solution(5307163576328103382)
XLA Ops:
  0.7 2.0 %project.1 = (f32[1024,128]{1,0:T(8,128)S(1)}, bf16[1024,512]{1,0:T(8,128)(2,1)S(1)}, bf16[512,128]{1,0:T(8,128)(2,1)S(1)}) custom-call(bf16[2048,512]{1,0:T(8,128)(2,1)} %feats_ref.3, bf16[512,128]{1,0:T(8,128)(2,1)} %w_hbm.1), custom_call_target="tpu_custom_call" | custom-call | tf_op jit(solution)/shard_map/project/pallas_call | solution.py:368
  2.7 0.4 project_rest.1.refs_6_
  3.1 3.3 %collective-permute-start.1 = (f32[1024,128]{1,0:T(8,128)S(1)}, f32[1024,128]{1,0:T(8,128)S(1)}, u32[]{:S(2)}, u32[]{:S(2)}) collective-permute-start(f32[1024,128]{1,0:T(8,128)S(1)} %project_rest.1.refs_6_), channel_id=1, source_target_pairs={{0,32},{32,0},{1,33},{33,1},{2,34},{34,2},{3,35},{35,3},{4,36},{36... | collective-permute-start | bytes 1572872 | tf_op jit(solution)/shard_map/ppermute | solution.py:364
  6.4 0.1 collective-permute-start
  7.2 1.6 %counts.1 = (bf16[2048,512]{1,0:T(8,128)(2,1)S(1)}, bf16[64,128,128]{2,1,0:T(8,128)(2,1)S(1)}) custom-call(s32[8,128]{1,0:T(8,128)S(1)} %bitcast.2, s32[8,128]{1,0:T(8,128)S(1)} %bitcast.3, bf16[64,128,128]{2,1,0:T(8,128)(2,1)} %refs_2_.3), custom_call_target="tpu_custom_call" | custom-call | tf_op jit(solution)/shard_map/counts/pallas_call | solution.py:394
  8.8 1.6 %partial.1 = bf16[16,128,128]{2,1,0:T(8,128)(2,1)S(1)} custom-call(s32[64]{0:T(128)S(1)} %copy-done.8, s32[64]{0:T(128)S(1)} %copy-done.9, s32[1]{0:T(128)S(6)} %copy.15.refs_2_, bf16[2048,512]{1,0:T(8,128)(2,1)S(1)} %get-tuple-element.14.refs_3_.count_ref, bf16[64,128,128]{2,1,0:T(8,128)(2,1)S(1)} %get-tuple-element.15.refs_4_.refs_5_, ...), custom_call_target="tpu_custom_call" | custom-call | tf_op jit(solution)/shard_map/partial/pallas_call | solution.py:406
  10.5 15.6 %all_to_all.35.part_ref = bf16[16,128,128]{2,1,0:T(8,128)(2,1)S(1)} all-to-all(bf16[16,128,128]{2,1,0:T(8,128)(2,1)S(1)} %partial.1), channel_id=1, replica_groups=mesh['y'=4,'core'=2,'z'=8,'x'=4] {'y','x'}, dimensions={0} | all-to-all | bytes 1048576 | tf_op jit(solution)/shard_map/all_to_all | solution.py:355
  26.1 0.1 fold.2
  26.2 17.2 %all_to_all.36.part_ref = bf16[8,128,128]{2,1,0:T(8,128)(2,1)S(1)} all-to-all(bf16[8,128,128]{2,1,0:T(8,128)(2,1)S(1)} %fold.2), channel_id=1, replica_groups=mesh['y'=4,'core'=2,'z'=8,'x'=4] {'z'}, dimensions={0} | all-to-all | bytes 524288 | tf_op jit(solution)/shard_map/all_to_all | solution.py:361
  43.5 13.4 %all_to_all.37.states_ref = bf16[16,128,128]{2,1,0:T(8,128)(2,1)S(1)} all-to-all(bf16[16,128,128]{2,1,0:T(8,128)(2,1)S(1)} %get-tuple-element.19), channel_id=1, replica_groups=mesh['y'=4,'core'=2,'z'=8,'x'=4] {'y','x'}, dimensions={0} | all-to-all | bytes 1048576 | tf_op jit(solution)/shard_map/all_to_all | solution.py:355
  56.9 0.6 message.1.mine_ref
  57.6 4.1 %collective-permute-start.2 = (f32[192,128]{1,0:T(8,128)S(1)}, f32[192,128]{1,0:T(8,128)S(1)}, u32[]{:S(2)}, u32[]{:S(2)}) collective-permute-start(f32[192,128]{1,0:T(8,128)S(1)} %message.1.mine_ref), channel_id=1, source_target_pairs={{0,32},{32,0},{1,33},{33,1},{2,34},{34,2},{3,35},{35,3},{4,36},{36... | collective-permute-start | bytes 294920 | tf_op jit(solution)/shard_map/ppermute | solution.py:364
  61.7 0.9 collective-permute-done.2.other_ref
  62.7 1.6 %gates.1 = (bf16[128,128]{1,0:T(8,128)(2,1)S(1)}, bf16[4,128,128]{2,1,0:T(8,128)(2,1)S(1)}) custom-call(f32[192,128]{1,0:T(8,128)S(1)} %message.1.mine_ref, f32[192,128]{1,0:T(8,128)S(1)} %collective-permute-done.2.other_ref, bf16[2048,512]{1,0:T(8,128)(2,1)S(1)} %get-tuple-element.14.refs_3_.count_ref, bf16[128,128]{1,0:T(8,128)(2,1)S(1)} %copy-done.4, ...), custom_call_target="tpu_custom_call" | custom-call | tf_op jit(solution)/shard_map/gates/pallas_call | solution.py:454
  64.2 7.2 %all_to_all.38.part_ref = bf16[4,128,128]{2,1,0:T(8,128)(2,1)S(1)} all-to-all(bf16[4,128,128]{2,1,0:T(8,128)(2,1)S(1)} %get-tuple-element.21), channel_id=1, replica_groups=mesh['y'=4,'core'=2,'z'=8,'x'=4] {'x'}, dimensions={0} | all-to-all | bytes 262144 | tf_op jit(solution)/shard_map/all_to_all | solution.py:358
  71.5 12.6 %all_to_all.39.part_ref = bf16[8,128,128]{2,1,0:T(8,128)(2,1)S(1)} all-to-all(bf16[8,128,128]{2,1,0:T(8,128)(2,1)S(1)} %fold.3), channel_id=1, replica_groups=mesh['y'=4,'core'=2,'z'=8,'x'=4] {'z'}, dimensions={0} | all-to-all | bytes 524288 | tf_op jit(solution)/shard_map/all_to_all | solution.py:361
  84.2 12.0 %all_to_all.40.refs_4_ = bf16[16,128,128]{2,1,0:T(8,128)(2,1)S(1)} all-to-all(bf16[16,128,128]{2,1,0:T(8,128)(2,1)S(1)} %first_grad.1), channel_id=1, replica_groups=mesh['y'=4,'core'=2,'z'=8,'x'=4] {'y','x'}, dimensions={0} | all-to-all | bytes 1048576 | tf_op jit(solution)/shard_map/all_to_all | solution.py:355
  96.1 2.0 %spread.1 = (bf16[128,2048]{1,0:T(8,128)(2,1)S(1)}, bf16[128,2048]{1,0:T(8,128)(2,1)S(1)}, bf16[128,128]{1,0:T(8,128)(2,1)}) custom-call(s32[64]{0:T(128)S(1)} %copy-done.8, s32[64]{0:T(128)S(1)} %copy-done.9, s32[1]{0:T(128)S(6)} %copy.15.refs_2_, bf16[128,128]{1,0:T(8,128)(2,1)S(1)} %get-tuple-element.20.refs_3_, ...), custom_call_target="tpu_custom_call" | custom-call | tf_op jit(solution)/shard_map/spread/pallas_call | solution.py:477
  98.1 3.6 %collective-permute-start.3 = (bf16[128,2048]{1,0:T(8,128)(2,1)S(1)}, bf16[128,2048]{1,0:T(8,128)(2,1)S(1)}, u32[]{:S(2)}, u32[]{:S(2)}) collective-permute-start(bf16[128,2048]{1,0:T(8,128)(2,1)S(1)} %get-tuple-element.24.high_ref), channel_id=1, source_target_pairs={{0,32},{32,0},{1,33},{33,1},{2,34},{34,2},{3,35},{35,3},{4,36},{36... | collective-permute-start | bytes 1572872 | tf_op jit(solution)/shard_map/ppermute | solution.py:364
  101.7 0.7 weight_own.1.part_ref
  102.4 0.8 collective-permute-done.3.spread_ref
  103.3 0.5 weight_all.1
  103.8 12.4 %all_to_all.41 = bf16[32,16,128]{2,1,0:T(8,128)(2,1)S(1)} all-to-all(bf16[32,16,128]{2,1,0:T(8,128)(2,1)S(1)} %weight_all.1), channel_id=1, replica_groups=mesh['y'=4,'core'=2,'z'=8,'x'=4] {'z','x'}, dimensions={0} | all-to-all | bytes 262144 | tf_op jit(solution)/shard_map/all_to_all | solution.py:352
  116.2 0.6 convert_reduce_fusion
  (25 shorter events, 0.2 us)
Async XLA Ops:
  0.6 6.5 %copy-start.7 = (s32[128,8]{0,1:T(8,128)S(1)}, s32[128,8]{0,1:T(8,128)}, u32[]{:S(2)}) copy-start(s32[128,8]{0,1:T(8,128)} %param.19) | copy-start | bytes 12292
  0.6 6.5 %copy-start.6 = (s32[128,8]{0,1:T(8,128)S(1)}, s32[128,8]{0,1:T(8,128)}, u32[]{:S(2)}) copy-start(s32[128,8]{0,1:T(8,128)} %param.18) | copy-start | bytes 12292
  2.6 6.2 %copy-start.8 = (s32[64]{0:T(128)S(1)}, s32[64]{0:T(128)}, u32[]{:S(2)}) copy-start(s32[64]{0:T(128)} %refs_0_.3) | copy-start | bytes 772
  2.7 6.2 %copy-start.9 = (s32[64]{0:T(128)S(1)}, s32[64]{0:T(128)}, u32[]{:S(2)}) copy-start(s32[64]{0:T(128)} %refs_1_.3) | copy-start | bytes 772
  3.1 5.7 %collective-permute-start.1 = (f32[1024,128]{1,0:T(8,128)S(1)}, f32[1024,128]{1,0:T(8,128)S(1)}, u32[]{:S(2)}, u32[]{:S(2)}) collective-permute-start(f32[1024,128]{1,0:T(8,128)S(1)} %project_rest.1.refs_6_), channel_id=1, source_target_pairs={{0,32},{32,0},{1,33},{33,1},{2,34},{34,2},{3,35},{35,3},{4,36},{36... | collective-permute-start | bytes 1572872 | tf_op jit(solution)/shard_map/ppermute | solution.py:364
  6.4 2.4 %collective-permute-start = (f32[1024,128]{1,0:T(8,128)S(1)}, f32[1024,128]{1,0:T(8,128)S(1)}, u32[]{:S(2)}, u32[]{:S(2)}) collective-permute-start(f32[1024,128]{1,0:T(8,128)S(1)} %get-tuple-element.16.refs_5_), channel_id=1, source_target_pairs={{0,32},{32,0},{1,33},{33,1},{2,34},{34,2},{3,35},{35,3},{4,36},{36... | collective-permute-start | bytes 1572872 | tf_op jit(solution)/shard_map/ppermute | solution.py:364
  10.5 46.4 %copy-start.1 = (bf16[128,512]{1,0:T(8,128)(2,1)S(1)}, bf16[128,512]{1,0:T(8,128)(2,1)}, u32[]{:S(2)}) copy-start(bf16[128,512]{1,0:T(8,128)(2,1)} %w_edge_ref.1) | copy-start | bytes 393220
  43.4 19.2 %copy-start.2 = (bf16[128,384]{1,0:T(8,128)(2,1)S(1)}, bf16[128,384]{1,0:T(8,128)(2,1)}, u32[]{:S(2)}) copy-start(bf16[128,384]{1,0:T(8,128)(2,1)} %w_in_ref.1) | copy-start | bytes 294916
  43.4 19.2 %copy-start.3 = (bf16[128,256]{1,0:T(8,128)(2,1)S(1)}, bf16[128,256]{1,0:T(8,128)(2,1)}, u32[]{:S(2)}) copy-start(bf16[128,256]{1,0:T(8,128)(2,1)} %w_state_ref.1) | copy-start | bytes 196612
  43.4 19.2 %copy-start.4 = (bf16[128,128]{1,0:T(8,128)(2,1)S(1)}, bf16[128,128]{1,0:T(8,128)(2,1)}, u32[]{:S(2)}) copy-start(bf16[128,128]{1,0:T(8,128)(2,1)} %grad_ref.1) | copy-start | bytes 98308
  43.4 19.2 %copy-start.5 = (bf16[128,128]{1,0:T(8,128)(2,1)S(1)}, bf16[128,128]{1,0:T(8,128)(2,1)}, u32[]{:S(2)}) copy-start(bf16[128,128]{1,0:T(8,128)(2,1)} %w_cand_ref.1) | copy-start | bytes 98308
  57.6 5.1 %collective-permute-start.2 = (f32[192,128]{1,0:T(8,128)S(1)}, f32[192,128]{1,0:T(8,128)S(1)}, u32[]{:S(2)}, u32[]{:S(2)}) collective-permute-start(f32[192,128]{1,0:T(8,128)S(1)} %message.1.mine_ref), channel_id=1, source_target_pairs={{0,32},{32,0},{1,33},{33,1},{2,34},{34,2},{3,35},{35,3},{4,36},{36... | collective-permute-start | bytes 294920 | tf_op jit(solution)/shard_map/ppermute | solution.py:364
  84.1 17.6 %copy-start = (bf16[2048,512]{1,0:T(8,128)(2,1)S(1)}, bf16[2048,512]{1,0:T(8,128)(2,1)}, u32[]{:S(2)}) copy-start(bf16[2048,512]{1,0:T(8,128)(2,1)} %feats_ref.3) | copy-start | bytes 6291460
  98.1 5.1 %collective-permute-start.3 = (bf16[128,2048]{1,0:T(8,128)(2,1)S(1)}, bf16[128,2048]{1,0:T(8,128)(2,1)S(1)}, u32[]{:S(2)}, u32[]{:S(2)}) collective-permute-start(bf16[128,2048]{1,0:T(8,128)(2,1)S(1)} %get-tuple-element.24.high_ref), channel_id=1, source_target_pairs={{0,32},{32,0},{1,33},{33,1},{2,34},{34,2},{3,35},{35,3},{4,36},{36... | collective-permute-start | bytes 1572872 | tf_op jit(solution)/shard_map/ppermute | solution.py:364

commit v8 on v7

--- a/solution.py
+++ b/solution.py
@@ -49,36 +49,17 @@
     return jnp.dot(a, b, preferred_element_type=F32)
 
 
-def project_kernel(feats_hbm, w_hbm, out_ref, rest_ref, w_ref, feats, sems):
-    rows, rest = feats.shape[0], rest_ref.shape[0]
-    parts = 4
-    chunk, rest_chunk = rows // parts, rest // parts
+def project_kernel(feats_hbm, w_hbm, out_ref, feats, w, sems):
+    parts = sems.shape[0] - 1
+    chunk = feats.shape[0] // parts
+    places = [pl.ds(i * chunk, chunk) for i in range(parts)]
     copies = start_all(
-        [(w_hbm, w_ref)]
-        + [
-            (feats_hbm.at[pl.ds(i * chunk, chunk)], feats.at[pl.ds(i * chunk, chunk)])
-            for i in range(parts)
-        ]
-        + [
-            (
-                feats_hbm.at[pl.ds(rows + i * rest_chunk, rest_chunk)],
-                rest_ref.at[pl.ds(i * rest_chunk, rest_chunk)],
-            )
-            for i in range(parts)
-        ],
-        sems,
+        [(w_hbm, w)] + [(feats_hbm.at[at], feats.at[at]) for at in places], sems
     )
     copies[0].wait()
-    for i in range(parts):
-        copies[1 + i].wait()
-        at = pl.ds(i * chunk, chunk)
-        out_ref[at, :] = dot(feats[at, :], w_ref[...])
-    for copy in copies[1 + parts :]:
+    for copy, at in zip(copies[1:], places):
         copy.wait()
-
-
-def project_rest_kernel(rest_ref, w_ref, out_ref):
-    out_ref[...] = dot(rest_ref[...], w_ref[...])
+        out_ref[at, :] = dot(feats[at, :], w[...])
 
 
 def own_rows(adj, slot, core, piece):
@@ -118,7 +99,7 @@
         copy.wait()
     core = lax.axis_index("core")
     count = count_ref[0]
-    step = 32
+    step = 64
 
     def some_slots(group, carry):
         for j in range(step):
@@ -291,7 +272,7 @@
         copy.wait()
     core = lax.axis_index("core")
     count = count_ref[0]
-    step = 32
+    step = 64
 
     def some_slots(group, carry):
         for j in range(step):
@@ -363,34 +344,24 @@
     def swap(x):
         return lax.ppermute(x, "core", [(0, 1), (1, 0)])
 
-    first_rows = nodes // 2
-    rest_rows = nodes - first_rows
-    projected, rest, w = pl.pallas_call(
+    projected = pl.pallas_call(
         project_kernel,
-        out_shape=(
-            jax.ShapeDtypeStruct((first_rows, hidden), F32),
-            jax.ShapeDtypeStruct((rest_rows, feat_cols), BF16),
-            jax.ShapeDtypeStruct((feat_cols, hidden), BF16),
-        ),
+        out_shape=jax.ShapeDtypeStruct((nodes, hidden), F32),
         in_specs=[hspec()] * 2,
-        out_specs=(vspec(), vspec(), vspec()),
-        scratch_shapes=[VMEM((first_rows, feat_cols), BF16), pltpu.SemaphoreType.DMA((9,))],
+        out_specs=vspec(),
+        scratch_shapes=[
+            VMEM((nodes, feat_cols), BF16),
+            VMEM((feat_cols, hidden), BF16),
+            pltpu.SemaphoreType.DMA((9,)),
+        ],
         compiler_params=params(),
         name="project",
     )(
         pltpu.with_memory_space_constraint(feats, pltpu.HBM),
         pltpu.with_memory_space_constraint(w_first, pltpu.HBM),
     )
-    projected_rest = pl.pallas_call(
-        project_rest_kernel,
-        out_shape=jax.ShapeDtypeStruct((rest_rows, hidden), F32),
-        in_specs=[vspec(), vspec()],
-        out_specs=vspec(),
-        compiler_params=params(),
-        name="project_rest",
-    )(rest, w)
-    mine_parts = [projected, projected_rest]
-    swapped = [swap(p) for p in mine_parts]
+    mine_parts = [projected]
+    swapped = [swap(projected)]
     counts, adj = pl.pallas_call(
         lambda *refs: count_kernel(*refs, cuts=cuts, block=block, near=near, far=far),
         out_shape=(

time: 117 us -> 117 us (level)
    pallas_call x2 -> x1, Pallas kernels: 2.41 us -> 2.85 us  [body(): pl.pallas_call(project_kernel, out_shape=jax.ShapeDtypeStruct((nodes, hid...]
    ppermute x4 -> x3, starting transfers between devices: 11.1 us -> 11 us  [swap(): return lax.ppermute(x, 'core', [(0, 1), (1, 0)])]
  transfers between devices with their start and end apart: 4 -> 3, of which waited for: 2 -> 2; matrix products, arithmetic and copies ran while one was open for 0% -> 0% of each run, Pallas kernels for 2% -> 2%
where the time goes in v8:
time: 117 us
  blocking collectives  90.5 us (77%)
  Pallas kernels  11.5 us (10%)
  starting transfers between devices  11 us (9%)
  waiting for transfers between devices  1.78 us (2%)
  between operations  1.46 us (1%)
    all_to_all x3, blocking collectives, over_plane(): return lax.all_to_all(x, ('y', 'x'), 0, 0, tiled=True)  41.1 us
    all_to_all x2, blocking collectives, over_far(): return lax.all_to_all(x, 'z', 0, 0, tiled=True)  29.8 us
    all_to_all x1, blocking collectives, over_dom(): return lax.all_to_all(x, ('z', 'x'), 0, 0, tiled=True)  12.4 us
    ppermute x3, starting transfers between devices, swap(): return lax.ppermute(x, 'core', [(0, 1), (1, 0)])  11 us
    all_to_all x1, blocking collectives, over_near(): return lax.all_to_all(x, 'x', 0, 0, tiled=True)  7.23 us
    pallas_call x1, Pallas kernels, body(): pl.pallas_call(project_kernel, out_shape=jax.ShapeDtypeStruct((nodes, hid...  2.85 us
  transfers between devices with their start and end apart: 3, of which 2 were waited for; matrix products, arithmetic and copies ran while one was open for 0% of the time, Pallas kernels for 2%

profile of v8, /device:TPU:1, one launch (start us, length us, event | category | flops | bytes accessed | tf_op | source)
XLA Modules:
  0.0 116.9 jit_solution(6193079393002047947)
XLA Ops:
  0.7 2.8 %project.1.refs_5_ = f32[2048,128]{1,0:T(8,128)S(1)} custom-call(bf16[2048,512]{1,0:T(8,128)(2,1)} %feats_ref.3, bf16[512,128]{1,0:T(8,128)(2,1)} %w_hbm.1), custom_call_target="tpu_custom_call" | custom-call | tf_op jit(solution)/shard_map/project/pallas_call | solution.py:347
  3.5 3.2 %collective-permute-start = (f32[2048,128]{1,0:T(8,128)S(1)}, f32[2048,128]{1,0:T(8,128)S(1)}, u32[]{:S(2)}, u32[]{:S(2)}) collective-permute-start(f32[2048,128]{1,0:T(8,128)S(1)} %project.1.refs_5_), channel_id=1, source_target_pairs={{0,32},{32,0},{1,33},{33,1},{2,34},{34,2},{3,35},{35,3},{4,36},{36... | collective-permute-start | bytes 3145736 | tf_op jit(solution)/shard_map/ppermute | solution.py:345
  7.4 1.6 %counts.1 = (bf16[2048,512]{1,0:T(8,128)(2,1)S(1)}, bf16[64,128,128]{2,1,0:T(8,128)(2,1)S(1)}) custom-call(s32[8,128]{1,0:T(8,128)S(1)} %bitcast.2, s32[8,128]{1,0:T(8,128)S(1)} %bitcast.3, bf16[64,128,128]{2,1,0:T(8,128)(2,1)} %refs_2_.3), custom_call_target="tpu_custom_call" | custom-call | tf_op jit(solution)/shard_map/counts/pallas_call | solution.py:365
  9.1 1.5 %partial.1 = bf16[16,128,128]{2,1,0:T(8,128)(2,1)S(1)} custom-call(s32[64]{0:T(128)S(1)} %copy-done.8, s32[64]{0:T(128)S(1)} %copy-done.9, s32[1]{0:T(128)S(6)} %copy.15.refs_2_, bf16[2048,512]{1,0:T(8,128)(2,1)S(1)} %get-tuple-element.11.refs_3_.count_ref, bf16[64,128,128]{2,1,0:T(8,128)(2,1)S(1)} %get-tuple-element.12.refs_4_.refs_5_, ...), custom_call_target="tpu_custom_call" | custom-call | tf_op jit(solution)/shard_map/partial/pallas_call | solution.py:377
  10.6 15.8 %all_to_all.35.part_ref = bf16[16,128,128]{2,1,0:T(8,128)(2,1)S(1)} all-to-all(bf16[16,128,128]{2,1,0:T(8,128)(2,1)S(1)} %partial.1), channel_id=1, replica_groups=mesh['y'=4,'core'=2,'z'=8,'x'=4] {'y','x'}, dimensions={0} | all-to-all | bytes 1048576 | tf_op jit(solution)/shard_map/all_to_all | solution.py:336
  26.4 0.1 fold.2
  26.5 17.2 %all_to_all.36.part_ref = bf16[8,128,128]{2,1,0:T(8,128)(2,1)S(1)} all-to-all(bf16[8,128,128]{2,1,0:T(8,128)(2,1)S(1)} %fold.2), channel_id=1, replica_groups=mesh['y'=4,'core'=2,'z'=8,'x'=4] {'z'}, dimensions={0} | all-to-all | bytes 524288 | tf_op jit(solution)/shard_map/all_to_all | solution.py:342
  43.7 0.1 state.1
  43.8 13.3 %all_to_all.37.states_ref = bf16[16,128,128]{2,1,0:T(8,128)(2,1)S(1)} all-to-all(bf16[16,128,128]{2,1,0:T(8,128)(2,1)S(1)} %get-tuple-element.13), channel_id=1, replica_groups=mesh['y'=4,'core'=2,'z'=8,'x'=4] {'y','x'}, dimensions={0} | all-to-all | bytes 1048576 | tf_op jit(solution)/shard_map/all_to_all | solution.py:336
  57.1 0.6 message.1.mine_ref
  57.8 4.2 %collective-permute-start.1 = (f32[192,128]{1,0:T(8,128)S(1)}, f32[192,128]{1,0:T(8,128)S(1)}, u32[]{:S(2)}, u32[]{:S(2)}) collective-permute-start(f32[192,128]{1,0:T(8,128)S(1)} %message.1.mine_ref), channel_id=1, source_target_pairs={{0,32},{32,0},{1,33},{33,1},{2,34},{34,2},{3,35},{35,3},{4,36},{36... | collective-permute-start | bytes 294920 | tf_op jit(solution)/shard_map/ppermute | solution.py:345
  61.9 0.9 collective-permute-done.1.other_ref
  62.9 1.6 %gates.1 = (bf16[128,128]{1,0:T(8,128)(2,1)S(1)}, bf16[4,128,128]{2,1,0:T(8,128)(2,1)S(1)}) custom-call(f32[192,128]{1,0:T(8,128)S(1)} %message.1.mine_ref, f32[192,128]{1,0:T(8,128)S(1)} %collective-permute-done.1.other_ref, bf16[2048,512]{1,0:T(8,128)(2,1)S(1)} %get-tuple-element.11.refs_3_.count_ref, bf16[128,128]{1,0:T(8,128)(2,1)S(1)} %copy-done.4, ...), custom_call_target="tpu_custom_call" | custom-call | tf_op jit(solution)/shard_map/gates/pallas_call | solution.py:425
  64.5 7.2 %all_to_all.38.part_ref = bf16[4,128,128]{2,1,0:T(8,128)(2,1)S(1)} all-to-all(bf16[4,128,128]{2,1,0:T(8,128)(2,1)S(1)} %get-tuple-element.15), channel_id=1, replica_groups=mesh['y'=4,'core'=2,'z'=8,'x'=4] {'x'}, dimensions={0} | all-to-all | bytes 262144 | tf_op jit(solution)/shard_map/all_to_all | solution.py:339
  71.7 12.6 %all_to_all.39.part_ref = bf16[8,128,128]{2,1,0:T(8,128)(2,1)S(1)} all-to-all(bf16[8,128,128]{2,1,0:T(8,128)(2,1)S(1)} %fold.3), channel_id=1, replica_groups=mesh['y'=4,'core'=2,'z'=8,'x'=4] {'z'}, dimensions={0} | all-to-all | bytes 524288 | tf_op jit(solution)/shard_map/all_to_all | solution.py:342
  84.4 0.1 first_grad.1
  84.4 12.0 %all_to_all.40.refs_4_ = bf16[16,128,128]{2,1,0:T(8,128)(2,1)S(1)} all-to-all(bf16[16,128,128]{2,1,0:T(8,128)(2,1)S(1)} %first_grad.1), channel_id=1, replica_groups=mesh['y'=4,'core'=2,'z'=8,'x'=4] {'y','x'}, dimensions={0} | all-to-all | bytes 1048576 | tf_op jit(solution)/shard_map/all_to_all | solution.py:336
  96.4 1.9 %spread.1 = (bf16[128,2048]{1,0:T(8,128)(2,1)S(1)}, bf16[128,2048]{1,0:T(8,128)(2,1)S(1)}, bf16[128,128]{1,0:T(8,128)(2,1)}) custom-call(s32[64]{0:T(128)S(1)} %copy-done.8, s32[64]{0:T(128)S(1)} %copy-done.9, s32[1]{0:T(128)S(6)} %copy.15.refs_2_, bf16[128,128]{1,0:T(8,128)(2,1)S(1)} %get-tuple-element.14.refs_3_, ...), custom_call_target="tpu_custom_call" | custom-call | tf_op jit(solution)/shard_map/spread/pallas_call | solution.py:448
  98.3 3.6 %collective-permute-start.2 = (bf16[128,2048]{1,0:T(8,128)(2,1)S(1)}, bf16[128,2048]{1,0:T(8,128)(2,1)S(1)}, u32[]{:S(2)}, u32[]{:S(2)}) collective-permute-start(bf16[128,2048]{1,0:T(8,128)(2,1)S(1)} %get-tuple-element.18.high_ref), channel_id=1, source_target_pairs={{0,32},{32,0},{1,33},{33,1},{2,34},{34,2},{3,35},{35,3},{4,36},{36... | collective-permute-start | bytes 1572872 | tf_op jit(solution)/shard_map/ppermute | solution.py:345
  101.8 0.7 weight_own.1.part_ref
  102.5 0.8 collective-permute-done.2.spread_ref
  103.4 0.5 weight_all.1
  103.9 12.4 %all_to_all.41 = bf16[32,16,128]{2,1,0:T(8,128)(2,1)S(1)} all-to-all(bf16[32,16,128]{2,1,0:T(8,128)(2,1)S(1)} %weight_all.1), channel_id=1, replica_groups=mesh['y'=4,'core'=2,'z'=8,'x'=4] {'z','x'}, dimensions={0} | all-to-all | bytes 262144 | tf_op jit(solution)/shard_map/all_to_all | solution.py:333
  116.3 0.6 convert_reduce_fusion
  (22 shorter events, 0.1 us)
Async XLA Ops:
  0.6 6.8 %copy-start.7 = (s32[128,8]{0,1:T(8,128)S(1)}, s32[128,8]{0,1:T(8,128)}, u32[]{:S(2)}) copy-start(s32[128,8]{0,1:T(8,128)} %param.19) | copy-start | bytes 12292
  0.6 6.8 %copy-start.6 = (s32[128,8]{0,1:T(8,128)S(1)}, s32[128,8]{0,1:T(8,128)}, u32[]{:S(2)}) copy-start(s32[128,8]{0,1:T(8,128)} %param.18) | copy-start | bytes 12292
  0.7 8.4 %copy-start.9 = (s32[64]{0:T(128)S(1)}, s32[64]{0:T(128)}, u32[]{:S(2)}) copy-start(s32[64]{0:T(128)} %refs_1_.3) | copy-start | bytes 772
  0.7 8.4 %copy-start.8 = (s32[64]{0:T(128)S(1)}, s32[64]{0:T(128)}, u32[]{:S(2)}) copy-start(s32[64]{0:T(128)} %refs_0_.3) | copy-start | bytes 772
  3.5 5.5 %collective-permute-start = (f32[2048,128]{1,0:T(8,128)S(1)}, f32[2048,128]{1,0:T(8,128)S(1)}, u32[]{:S(2)}, u32[]{:S(2)}) collective-permute-start(f32[2048,128]{1,0:T(8,128)S(1)} %project.1.refs_5_), channel_id=1, source_target_pairs={{0,32},{32,0},{1,33},{33,1},{2,34},{34,2},{3,35},{35,3},{4,36},{36... | collective-permute-start | bytes 3145736 | tf_op jit(solution)/shard_map/ppermute | solution.py:345
  10.6 46.5 %copy-start.1 = (bf16[128,512]{1,0:T(8,128)(2,1)S(1)}, bf16[128,512]{1,0:T(8,128)(2,1)}, u32[]{:S(2)}) copy-start(bf16[128,512]{1,0:T(8,128)(2,1)} %w_edge_ref.1) | copy-start | bytes 393220
  43.7 19.2 %copy-start.2 = (bf16[128,384]{1,0:T(8,128)(2,1)S(1)}, bf16[128,384]{1,0:T(8,128)(2,1)}, u32[]{:S(2)}) copy-start(bf16[128,384]{1,0:T(8,128)(2,1)} %w_in_ref.1) | copy-start | bytes 294916
  43.7 19.2 %copy-start.3 = (bf16[128,256]{1,0:T(8,128)(2,1)S(1)}, bf16[128,256]{1,0:T(8,128)(2,1)}, u32[]{:S(2)}) copy-start(bf16[128,256]{1,0:T(8,128)(2,1)} %w_state_ref.1) | copy-start | bytes 196612
  43.7 19.2 %copy-start.4 = (bf16[128,128]{1,0:T(8,128)(2,1)S(1)}, bf16[128,128]{1,0:T(8,128)(2,1)}, u32[]{:S(2)}) copy-start(bf16[128,128]{1,0:T(8,128)(2,1)} %grad_ref.1) | copy-start | bytes 98308
  43.7 19.2 %copy-start.5 = (bf16[128,128]{1,0:T(8,128)(2,1)S(1)}, bf16[128,128]{1,0:T(8,128)(2,1)}, u32[]{:S(2)}) copy-start(bf16[128,128]{1,0:T(8,128)(2,1)} %w_cand_ref.1) | copy-start | bytes 98308
  57.8 5.1 %collective-permute-start.1 = (f32[192,128]{1,0:T(8,128)S(1)}, f32[192,128]{1,0:T(8,128)S(1)}, u32[]{:S(2)}, u32[]{:S(2)}) collective-permute-start(f32[192,128]{1,0:T(8,128)S(1)} %message.1.mine_ref), channel_id=1, source_target_pairs={{0,32},{32,0},{1,33},{33,1},{2,34},{34,2},{3,35},{35,3},{4,36},{36... | collective-permute-start | bytes 294920 | tf_op jit(solution)/shard_map/ppermute | solution.py:345
  84.3 17.5 %copy-start = (bf16[2048,512]{1,0:T(8,128)(2,1)S(1)}, bf16[2048,512]{1,0:T(8,128)(2,1)}, u32[]{:S(2)}) copy-start(bf16[2048,512]{1,0:T(8,128)(2,1)} %feats_ref.3) | copy-start | bytes 6291460
  98.3 5.1 %collective-permute-start.2 = (bf16[128,2048]{1,0:T(8,128)(2,1)S(1)}, bf16[128,2048]{1,0:T(8,128)(2,1)S(1)}, u32[]{:S(2)}, u32[]{:S(2)}) collective-permute-start(bf16[128,2048]{1,0:T(8,128)(2,1)S(1)} %get-tuple-element.18.high_ref), channel_id=1, source_target_pairs={{0,32},{32,0},{1,33},{33,1},{2,34},{34,2},{3,35},{35,3},{4,36},{36... | collective-permute-start | bytes 1572872 | tf_op jit(solution)/shard_map/ppermute | solution.py:345

commit v9 on v7

--- a/solution.py
+++ b/solution.py
@@ -5,6 +5,7 @@
 from jax.experimental.pallas import tpu as pltpu
 from jax.sharding import PartitionSpec as P
 
+
 F32 = jnp.float32
 BF16 = jnp.bfloat16
 VMEM = pltpu.VMEM
@@ -13,10 +14,6 @@
 
 def vspec():
     return pl.BlockSpec(memory_space=pltpu.VMEM)
-
-
-def sspec():
-    return pl.BlockSpec(memory_space=pltpu.SMEM)
 
 
 def hspec():
@@ -118,7 +115,7 @@
         copy.wait()
     core = lax.axis_index("core")
     count = count_ref[0]
-    step = 32
+    step = 64
 
     def some_slots(group, carry):
         for j in range(step):
@@ -139,9 +136,8 @@
 
 
 def count_kernel(
-    nbr_ref, type_ref, adj_hbm, count_ref, adj_ref, sems, *, cuts, block, near, far
+    nbr_ref, type_ref, count_ref, *, cuts, block, near, far
 ):
-    copies = start_all([(adj_hbm, adj_ref)], sems)
     fanout, rows = nbr_ref.shape
     cells = count_ref.shape[0]
     types = count_ref.shape[1] // rows
@@ -162,7 +158,6 @@
         for e in range(types):
             part = jnp.bitwise_and(jnp.right_shift(total, 4 * e), 15)
             count_ref[start : start + tile, e * rows : (e + 1) * rows] = part.astype(F32).astype(BF16)
-    copies[0].wait()
 
 
 def fold_kernel(part_ref, out_ref):
@@ -181,7 +176,7 @@
 
 
 def message_kernel(count_ref, states_ref, w_ref, out_ref):
-    planes, group, hidden = states_ref.shape
+    planes, _, hidden = states_ref.shape
     rows = out_ref.shape[0] * 2 // 3
     near = lax.axis_size("x")
     pairs = planes // near
@@ -273,7 +268,6 @@
     turned, acc, dst_ref, src_ref, count_ref, sems, *, near, far,
 ):
     slots, block, _ = adj.shape
-    hidden = grads_ref.shape[2]
     piece = grads_ref.shape[1] // far
     pairs = grads_ref.shape[0] // near
     copies = start_all(
@@ -291,7 +285,7 @@
         copy.wait()
     core = lax.axis_index("core")
     count = count_ref[0]
-    step = 32
+    step = 64
 
     def some_slots(group, carry):
         for j in range(step):
@@ -390,19 +384,17 @@
         name="project_rest",
     )(rest, w)
     mine_parts = [projected, projected_rest]
-    swapped = [swap(p) for p in mine_parts]
-    counts, adj = pl.pallas_call(
+    swapped = []
+    for part in mine_parts:
+        swapped.append(swap(part))
+    counts = pl.pallas_call(
         lambda *refs: count_kernel(*refs, cuts=cuts, block=block, near=near, far=far),
-        out_shape=(
-            jax.ShapeDtypeStruct((pairs * local, types * rows), BF16),
-            jax.ShapeDtypeStruct(adjacency.shape, BF16),
-        ),
-        in_specs=[vspec(), vspec(), hspec()],
-        out_specs=(vspec(), vspec()),
-        scratch_shapes=[pltpu.SemaphoreType.DMA((1,))],
+        out_shape=jax.ShapeDtypeStruct((pairs * local, types * rows), BF16),
+        in_specs=[vspec(), vspec()],
+        out_specs=vspec(),
         compiler_params=params(),
         name="counts",
-    )(nbr_ids.T, edge_types.T, pltpu.with_memory_space_constraint(adjacency, pltpu.HBM))
+    )(nbr_ids.T, edge_types.T)
     partial = pl.pallas_call(
         lambda *refs: partial_kernel(*refs, near=near, far=far),
         out_shape=jax.ShapeDtypeStruct((pairs * near, far * piece, hidden), BF16),
@@ -418,7 +410,7 @@
         ],
         compiler_params=params(),
         name="partial",
-    )(blk_dst, blk_src, blk_count, counts, adj, *mine_parts, *swapped)
+    )(blk_dst, blk_src, blk_count, counts, adjacency, *mine_parts, *swapped)
     group = far * piece
     tiled = lambda n: jax.ShapeDtypeStruct((n, group, hidden), BF16)
 
@@ -493,7 +485,7 @@
         ],
         compiler_params=params(),
         name="spread",
-    )(blk_dst, blk_src, blk_count, new_rows, grads, adj)
+    )(blk_dst, blk_src, blk_count, new_rows, grads, adjacency)
     other = swap(mine)
     own_part = pl.pallas_call(
         weight_kernel,
@@ -522,6 +514,7 @@
     )
     dom = ("z", "x")
     cut = ("y", "core")
+
     return jax.shard_map(
         body,
         mesh=fine,

time: 117 us -> 117 us (level)
  transfers between devices with their start and end apart: 4 -> 4, of which waited for: 2 -> 3; matrix products, arithmetic and copies ran while one was open for 0% -> 0% of each run, Pallas kernels for 2% -> 2%
where the time goes in v9:
time: 117 us
  blocking collectives  90.5 us (77%)
  starting transfers between devices  11.1 us (9%)
  Pallas kernels  10.9 us (9%)
  waiting for transfers between devices  1.86 us (2%)
  between operations  1.46 us (1%)
    all_to_all x3, blocking collectives, over_plane(): return lax.all_to_all(x, ('y', 'x'), 0, 0, tiled=True)  41.1 us
    all_to_all x2, blocking collectives, over_far(): return lax.all_to_all(x, 'z', 0, 0, tiled=True)  29.8 us
    all_to_all x1, blocking collectives, over_dom(): return lax.all_to_all(x, ('z', 'x'), 0, 0, tiled=True)  12.4 us
    ppermute x4, starting transfers between devices, swap(): return lax.ppermute(x, 'core', [(0, 1), (1, 0)])  11.1 us
    all_to_all x1, blocking collectives, over_near(): return lax.all_to_all(x, 'x', 0, 0, tiled=True)  7.23 us
  transfers between devices with their start and end apart: 4, of which 3 were waited for; matrix products, arithmetic and copies ran while one was open for 0% of the time, Pallas kernels for 2%

profile of v9, /device:TPU:1, one launch (start us, length us, event | category | flops | bytes accessed | tf_op | source)
XLA Modules:
  0.0 116.5 jit_solution(16099370112116087937)
XLA Ops:
  0.7 2.0 %project.1 = (f32[1024,128]{1,0:T(8,128)S(1)}, bf16[1024,512]{1,0:T(8,128)(2,1)S(1)}, bf16[512,128]{1,0:T(8,128)(2,1)S(1)}) custom-call(bf16[2048,512]{1,0:T(8,128)(2,1)} %feats_ref.3, bf16[512,128]{1,0:T(8,128)(2,1)} %w_hbm.1), custom_call_target="tpu_custom_call" | custom-call | tf_op jit(solution)/shard_map/project/pallas_call | solution.py:362
  2.7 0.4 project_rest.1.refs_6_
  3.1 3.3 %collective-permute-start.1 = (f32[1024,128]{1,0:T(8,128)S(1)}, f32[1024,128]{1,0:T(8,128)S(1)}, u32[]{:S(2)}, u32[]{:S(2)}) collective-permute-start(f32[1024,128]{1,0:T(8,128)S(1)} %project_rest.1.refs_6_), channel_id=1, source_target_pairs={{0,32},{32,0},{1,33},{33,1},{2,34},{34,2},{3,35},{35,3},{4,36},{36... | collective-permute-start | bytes 1572872 | tf_op jit(solution)/shard_map/ppermute | solution.py:358
  6.4 0.1 collective-permute-start
  7.2 1.4 %counts.1.refs_3_.count_ref = bf16[2048,512]{1,0:T(8,128)(2,1)S(1)} custom-call(s32[8,128]{1,0:T(8,128)S(1)} %bitcast.2, s32[8,128]{1,0:T(8,128)S(1)} %bitcast.3), custom_call_target="tpu_custom_call" | custom-call | tf_op jit(solution)/shard_map/counts/pallas_call | solution.py:390
  8.6 0.1 collective-permute-done.refs_7_
  8.7 1.6 %partial.1 = bf16[16,128,128]{2,1,0:T(8,128)(2,1)S(1)} custom-call(s32[64]{0:T(128)S(1)} %copy-done.9, s32[64]{0:T(128)S(1)} %copy-done.10, s32[1]{0:T(128)S(6)} %copy.15.refs_2_, bf16[2048,512]{1,0:T(8,128)(2,1)S(1)} %counts.1.refs_3_.count_ref, bf16[64,128,128]{2,1,0:T(8,128)(2,1)S(1)} %copy-done.1, f32[1024,128]{1,0:T(8,128)S(1)} %get-tuple-element.12.refs_5_, ...), custom_call_target="tpu_custom_call" | custom-call | tf_op jit(solution)/shard_map/partial/pallas_call | solution.py:398
  10.3 15.7 %all_to_all.35.part_ref = bf16[16,128,128]{2,1,0:T(8,128)(2,1)S(1)} all-to-all(bf16[16,128,128]{2,1,0:T(8,128)(2,1)S(1)} %partial.1), channel_id=1, replica_groups=mesh['y'=4,'core'=2,'z'=8,'x'=4] {'y','x'}, dimensions={0} | all-to-all | bytes 1048576 | tf_op jit(solution)/shard_map/all_to_all | solution.py:349
  26.0 17.2 %all_to_all.36.part_ref = bf16[8,128,128]{2,1,0:T(8,128)(2,1)S(1)} all-to-all(bf16[8,128,128]{2,1,0:T(8,128)(2,1)S(1)} %fold.2), channel_id=1, replica_groups=mesh['y'=4,'core'=2,'z'=8,'x'=4] {'z'}, dimensions={0} | all-to-all | bytes 524288 | tf_op jit(solution)/shard_map/all_to_all | solution.py:355
  43.3 13.4 %all_to_all.37.states_ref = bf16[16,128,128]{2,1,0:T(8,128)(2,1)S(1)} all-to-all(bf16[16,128,128]{2,1,0:T(8,128)(2,1)S(1)} %get-tuple-element.15), channel_id=1, replica_groups=mesh['y'=4,'core'=2,'z'=8,'x'=4] {'y','x'}, dimensions={0} | all-to-all | bytes 1048576 | tf_op jit(solution)/shard_map/all_to_all | solution.py:349
  56.7 0.6 message.1.mine_ref
  57.4 4.1 %collective-permute-start.2 = (f32[192,128]{1,0:T(8,128)S(1)}, f32[192,128]{1,0:T(8,128)S(1)}, u32[]{:S(2)}, u32[]{:S(2)}) collective-permute-start(f32[192,128]{1,0:T(8,128)S(1)} %message.1.mine_ref), channel_id=1, source_target_pairs={{0,32},{32,0},{1,33},{33,1},{2,34},{34,2},{3,35},{35,3},{4,36},{36... | collective-permute-start | bytes 294920 | tf_op jit(solution)/shard_map/ppermute | solution.py:358
  61.5 0.9 collective-permute-done.2.other_ref
  62.5 1.6 %gates.1 = (bf16[128,128]{1,0:T(8,128)(2,1)S(1)}, bf16[4,128,128]{2,1,0:T(8,128)(2,1)S(1)}) custom-call(f32[192,128]{1,0:T(8,128)S(1)} %message.1.mine_ref, f32[192,128]{1,0:T(8,128)S(1)} %collective-permute-done.2.other_ref, bf16[2048,512]{1,0:T(8,128)(2,1)S(1)} %counts.1.refs_3_.count_ref, bf16[128,128]{1,0:T(8,128)(2,1)S(1)} %copy-done.5, ...), custom_call_target="tpu_custom_call" | custom-call | tf_op jit(solution)/shard_map/gates/pallas_call | solution.py:446
  64.0 7.2 %all_to_all.38.part_ref = bf16[4,128,128]{2,1,0:T(8,128)(2,1)S(1)} all-to-all(bf16[4,128,128]{2,1,0:T(8,128)(2,1)S(1)} %get-tuple-element.17), channel_id=1, replica_groups=mesh['y'=4,'core'=2,'z'=8,'x'=4] {'x'}, dimensions={0} | all-to-all | bytes 262144 | tf_op jit(solution)/shard_map/all_to_all | solution.py:352
  71.3 12.6 %all_to_all.39.part_ref = bf16[8,128,128]{2,1,0:T(8,128)(2,1)S(1)} all-to-all(bf16[8,128,128]{2,1,0:T(8,128)(2,1)S(1)} %fold.3), channel_id=1, replica_groups=mesh['y'=4,'core'=2,'z'=8,'x'=4] {'z'}, dimensions={0} | all-to-all | bytes 524288 | tf_op jit(solution)/shard_map/all_to_all | solution.py:355
  84.0 12.0 %all_to_all.40.refs_4_ = bf16[16,128,128]{2,1,0:T(8,128)(2,1)S(1)} all-to-all(bf16[16,128,128]{2,1,0:T(8,128)(2,1)S(1)} %first_grad.1), channel_id=1, replica_groups=mesh['y'=4,'core'=2,'z'=8,'x'=4] {'y','x'}, dimensions={0} | all-to-all | bytes 1048576 | tf_op jit(solution)/shard_map/all_to_all | solution.py:349
  95.9 1.9 %spread.1 = (bf16[128,2048]{1,0:T(8,128)(2,1)S(1)}, bf16[128,2048]{1,0:T(8,128)(2,1)S(1)}, bf16[128,128]{1,0:T(8,128)(2,1)}) custom-call(s32[64]{0:T(128)S(1)} %copy-done.9, s32[64]{0:T(128)S(1)} %copy-done.10, s32[1]{0:T(128)S(6)} %copy.15.refs_2_, bf16[128,128]{1,0:T(8,128)(2,1)S(1)} %get-tuple-element.16.refs_3_, ...), custom_call_target="tpu_custom_call" | custom-call | tf_op jit(solution)/shard_map/spread/pallas_call | solution.py:469
  97.8 3.6 %collective-permute-start.3 = (bf16[128,2048]{1,0:T(8,128)(2,1)S(1)}, bf16[128,2048]{1,0:T(8,128)(2,1)S(1)}, u32[]{:S(2)}, u32[]{:S(2)}) collective-permute-start(bf16[128,2048]{1,0:T(8,128)(2,1)S(1)} %get-tuple-element.20.high_ref), channel_id=1, source_target_pairs={{0,32},{32,0},{1,33},{33,1},{2,34},{34,2},{3,35},{35,3},{4,36},{36... | collective-permute-start | bytes 1572872 | tf_op jit(solution)/shard_map/ppermute | solution.py:358
  101.4 0.7 weight_own.1.part_ref
  102.1 0.8 collective-permute-done.3.spread_ref
  102.9 0.5 weight_all.1
  103.5 12.4 %all_to_all.41 = bf16[32,16,128]{2,1,0:T(8,128)(2,1)S(1)} all-to-all(bf16[32,16,128]{2,1,0:T(8,128)(2,1)S(1)} %weight_all.1), channel_id=1, replica_groups=mesh['y'=4,'core'=2,'z'=8,'x'=4] {'z','x'}, dimensions={0} | all-to-all | bytes 262144 | tf_op jit(solution)/shard_map/all_to_all | solution.py:346
  115.9 0.6 convert_reduce_fusion
  (27 shorter events, 0.3 us)
Async XLA Ops:
  0.6 6.5 %copy-start.8 = (s32[128,8]{0,1:T(8,128)S(1)}, s32[128,8]{0,1:T(8,128)}, u32[]{:S(2)}) copy-start(s32[128,8]{0,1:T(8,128)} %param.19) | copy-start | bytes 12292
  0.6 6.5 %copy-start.7 = (s32[128,8]{0,1:T(8,128)S(1)}, s32[128,8]{0,1:T(8,128)}, u32[]{:S(2)}) copy-start(s32[128,8]{0,1:T(8,128)} %param.18) | copy-start | bytes 12292
  2.6 6.0 %copy-start.1 = (bf16[64,128,128]{2,1,0:T(8,128)(2,1)S(1)}, bf16[64,128,128]{2,1,0:T(8,128)(2,1)}, u32[]{:S(2)}) copy-start(bf16[64,128,128]{2,1,0:T(8,128)(2,1)} %refs_5_.1) | copy-start | bytes 6291460
  2.7 6.0 %copy-start.9 = (s32[64]{0:T(128)S(1)}, s32[64]{0:T(128)}, u32[]{:S(2)}) copy-start(s32[64]{0:T(128)} %refs_0_.3) | copy-start | bytes 772
  2.7 6.0 %copy-start.10 = (s32[64]{0:T(128)S(1)}, s32[64]{0:T(128)}, u32[]{:S(2)}) copy-start(s32[64]{0:T(128)} %refs_1_.3) | copy-start | bytes 772
  3.1 5.5 %collective-permute-start.1 = (f32[1024,128]{1,0:T(8,128)S(1)}, f32[1024,128]{1,0:T(8,128)S(1)}, u32[]{:S(2)}, u32[]{:S(2)}) collective-permute-start(f32[1024,128]{1,0:T(8,128)S(1)} %project_rest.1.refs_6_), channel_id=1, source_target_pairs={{0,32},{32,0},{1,33},{33,1},{2,34},{34,2},{3,35},{35,3},{4,36},{36... | collective-permute-start | bytes 1572872 | tf_op jit(solution)/shard_map/ppermute | solution.py:358
  6.4 2.3 %collective-permute-start = (f32[1024,128]{1,0:T(8,128)S(1)}, f32[1024,128]{1,0:T(8,128)S(1)}, u32[]{:S(2)}, u32[]{:S(2)}) collective-permute-start(f32[1024,128]{1,0:T(8,128)S(1)} %get-tuple-element.12.refs_5_), channel_id=1, source_target_pairs={{0,32},{32,0},{1,33},{33,1},{2,34},{34,2},{3,35},{35,3},{4,36},{36... | collective-permute-start | bytes 1572872 | tf_op jit(solution)/shard_map/ppermute | solution.py:358
  10.3 46.5 %copy-start.2 = (bf16[128,512]{1,0:T(8,128)(2,1)S(1)}, bf16[128,512]{1,0:T(8,128)(2,1)}, u32[]{:S(2)}) copy-start(bf16[128,512]{1,0:T(8,128)(2,1)} %w_edge_ref.1) | copy-start | bytes 393220
  43.2 19.2 %copy-start.3 = (bf16[128,384]{1,0:T(8,128)(2,1)S(1)}, bf16[128,384]{1,0:T(8,128)(2,1)}, u32[]{:S(2)}) copy-start(bf16[128,384]{1,0:T(8,128)(2,1)} %w_in_ref.1) | copy-start | bytes 294916
  43.2 19.2 %copy-start.4 = (bf16[128,256]{1,0:T(8,128)(2,1)S(1)}, bf16[128,256]{1,0:T(8,128)(2,1)}, u32[]{:S(2)}) copy-start(bf16[128,256]{1,0:T(8,128)(2,1)} %w_state_ref.1) | copy-start | bytes 196612
  43.2 19.2 %copy-start.5 = (bf16[128,128]{1,0:T(8,128)(2,1)S(1)}, bf16[128,128]{1,0:T(8,128)(2,1)}, u32[]{:S(2)}) copy-start(bf16[128,128]{1,0:T(8,128)(2,1)} %grad_ref.1) | copy-start | bytes 98308
  43.2 19.2 %copy-start.6 = (bf16[128,128]{1,0:T(8,128)(2,1)S(1)}, bf16[128,128]{1,0:T(8,128)(2,1)}, u32[]{:S(2)}) copy-start(bf16[128,128]{1,0:T(8,128)(2,1)} %w_cand_ref.1) | copy-start | bytes 98308
  57.4 5.1 %collective-permute-start.2 = (f32[192,128]{1,0:T(8,128)S(1)}, f32[192,128]{1,0:T(8,128)S(1)}, u32[]{:S(2)}, u32[]{:S(2)}) collective-permute-start(f32[192,128]{1,0:T(8,128)S(1)} %message.1.mine_ref), channel_id=1, source_target_pairs={{0,32},{32,0},{1,33},{33,1},{2,34},{34,2},{3,35},{35,3},{4,36},{36... | collective-permute-start | bytes 294920 | tf_op jit(solution)/shard_map/ppermute | solution.py:358
  83.9 17.5 %copy-start = (bf16[2048,512]{1,0:T(8,128)(2,1)S(1)}, bf16[2048,512]{1,0:T(8,128)(2,1)}, u32[]{:S(2)}) copy-start(bf16[2048,512]{1,0:T(8,128)(2,1)} %feats_ref.3) | copy-start | bytes 6291460
  97.8 5.1 %collective-permute-start.3 = (bf16[128,2048]{1,0:T(8,128)(2,1)S(1)}, bf16[128,2048]{1,0:T(8,128)(2,1)S(1)}, u32[]{:S(2)}, u32[]{:S(2)}) collective-permute-start(bf16[128,2048]{1,0:T(8,128)(2,1)S(1)} %get-tuple-element.20.high_ref), channel_id=1, source_target_pairs={{0,32},{32,0},{1,33},{33,1},{2,34},{34,2},{3,35},{35,3},{4,36},{36... | collective-permute-start | bytes 1572872 | tf_op jit(solution)/shard_map/ppermute | solution.py:358

commit v10 on v9

--- a/solution.py
+++ b/solution.py
@@ -99,7 +99,7 @@
     )
     slots, block, _ = adj.shape
     pairs = acc.shape[0]
-    piece = acc.shape[1] // (near * far)
+    piece = acc.shape[1] // (near * far + 1)
     hidden = acc.shape[2]
     half = len(parts) // 2
     acc[...] = jnp.zeros_like(acc)
@@ -123,16 +123,16 @@
             right = projected[pl.ds(pl.multiple_of(src_ref[slot] * block, block), block), :]
             result = dot(own_rows(adj, slot, core, piece), right)
             result = result[:, :hidden] + result[:, hidden:]
-            result = jnp.where(slot < count, result, 0.0)
             d = dst_ref[slot]
             place = ((d % near) * far + d // near) * piece
+            place = jnp.where(slot < count, place, near * far * piece)
             at = pl.ds(pl.multiple_of(place, piece), piece)
             for y in range(pairs):
                 acc[y, at, :] += result[y * piece : (y + 1) * piece]
         return carry
 
     lax.fori_loop(0, slots // step, some_slots, 0)
-    out_ref[...] = acc[...].astype(BF16).reshape(out_ref.shape)
+    out_ref[...] = acc[:, : near * far * piece, :].astype(BF16).reshape(out_ref.shape)
 
 
 def count_kernel(
@@ -232,21 +232,23 @@
     reset_in = lax.dot_general(cand_grad, w_cand, contract, preferred_element_type=F32)
     reset_pre = reset_in * value * reset * (1.0 - reset)
     gates = jnp.concatenate([update_pre.astype(BF16), reset_pre.astype(BF16), cand_grad], axis=1)
-    message_grad_t = lax.dot_general(w_in, gates, contract, preferred_element_type=F32).astype(BF16)
+    message_grad = lax.dot_general(gates, w_in, contract, preferred_element_type=F32).astype(BF16)
     own[...] = (
         out_grad * update
         + reset_in * reset
         + lax.dot_general(gates[:, : 2 * hidden], w_state, contract, preferred_element_type=F32)
     )
-    total = jnp.zeros((hidden, local), F32)
     mine = pl.ds(pl.multiple_of(lax.axis_index("y") * local, local), local)
-    for e in range(count_ref.shape[1] // rows):
-        counts = count_ref[mine, e * rows : (e + 1) * rows]
-        picked = lax.dot_general(
-            message_grad_t, counts, contract, preferred_element_type=F32
-        ).astype(BF16)
-        total += dot(w_edge_ref[:, e * hidden : (e + 1) * hidden], picked)
-    spread[...] = total.T
+    picked = jnp.concatenate(
+        [
+            dot(count_ref[mine, e * rows : (e + 1) * rows], message_grad).astype(BF16)
+            for e in range(count_ref.shape[1] // rows)
+        ],
+        axis=1,
+    )
+    spread[...] = lax.dot_general(
+        picked, w_edge_ref[...], contract, preferred_element_type=F32
+    )
     far = back_ref.shape[1] // piece
     place = (lax.axis_index("x") * far + lax.axis_index("z")) * piece
     spread[pl.ds(pl.multiple_of(place, piece), piece), :] += own[
@@ -291,11 +293,11 @@
         for j in range(step):
             slot = group * step + j
             result = dot(turned[dst_ref[slot]], own_rows(adj, slot, core, piece))
-            acc[src_ref[slot]] += jnp.where(slot < count, result, 0.0)
+            acc[jnp.where(slot < count, src_ref[slot], acc.shape[0] - 1)] += result
         return carry
 
     lax.fori_loop(0, slots // step, some_slots, 0)
-    for s in range(acc.shape[0]):
+    for s in range(acc.shape[0] - 1):
         high = acc[s].astype(BF16)
         out_ref[:, s * block : (s + 1) * block] = high
         low_ref[:, s * block : (s + 1) * block] = (acc[s] - high.astype(F32)).astype(BF16)
@@ -402,7 +404,7 @@
         out_specs=vspec(),
         scratch_shapes=[
             VMEM((nodes, 2 * hidden), BF16),
-            VMEM((pairs, local, hidden), F32),
+            VMEM((pairs, local + piece, hidden), F32),
             SMEM((slots,), jnp.int32),
             SMEM((slots,), jnp.int32),
             SMEM((1,), jnp.int32),
@@ -477,7 +479,7 @@
         out_specs=(vspec(), vspec(), aspec()),
         scratch_shapes=[
             VMEM((domains, hidden, pairs * piece), BF16),
-            VMEM((nodes // block, hidden, block), F32),
+            VMEM((nodes // block + 1, hidden, block), F32),
             SMEM((slots,), jnp.int32),
             SMEM((slots,), jnp.int32),
             SMEM((1,), jnp.int32),

time: 117 us -> 116 us (level)
  no operation moved by 1% of the time
where the time goes in v10:
time: 116 us
  blocking collectives  90.5 us (78%)
  starting transfers between devices  11.1 us (10%)
  Pallas kernels  10.5 us (9%)
  waiting for transfers between devices  1.86 us (2%)
  between operations  1.46 us (1%)
    all_to_all x3, blocking collectives, over_plane(): return lax.all_to_all(x, ('y', 'x'), 0, 0, tiled=True)  41.1 us
    all_to_all x2, blocking collectives, over_far(): return lax.all_to_all(x, 'z', 0, 0, tiled=True)  29.8 us
    all_to_all x1, blocking collectives, over_dom(): return lax.all_to_all(x, ('z', 'x'), 0, 0, tiled=True)  12.4 us
    ppermute x4, starting transfers between devices, swap(): return lax.ppermute(x, 'core', [(0, 1), (1, 0)])  11.1 us
    all_to_all x1, blocking collectives, over_near(): return lax.all_to_all(x, 'x', 0, 0, tiled=True)  7.23 us
  transfers between devices with their start and end apart: 4, of which 3 were waited for; matrix products, arithmetic and copies ran while one was open for 0% of the time, Pallas kernels for 2%

profile of v10, /device:TPU:1, one launch (start us, length us, event | category | flops | bytes accessed | tf_op | source)
XLA Modules:
  0.0 116.1 jit_solution(2183380086607242856)
XLA Ops:
  0.7 2.0 %project.1 = (f32[1024,128]{1,0:T(8,128)S(1)}, bf16[1024,512]{1,0:T(8,128)(2,1)S(1)}, bf16[512,128]{1,0:T(8,128)(2,1)S(1)}) custom-call(bf16[2048,512]{1,0:T(8,128)(2,1)} %feats_ref.3, bf16[512,128]{1,0:T(8,128)(2,1)} %w_hbm.1), custom_call_target="tpu_custom_call" | custom-call | tf_op jit(solution)/shard_map/project/pallas_call | solution.py:364
  2.7 0.4 project_rest.1.refs_6_
  3.1 3.3 %collective-permute-start.1 = (f32[1024,128]{1,0:T(8,128)S(1)}, f32[1024,128]{1,0:T(8,128)S(1)}, u32[]{:S(2)}, u32[]{:S(2)}) collective-permute-start(f32[1024,128]{1,0:T(8,128)S(1)} %project_rest.1.refs_6_), channel_id=1, source_target_pairs={{0,32},{32,0},{1,33},{33,1},{2,34},{34,2},{3,35},{35,3},{4,36},{36... | collective-permute-start | bytes 1572872 | tf_op jit(solution)/shard_map/ppermute | solution.py:360
  6.4 0.1 collective-permute-start
  7.2 1.4 %counts.1.refs_3_.count_ref = bf16[2048,512]{1,0:T(8,128)(2,1)S(1)} custom-call(s32[8,128]{1,0:T(8,128)S(1)} %bitcast.2, s32[8,128]{1,0:T(8,128)S(1)} %bitcast.3), custom_call_target="tpu_custom_call" | custom-call | tf_op jit(solution)/shard_map/counts/pallas_call | solution.py:392
  8.6 0.1 collective-permute-done.refs_7_
  8.7 1.5 %partial.1 = bf16[16,128,128]{2,1,0:T(8,128)(2,1)S(1)} custom-call(s32[64]{0:T(128)S(1)} %copy-done.9, s32[64]{0:T(128)S(1)} %copy-done.10, s32[1]{0:T(128)S(6)} %copy.15.refs_2_, bf16[2048,512]{1,0:T(8,128)(2,1)S(1)} %counts.1.refs_3_.count_ref, bf16[64,128,128]{2,1,0:T(8,128)(2,1)S(1)} %copy-done.1, f32[1024,128]{1,0:T(8,128)S(1)} %get-tuple-element.12.refs_5_, ...), custom_call_target="tpu_custom_call" | custom-call | tf_op jit(solution)/shard_map/partial/pallas_call | solution.py:400
  10.2 15.7 %all_to_all.35.part_ref = bf16[16,128,128]{2,1,0:T(8,128)(2,1)S(1)} all-to-all(bf16[16,128,128]{2,1,0:T(8,128)(2,1)S(1)} %partial.1), channel_id=1, replica_groups=mesh['y'=4,'core'=2,'z'=8,'x'=4] {'y','x'}, dimensions={0} | all-to-all | bytes 1048576 | tf_op jit(solution)/shard_map/all_to_all | solution.py:351
  26.0 17.2 %all_to_all.36.part_ref = bf16[8,128,128]{2,1,0:T(8,128)(2,1)S(1)} all-to-all(bf16[8,128,128]{2,1,0:T(8,128)(2,1)S(1)} %fold.2), channel_id=1, replica_groups=mesh['y'=4,'core'=2,'z'=8,'x'=4] {'z'}, dimensions={0} | all-to-all | bytes 524288 | tf_op jit(solution)/shard_map/all_to_all | solution.py:357
  43.3 13.4 %all_to_all.37.states_ref = bf16[16,128,128]{2,1,0:T(8,128)(2,1)S(1)} all-to-all(bf16[16,128,128]{2,1,0:T(8,128)(2,1)S(1)} %get-tuple-element.15), channel_id=1, replica_groups=mesh['y'=4,'core'=2,'z'=8,'x'=4] {'y','x'}, dimensions={0} | all-to-all | bytes 1048576 | tf_op jit(solution)/shard_map/all_to_all | solution.py:351
  56.7 0.6 message.1.mine_ref
  57.4 4.1 %collective-permute-start.2 = (f32[192,128]{1,0:T(8,128)S(1)}, f32[192,128]{1,0:T(8,128)S(1)}, u32[]{:S(2)}, u32[]{:S(2)}) collective-permute-start(f32[192,128]{1,0:T(8,128)S(1)} %message.1.mine_ref), channel_id=1, source_target_pairs={{0,32},{32,0},{1,33},{33,1},{2,34},{34,2},{3,35},{35,3},{4,36},{36... | collective-permute-start | bytes 294920 | tf_op jit(solution)/shard_map/ppermute | solution.py:360
  61.5 0.9 collective-permute-done.2.other_ref
  62.5 1.1 gates.1
  63.6 7.2 %all_to_all.38.part_ref = bf16[4,128,128]{2,1,0:T(8,128)(2,1)S(1)} all-to-all(bf16[4,128,128]{2,1,0:T(8,128)(2,1)S(1)} %get-tuple-element.17), channel_id=1, replica_groups=mesh['y'=4,'core'=2,'z'=8,'x'=4] {'x'}, dimensions={0} | all-to-all | bytes 262144 | tf_op jit(solution)/shard_map/all_to_all | solution.py:354
  70.8 12.6 %all_to_all.39.part_ref = bf16[8,128,128]{2,1,0:T(8,128)(2,1)S(1)} all-to-all(bf16[8,128,128]{2,1,0:T(8,128)(2,1)S(1)} %fold.3), channel_id=1, replica_groups=mesh['y'=4,'core'=2,'z'=8,'x'=4] {'z'}, dimensions={0} | all-to-all | bytes 524288 | tf_op jit(solution)/shard_map/all_to_all | solution.py:357
  83.5 12.0 %all_to_all.40.refs_4_ = bf16[16,128,128]{2,1,0:T(8,128)(2,1)S(1)} all-to-all(bf16[16,128,128]{2,1,0:T(8,128)(2,1)S(1)} %first_grad.1), channel_id=1, replica_groups=mesh['y'=4,'core'=2,'z'=8,'x'=4] {'y','x'}, dimensions={0} | all-to-all | bytes 1048576 | tf_op jit(solution)/shard_map/all_to_all | solution.py:351
  95.5 1.9 %spread.1 = (bf16[128,2048]{1,0:T(8,128)(2,1)S(1)}, bf16[128,2048]{1,0:T(8,128)(2,1)S(1)}, bf16[128,128]{1,0:T(8,128)(2,1)}) custom-call(s32[64]{0:T(128)S(1)} %copy-done.9, s32[64]{0:T(128)S(1)} %copy-done.10, s32[1]{0:T(128)S(6)} %copy.15.refs_2_, bf16[128,128]{1,0:T(8,128)(2,1)S(1)} %get-tuple-element.16.refs_3_, ...), custom_call_target="tpu_custom_call" | custom-call | tf_op jit(solution)/shard_map/spread/pallas_call | solution.py:471
  97.4 3.6 %collective-permute-start.3 = (bf16[128,2048]{1,0:T(8,128)(2,1)S(1)}, bf16[128,2048]{1,0:T(8,128)(2,1)S(1)}, u32[]{:S(2)}, u32[]{:S(2)}) collective-permute-start(bf16[128,2048]{1,0:T(8,128)(2,1)S(1)} %get-tuple-element.20.high_ref), channel_id=1, source_target_pairs={{0,32},{32,0},{1,33},{33,1},{2,34},{34,2},{3,35},{35,3},{4,36},{36... | collective-permute-start | bytes 1572872 | tf_op jit(solution)/shard_map/ppermute | solution.py:360
  101.0 0.7 weight_own.1.part_ref
  101.7 0.8 collective-permute-done.3.spread_ref
  102.5 0.5 weight_all.1
  103.0 12.4 %all_to_all.41 = bf16[32,16,128]{2,1,0:T(8,128)(2,1)S(1)} all-to-all(bf16[32,16,128]{2,1,0:T(8,128)(2,1)S(1)} %weight_all.1), channel_id=1, replica_groups=mesh['y'=4,'core'=2,'z'=8,'x'=4] {'z','x'}, dimensions={0} | all-to-all | bytes 262144 | tf_op jit(solution)/shard_map/all_to_all | solution.py:348
  115.5 0.6 convert_reduce_fusion
  (27 shorter events, 0.3 us)
Async XLA Ops:
  0.6 6.5 %copy-start.8 = (s32[128,8]{0,1:T(8,128)S(1)}, s32[128,8]{0,1:T(8,128)}, u32[]{:S(2)}) copy-start(s32[128,8]{0,1:T(8,128)} %param.19) | copy-start | bytes 12292
  0.6 6.5 %copy-start.7 = (s32[128,8]{0,1:T(8,128)S(1)}, s32[128,8]{0,1:T(8,128)}, u32[]{:S(2)}) copy-start(s32[128,8]{0,1:T(8,128)} %param.18) | copy-start | bytes 12292
  2.6 6.0 %copy-start.1 = (bf16[64,128,128]{2,1,0:T(8,128)(2,1)S(1)}, bf16[64,128,128]{2,1,0:T(8,128)(2,1)}, u32[]{:S(2)}) copy-start(bf16[64,128,128]{2,1,0:T(8,128)(2,1)} %refs_5_.1) | copy-start | bytes 6291460
  2.7 6.0 %copy-start.9 = (s32[64]{0:T(128)S(1)}, s32[64]{0:T(128)}, u32[]{:S(2)}) copy-start(s32[64]{0:T(128)} %refs_0_.3) | copy-start | bytes 772
  2.7 6.0 %copy-start.10 = (s32[64]{0:T(128)S(1)}, s32[64]{0:T(128)}, u32[]{:S(2)}) copy-start(s32[64]{0:T(128)} %refs_1_.3) | copy-start | bytes 772
  3.1 5.5 %collective-permute-start.1 = (f32[1024,128]{1,0:T(8,128)S(1)}, f32[1024,128]{1,0:T(8,128)S(1)}, u32[]{:S(2)}, u32[]{:S(2)}) collective-permute-start(f32[1024,128]{1,0:T(8,128)S(1)} %project_rest.1.refs_6_), channel_id=1, source_target_pairs={{0,32},{32,0},{1,33},{33,1},{2,34},{34,2},{3,35},{35,3},{4,36},{36... | collective-permute-start | bytes 1572872 | tf_op jit(solution)/shard_map/ppermute | solution.py:360
  6.4 2.3 %collective-permute-start = (f32[1024,128]{1,0:T(8,128)S(1)}, f32[1024,128]{1,0:T(8,128)S(1)}, u32[]{:S(2)}, u32[]{:S(2)}) collective-permute-start(f32[1024,128]{1,0:T(8,128)S(1)} %get-tuple-element.12.refs_5_), channel_id=1, source_target_pairs={{0,32},{32,0},{1,33},{33,1},{2,34},{34,2},{3,35},{35,3},{4,36},{36... | collective-permute-start | bytes 1572872 | tf_op jit(solution)/shard_map/ppermute | solution.py:360
  10.2 46.5 %copy-start.2 = (bf16[128,512]{1,0:T(8,128)(2,1)S(1)}, bf16[128,512]{1,0:T(8,128)(2,1)}, u32[]{:S(2)}) copy-start(bf16[128,512]{1,0:T(8,128)(2,1)} %w_edge_ref.1) | copy-start | bytes 393220
  43.2 19.2 %copy-start.3 = (bf16[128,384]{1,0:T(8,128)(2,1)S(1)}, bf16[128,384]{1,0:T(8,128)(2,1)}, u32[]{:S(2)}) copy-start(bf16[128,384]{1,0:T(8,128)(2,1)} %w_in_ref.1) | copy-start | bytes 294916
  43.2 19.2 %copy-start.4 = (bf16[128,256]{1,0:T(8,128)(2,1)S(1)}, bf16[128,256]{1,0:T(8,128)(2,1)}, u32[]{:S(2)}) copy-start(bf16[128,256]{1,0:T(8,128)(2,1)} %w_state_ref.1) | copy-start | bytes 196612
  43.2 19.2 %copy-start.5 = (bf16[128,128]{1,0:T(8,128)(2,1)S(1)}, bf16[128,128]{1,0:T(8,128)(2,1)}, u32[]{:S(2)}) copy-start(bf16[128,128]{1,0:T(8,128)(2,1)} %grad_ref.1) | copy-start | bytes 98308
  43.2 19.2 %copy-start.6 = (bf16[128,128]{1,0:T(8,128)(2,1)S(1)}, bf16[128,128]{1,0:T(8,128)(2,1)}, u32[]{:S(2)}) copy-start(bf16[128,128]{1,0:T(8,128)(2,1)} %w_cand_ref.1) | copy-start | bytes 98308
  57.4 5.1 %collective-permute-start.2 = (f32[192,128]{1,0:T(8,128)S(1)}, f32[192,128]{1,0:T(8,128)S(1)}, u32[]{:S(2)}, u32[]{:S(2)}) collective-permute-start(f32[192,128]{1,0:T(8,128)S(1)} %message.1.mine_ref), channel_id=1, source_target_pairs={{0,32},{32,0},{1,33},{33,1},{2,34},{34,2},{3,35},{35,3},{4,36},{36... | collective-permute-start | bytes 294920 | tf_op jit(solution)/shard_map/ppermute | solution.py:360
  83.4 17.6 %copy-start = (bf16[2048,512]{1,0:T(8,128)(2,1)S(1)}, bf16[2048,512]{1,0:T(8,128)(2,1)}, u32[]{:S(2)}) copy-start(bf16[2048,512]{1,0:T(8,128)(2,1)} %feats_ref.3) | copy-start | bytes 6291460
  97.4 5.1 %collective-permute-start.3 = (bf16[128,2048]{1,0:T(8,128)(2,1)S(1)}, bf16[128,2048]{1,0:T(8,128)(2,1)S(1)}, u32[]{:S(2)}, u32[]{:S(2)}) collective-permute-start(bf16[128,2048]{1,0:T(8,128)(2,1)S(1)} %get-tuple-element.20.high_ref), channel_id=1, source_target_pairs={{0,32},{32,0},{1,33},{33,1},{2,34},{34,2},{3,35},{35,3},{4,36},{36... | collective-permute-start | bytes 1572872 | tf_op jit(solution)/shard_map/ppermute | solution.py:360
